TPU v7x, 32 devices: a whole 2x2x4 slice. The times are simulated.
32 devices in a mesh: dp: 16 (over z, y, x), tensor: 2 (over core).
Axes of the slice: x: 2, y: 2, z: 4, core: 2. Of those that a mesh axis runs over, the one named last changes fastest.
Arguments:
- tokens: bfloat16 [4096, 1024], P(('dp', 'tensor'))
- cotangent: bfloat16 [4096, 1024], P(('dp', 'tensor')), may hold values from -6 to 6
- route: int32 [4096], P(('dp', 'tensor')), may hold values from 0 to 4095, as said below
- lengths: int32 [16, 4], P('dp'), may hold values from 1 to 128, 224 in all within a row
- clip_tau: int32 [1], replicated, may hold values from 2 to 11
- attn_norm_gain: bfloat16 [1024], replicated, may hold values from 0.5 to 1.5
- attn_norm_bias: bfloat16 [1024], replicated, may hold values from -4 to 4
- qkv_weight: bfloat16 [1024, 3, 1024], P(None, None, 'tensor')
- qv_bias: bfloat16 [2, 1024], P(None, 'tensor'), may hold values from -6 to 6
- out_weight: bfloat16 [1024, 1024], P('tensor'), may hold values from -1.5 to 1.5
- out_bias: bfloat16 [1024], replicated, may hold values from -4 to 4
- mlp_norm_gain: bfloat16 [1024], replicated, may hold values from 0.5 to 1.5
- mlp_norm_bias: bfloat16 [1024], replicated, may hold values from -4 to 4
- up_weight: bfloat16 [1024, 4096], P(None, 'tensor'), may hold values from -0.1875 to 0.1875
- up_bias: bfloat16 [4096], P('tensor'), may hold values from -6 to 6
- down_weight: bfloat16 [4096, 1024], P('tensor'), may hold values from -0.09375 to 0.09375
- down_bias: bfloat16 [1024], replicated, may hold values from -4 to 4
Outputs:
- out_tokens: bfloat16 [4096, 1024], P(('dp', 'tensor'))
- grad_tokens: bfloat16 [4096, 1024], P(('dp', 'tensor'))
- grad_qkv: float32 [1024, 3, 1024], P('dp', None, 'tensor')
- grad_out_weight: float32 [1024, 1024], P('tensor', 'dp')
- grad_up_weight: float32 [1024, 4096], P('dp', 'tensor')
- grad_down_weight: float32 [4096, 1024], P('tensor', 'dp')
- grad_qv_bias: float32 [2, 1024], replicated
- grad_up_bias: float32 [4096], replicated
- grad_vectors: float32 [6, 1024], replicated
- head_factor: float32 [16], P('tensor')
- clipped_qk: bfloat16 [1024, 2, 1024], P(None, None, 'tensor')
- clipped_q_bias: bfloat16 [1024], P('tensor')
Inputs may be any that keep to these rules, and one draw needn't show every extreme that they name: `route`: every packed position is named once. A token stored on device (d, t) of the dp and tensor axes goes to a position held by some device (d', t), and each such pair of devices gets exactly 8 tokens. Each group's lengths add up to 224; the longest of each group is exactly 128.
All inputs are finite; a program needn't handle non-finite values.
Results may differ from a plain program's by a relative error of at most 0.015.
Values may be sent and summed in bfloat16 or wider, within the bound.
No kernel may reach another device: no remote copies, remote signals or barrier semaphores. Data moves between devices by JAX's collectives and lax.ppermute only.
A program may use at most 128 MiB of HBM per device.

v0:
```python
import functools
import jax
import jax.numpy as jnp
from jax import lax
from jax.experimental import pallas as pl
from jax.experimental.pallas import tpu as pltpu
from jax.sharding import PartitionSpec as P

HD = 64
AG_BITS = (0, 1)
PAD = 128
COST = 1

epsilon = 1e-05
masked_value = -1e30
gelu_coef = 0.7978845608028654
F32 = jnp.float32
BF16 = jnp.bfloat16
I32 = jnp.int32


def f(x):
    return x.astype(F32)


def dot(a, b, ca, cb):
    return lax.dot_general(a, b, (((ca,), (cb,)), ((), ())), preferred_element_type=F32)


def nn(a, b):
    return dot(a, b, 1, 0)


def nt(a, b):
    return dot(a, b, 1, 1)


def tn(a, b):
    return dot(a, b, 0, 0)


def norm_stats(values):
    row_mean = jnp.mean(values, axis=-1, keepdims=True)
    centered = values - row_mean
    variance = jnp.mean(centered * centered, axis=-1, keepdims=True)
    inv = lax.rsqrt(variance + epsilon)
    return centered * inv, inv


def norm_grad(xhat, inv, gain, grad):
    scaled = grad * gain
    a = jnp.mean(scaled, axis=-1, keepdims=True)
    b = jnp.mean(scaled * xhat, axis=-1, keepdims=True)
    return inv * (scaled - a - xhat * b)


def gelu_parts(p):
    p2 = p * p
    th = jnp.tanh(gelu_coef * (p + 0.044715 * p2 * p))
    half = 0.5 * (1.0 + th)
    slope = half + 0.5 * p * (1.0 - th * th) * (gelu_coef * (1.0 + 3.0 * 0.044715 * p2))
    return p * half, slope


def iota(shape, axis):
    return lax.broadcasted_iota(I32, shape, axis)


def place_matrix(ids):
    rows = ids.shape[0]
    return (ids == f(iota((rows, rows), 1))).astype(BF16)


def pair_mask(ends, core, rows):
    group = 2 * rows
    pos_r = (iota((group, 1), 0) + core * rows) & (group - 1)
    pos_c = (iota((1, group), 1) + core * rows) & (group - 1)
    sid_r = sum((pos_r >= e).astype(I32) for e in ends)
    sid_c = sum((pos_c >= e).astype(I32) for e in ends)
    sid_r = jnp.where(pos_r < ends[-1], sid_r, -1)
    same = (sid_r == sid_c).astype(I32) * (pos_c <= pos_r).astype(I32)
    diagonal = (pos_r == pos_c).astype(I32)
    return (same + diagonal) > 0, sid_r >= 0


def half_lanes():
    lane = iota((1, PAD), 1)
    low = (lane < HD).astype(F32)
    return (low.astype(BF16), (1.0 - low).astype(BF16)), (low, 1.0 - low)


def head_probs(q2, k2, lanes, mask):
    s = jnp.where(mask, nt(q2 * lanes, k2) * 0.125, masked_value)
    top = jnp.max(s, axis=-1, keepdims=True)
    e = jnp.exp(s - top)
    total = jnp.sum(e, axis=-1, keepdims=True)
    return e, top, total


def head_grad(q2, k2, v2, gc2, lanes, p):
    gp = nt(gc2 * lanes, v2)
    row_dot = jnp.sum(p * gp, axis=-1, keepdims=True)
    ds = (p * (gp - row_dot)).astype(BF16)
    return nn(ds, k2) * 0.125, tn(ds, q2) * 0.125, tn(p.astype(BF16), gc2)


class Fetched:
    def __init__(self, ref, copies):
        self.ref, self.copies, self.shape = ref, copies, ref.shape

    def wait(self, k=None):
        for c in self.copies if k is None else [self.copies[k]]:
            c.wait()
        return self.ref


def whole(shape):
    return shape, lambda src, dst, sc: [(src, dst)]


def kernel_call(body, outs, args, smem=(), hbm=None, flops=0, scratch=(), limit=12):
    hbm = hbm or {}
    specs = []
    n_bytes = 0
    for i, a in enumerate(args):
        n_bytes += a.size * a.dtype.itemsize
        space = pltpu.HBM if i in hbm else pltpu.SMEM if i in smem else pltpu.VMEM
        specs.append(pl.BlockSpec(memory_space=space))
    shapes = [jax.ShapeDtypeStruct(s, d) for s, d in outs]
    out_specs = [pl.BlockSpec(memory_space=pltpu.VMEM) for _ in outs]
    args = [pltpu.with_memory_space_constraint(a, pltpu.HBM) if i in hbm else a for i, a in enumerate(args)]
    n_in, n_out, n_scratch = len(args), len(outs), len(scratch)
    extra = []
    for i, (shape, chunks) in hbm.items():
        extra.append(pltpu.VMEM(shape, args[i].dtype))
    n_chunks = {}
    for i, (shape, chunks) in hbm.items():
        n_chunks[i] = getattr(chunks, "count", 1)
        extra.append(pltpu.SemaphoreType.DMA((n_chunks[i],)))

    def run(*refs):
        ins = list(refs[:n_in])
        rest = refs[n_in + n_out + n_scratch :]
        sc = ins[0]
        for j, (i, (_, chunks)) in enumerate(hbm.items()):
            dst, sem = rest[j], rest[len(hbm) + j]
            copies = [
                pltpu.make_async_copy(a, b, sem.at[k]) for k, (a, b) in enumerate(chunks(ins[i], dst, sc))
            ]
            for c in copies:
                c.start()
            ins[i] = Fetched(dst, copies)
        body(*ins, *refs[n_in : n_in + n_out + n_scratch])

    return pl.pallas_call(
        run,
        out_shape=shapes,
        in_specs=specs,
        out_specs=out_specs,
        scratch_shapes=list(scratch) + extra,
        compiler_params=pltpu.CompilerParams(vmem_limit_bytes=limit << 20),
        cost_estimate=pl.CostEstimate(
            flops=int(flops * COST), transcendentals=0, bytes_accessed=int(n_bytes * COST)
        ),
        name=body.func.__name__ if hasattr(body, "func") else body.__name__,
    )(*args)


def chunked(count, make):
    def chunks(src, dst, sc):
        return [make(src, dst, sc, k) for k in range(count)]

    chunks.count = count
    return chunks


def by_row(count):
    return chunked(count, lambda src, dst, sc, k: (src.at[k], dst.at[k]))


def tiles(count, axis):
    def make(src, dst, sc, k):
        at = pl.ds(k * TILE, TILE)
        return (src.at[at, :], dst.at[at, :]) if axis == 0 else (src.at[:, at], dst.at[:, at])

    return chunked(count, make)


def columns(n, axis):
    def chunks(src, dst, sc):
        at = pl.ds(pl.multiple_of(sc[2] * n, n), n)
        if axis == 0:
            return [(src.at[at, :], dst)]
        return [(src.at[(slice(None),) * (len(src.shape) - 1) + (at,)], dst)]

    return chunks


def route_kernel(n_dp, route, lens, tokens, cotangent, msg, msg_cot, pick_out):
    rows, width = tokens.shape
    row = jnp.broadcast_to(f(route.wait()[...]), (rows, rows))
    col = row.T
    group = float(2 * rows)
    dest_r = jnp.floor(row / group)
    dest_c = jnp.floor(col / group)
    before = iota((rows, rows), 0) < iota((rows, rows), 1)
    same = jnp.where(before, (dest_r == dest_c).astype(F32), 0.0)
    rank = dest_r[0:1] * (rows // n_dp) + jnp.sum(same, axis=0, keepdims=True)
    pick = (jnp.broadcast_to(rank, (rows, rows)) == f(iota((rows, rows), 0))).astype(F32)
    place = row - jnp.floor(row / float(rows)) * float(rows)
    ids = jnp.sum(pick * place, axis=1, keepdims=True)
    lane = iota((rows, PAD), 1)
    extra = jnp.where(lane == 0, ids, 0.0)
    lens = f(lens.wait()[...])
    for i in range(4):
        extra = jnp.where(lane == i + 1, lens[:, i : i + 1], extra)
    pick_b = pick.astype(BF16)
    pick_out[...] = pick_b
    msg[:, :width] = nn(pick_b, tokens.wait()[...]).astype(BF16)
    msg[:, width:] = extra.astype(BF16)
    msg_cot[...] = nn(pick_b, cotangent.wait()[...]).astype(BF16)


def ends_of(sc):
    e = [sc[4]]
    for i in range(1, 4):
        e.append(e[-1] + sc[4 + i])
    return e


def attn_kernel(
    sc, mine, other, vecs, w_qkv, qv_bias, w_out, x_out, normed_out, qkv_out, lse_out, top_out, part_out, ctx_out
):
    rows = mine.shape[0]
    width = w_out.shape[1]
    cols = w_out.shape[0]
    for i, half in enumerate((mine, other)):
        put = place_matrix(f(half[:, width : width + 1]))
        x = tn(put, half[:, :width])
        s = slice(i * rows, (i + 1) * rows)
        x_out[s, :] = x.astype(BF16)
        xhat, _ = norm_stats(x)
        normed_out[s, :] = (xhat * vecs[0:1, :] + vecs[1:2, :]).astype(BF16)
    normed = normed_out[...]
    qv_bias = qv_bias.wait()
    for c in range(3):
        y = nn(normed, w_qkv.wait(c)[c])
        if c == 0:
            y = y + f(qv_bias[0:1, :])
        if c == 2:
            y = y + f(qv_bias[1:2, :])
        qkv_out[:, c * cols : (c + 1) * cols] = y.astype(BF16)
    mask, live = pair_mask(ends_of(sc), sc[0], rows)
    lanes_b, lanes_f = half_lanes()
    lane = iota((1, PAD), 1)
    lse = jnp.zeros((2 * rows, PAD), F32)
    for pair in range(cols // PAD):
        s = slice(pair * PAD, (pair + 1) * PAD)
        q2 = qkv_out[:, s]
        k2 = qkv_out[:, slice(cols + pair * PAD, cols + (pair + 1) * PAD)]
        v2 = qkv_out[:, slice(2 * cols + pair * PAD, 2 * cols + (pair + 1) * PAD)]
        out = jnp.zeros((2 * rows, PAD), F32)
        for i in range(2):
            e, top, total = head_probs(q2, k2, lanes_b[i], mask)
            probs = (e * (1.0 / total)).astype(BF16)
            out = out + nn(probs, v2) * lanes_f[i]
            h = 2 * pair + i
            lse = jnp.where(lane == h, top + jnp.log(total), lse)
            best = jnp.max(jnp.where(live, top, masked_value), axis=0, keepdims=True)
            top_out[h : h + 1, :] = jnp.broadcast_to(best, (1, PAD))
        ctx_out[:, s] = out.astype(BF16)
    lse_out[...] = lse
    part_out[...] = nn(ctx_out[...], w_out.wait()[...]).astype(BF16)


def middle_kernel(x, part, recv, vecs, mine, other, cot_mine, cot_other, middle_out, mid_out, cot_out, msg_out):
    rows, width = cot_mine.shape
    for i, (ids, c) in enumerate(((mine, cot_mine), (other, cot_other))):
        s = slice(i * rows, (i + 1) * rows)
        o = slice((1 - i) * rows, (2 - i) * rows)
        put = place_matrix(f(ids[:, width : width + 1]))
        cot = tn(put, c[...]).astype(BF16)
        cot_out[s, :] = cot
        middle = f(x[s, :]) + (f(part[s, :]) + f(recv[o, :])) + vecs[2:3, :]
        middle_out[s, :] = middle
        mhat, _ = norm_stats(middle)
        mid = (mhat * vecs[3:4, :] + vecs[4:5, :]).astype(BF16)
        mid_out[s, :] = mid
        if i == 0:
            msg_out[:, :width] = mid
            msg_out[:, width:] = cot


TILE = 512


def mlp_kernel(mid, cot, vecs, up, down, gmid_out, mine_out, other_out, sums_out, acc, acc_y):
    width, hidden = up.shape
    rows = mine_out.shape[0]
    per_row = width // TILE
    for t in range(hidden // TILE):
        s = slice(t * TILE, (t + 1) * TILE)
        bias = vecs[6 + t // per_row : 7 + t // per_row, (t % per_row) * TILE : (t % per_row + 1) * TILE]
        act, slope = gelu_parts(nn(mid[...], up.wait(t)[:, s]) + bias)
        gpre = (nt(cot[...], down.wait(t)[s, :]) * slope).astype(BF16)
        sums_out[:, s] = jnp.sum(f(gpre), axis=0, keepdims=True)
        g = nt(gpre, up.ref[:, s])
        y = nn(act.astype(BF16), down.ref[s, :])
        if t == 0:
            acc[...] = g
            acc_y[...] = y
        else:
            acc[...] += g
            acc_y[...] += y
    gmid_out[...] = acc[...].astype(BF16)
    mine_out[...] = acc_y[:rows, :]
    other_out[...] = acc_y[rows:, :].astype(BF16)


def gmid_kernel(part, recv, middle, cot, normed, vecs, gmid_out, gattn_out, sums_out, msg_out):
    rows, width = gmid_out.shape
    msg_out[:, width:] = normed[:rows, :]
    for i in range(2):
        s = slice(i * rows, (i + 1) * rows)
        o = slice((1 - i) * rows, (2 - i) * rows)
        g = f(part[s, :]) + f(recv[o, :])
        mhat, inv = norm_stats(middle[s, :])
        c = f(cot[s, :])
        gm = c + norm_grad(mhat, inv, vecs[3:4, :], g)
        gattn = gm.astype(BF16)
        gattn_out[s, :] = gattn
        if i == 0:
            gmid_out[...] = gm
            msg_out[:, :width] = gattn
            sums_out[0:1, :] = jnp.sum(gm, axis=0, keepdims=True)
            sums_out[1:2, :] = jnp.sum(g * mhat, axis=0, keepdims=True)
            sums_out[2:3, :] = jnp.sum(g, axis=0, keepdims=True)
            sums_out[3:4, :] = jnp.sum(c, axis=0, keepdims=True)
            sums_out[4:8, :] = jnp.zeros((4, sums_out.shape[1]), F32)


def attn_grad_kernel(sc, gattn, w_out, qkv, lse, w_qkv, mine_out, other_out, sums_out, gqkv):
    rows = gattn.shape[0] // 2
    cols = w_out.shape[0]
    mask, _ = pair_mask(ends_of(sc), sc[0], rows)
    gctx = nt(gattn[...], w_out.wait()[...]).astype(BF16)
    lanes_b, lanes_f = half_lanes()
    for pair in range(cols // PAD):
        cut = [slice(c * cols + pair * PAD, c * cols + (pair + 1) * PAD) for c in range(3)]
        q2, k2, v2 = (qkv[:, c] for c in cut)
        gc2 = gctx[:, pair * PAD : (pair + 1) * PAD]
        total = None
        for i in range(2):
            h = 2 * pair + i
            s = jnp.where(mask, nt(q2 * lanes_b[i], k2) * 0.125, masked_value)
            p = jnp.exp(s - lse[:, h : h + 1])
            g3 = [g * lanes_f[i] for g in head_grad(q2, k2, v2, gc2, lanes_b[i], p)]
            total = g3 if total is None else [a + b for a, b in zip(total, g3)]
        for c in range(3):
            g = total[c].astype(BF16)
            gqkv[:, cut[c]] = g
            sums_out[c : c + 1, pair * PAD : (pair + 1) * PAD] = jnp.sum(f(g), axis=0, keepdims=True)
    y = sum(nt(gqkv[:, c * cols : (c + 1) * cols], w_qkv.wait(c)[c]) for c in range(3))
    mine_out[...] = y[:rows]
    other_out[...] = y[rows:].astype(BF16)


def last_kernel(part, recv, x, gmid, middle, y_mine, y_other, vecs, ids, msg_out, sums_out):
    rows, width = part.shape
    put = place_matrix(f(ids[:, width : width + 1]))
    res = middle[:rows, :] + (y_mine[...] + f(y_other[...])) + vecs[5:6, :]
    msg_out[:, :width] = nn(put, res.astype(BF16)).astype(BF16)
    g = part[...] + f(recv[...])
    xhat, inv = norm_stats(f(x[:rows, :]))
    grad = (gmid[...] + norm_grad(xhat, inv, vecs[0:1, :], g)).astype(BF16)
    sums_out[0:1, :] = jnp.sum(g * xhat, axis=0, keepdims=True)
    sums_out[1:2, :] = jnp.sum(g, axis=0, keepdims=True)
    msg_out[:, width:] = nn(put, grad).astype(BF16)


def restore_kernel(pick, msg, out, grad):
    width = out.shape[1]
    y = tn(pick[...], msg[...]).astype(BF16)
    out[...] = y[:, :width]
    grad[...] = y[:, width:]


def clip_kernel(w, factor, out):
    for c in range(2):
        out[:, c, :] = (f(w[c]) * factor[...]).astype(BF16)


def run_lengths(bits, block):
    return {b: block << i for i, b in enumerate(sorted(bits))}


def split_rows(src, run, mine, send_out, keep_out, at):
    n = src.shape[0]
    for j in range(n // (2 * run)):
        k = pl.multiple_of(2 * run * j + mine * run, run)
        s = pl.multiple_of(2 * run * j + (1 - mine) * run, run)
        dst = slice(j * run, (j + 1) * run)
        keep_out[dst, at] = src[pl.ds(k, run), :]
        send_out[dst, at] = src[pl.ds(s, run), :].astype(BF16)


def gather_rows(own, halves, dst, at):
    n, width = own.shape
    dst[:n, :] = own[...]
    for h in halves:
        r = h.shape[0]
        dst[n : n + r, :] = h[:, at * width : (at + 1) * width]
        n += r


def mlp_weights_kernel(
    n_bits, bit, sc, mid, cot, m1, m2, m3, o1, o2, o3, bias, up, down,
    send_down, keep_down, send_up, keep_up, mids, cots, grad,
):
    gather_rows(mid, (m1, o1, m2, o2, m3, o3), mids, 0)
    gather_rows(cot, (m1, o1, m2, o2, m3, o3), cots, 1)
    mine = (sc[1] >> bit) & 1
    run = (mids.shape[1] >> n_bits) << bit
    act, slope = gelu_parts(nn(mids[...], up.wait()[...]) + f(bias.wait()[...]))
    every = slice(None)
    grad[...] = tn(cots[...], act.astype(BF16))
    split_rows(grad, run, mine, send_down, keep_down, every)
    gpre = (nt(cots[...], down.wait()[...]) * slope).astype(BF16)
    grad[...] = tn(mids[...], gpre)
    split_rows(grad, run, mine, send_up, keep_up, every)


def attn_weights_kernel(
    n_bits, bit, n_dp, sc, ids, nrm, ga, m1, m2, m3, o1, o2, o3, qv_bias, w_qkv, w_out,
    send_out, keep_out, norms, gattns, ctx, gqkv, grad,
):
    gather_rows(ga, (m1, o1, m2, o2, m3, o3), gattns, 0)
    gather_rows(nrm, (m1, o1, m2, o2, m3, o3), norms, 1)
    rows = nrm.shape[0] // 2
    group = 2 * rows
    me = sc[1]
    mine = (me >> bit) & 1
    run = (norms.shape[1] >> n_bits) << bit
    masks = (0, 1 << AG_BITS[0], 1 << AG_BITS[1], (1 << AG_BITS[0]) | (1 << AG_BITS[1]))
    norm4 = norms[...]
    w_qkv, qv_bias = w_qkv.wait(), qv_bias.wait()
    q4 = (nn(norm4, w_qkv[0]) + f(qv_bias[0:1, :])).astype(BF16)
    k4 = nn(norm4, w_qkv[1]).astype(BF16)
    v4 = (nn(norm4, w_qkv[2]) + f(qv_bias[1:2, :])).astype(BF16)
    gc4 = nt(gattns[...], w_out.wait()[...]).astype(BF16)
    lanes_b, lanes_f = half_lanes()
    table = f(ids[:, norms.shape[1] :])
    from_dp = iota((rows, 1), 0) // (rows // n_dp)
    first = iota((rows, 1), 0) == from_dp * (rows // n_dp)
    for g in range(4):
        chosen = jnp.where((from_dp == (me ^ masks[g])) & first, table, 0.0)
        lens = jnp.sum(chosen, axis=0, keepdims=True)
        ends = [lens[:, 1:2]]
        for i in range(2, 5):
            ends.append(ends[-1] + lens[:, i : i + 1])
        mask, _ = pair_mask([e.astype(I32) for e in ends], sc[0], rows)
        s = slice(g * group, (g + 1) * group)
        q2, k2, v2, gc2 = q4[s], k4[s], v4[s], gc4[s]
        out = jnp.zeros((group, PAD), F32)
        total = None
        for i in range(2):
            e, _, denom = head_probs(q2, k2, lanes_b[i], mask)
            p = e * (1.0 / denom)
            out = out + nn(p.astype(BF16), v2) * lanes_f[i]
            g3 = [x * lanes_f[i] for x in head_grad(q2, k2, v2, gc2, lanes_b[i], p)]
            total = g3 if total is None else [a + b for a, b in zip(total, g3)]
        ctx[s, :] = out.astype(BF16)
        for c in range(3):
            gqkv[s, c * PAD : (c + 1) * PAD] = total[c].astype(BF16)
    grad[:, : 3 * PAD] = tn(norm4, gqkv[...])
    grad[:, 3 * PAD :] = tn(gattns[...], ctx[...])
    split_rows(grad, run, mine, send_out, keep_out, slice(None))


def step_kernel(bit, run, sc, keep, recv, send_out, keep_out, cur):
    cur[...] = keep[...] + f(recv[...])
    split_rows(cur, run, (sc[1] >> bit) & 1, send_out, keep_out, slice(None))


def pieces_kernel(n_pairs, sc, *refs):
    pairs, (own, p1, p2, p3), cur = refs[: 2 * n_pairs], refs[2 * n_pairs : -1], refs[-1]
    n = own.shape[0]
    w = pairs[0].shape[1]
    for i in range(n_pairs):
        cur[:, i * w : (i + 1) * w] = pairs[2 * i][...] + f(pairs[2 * i + 1][...])
    q = sc[2]
    for j, out in enumerate((own, p1, p2, p3)):
        out[...] = cur[pl.ds(pl.multiple_of((q ^ j) * n, n), n), :].astype(out.dtype)


def join_mlp_kernel(sc, own, p1, p2, p3, down_out, up_out):
    w = own.shape[1] // 2
    for j, p in enumerate((own, p1, p2, p3)):
        at = pl.ds(pl.multiple_of((sc[2] ^ j) * w, w), w)
        down_out[:, at] = f(p[:, :w])
        up_out[:, at] = f(p[:, w:])


def join_attn_kernel(sc, own, p1, p2, p3, qkv_out, out_out):
    w = own.shape[1] // 4
    for j, p in enumerate((own, p1, p2, p3)):
        at = pl.ds(pl.multiple_of((sc[2] ^ j) * w, w), w)
        for c in range(3):
            qkv_out[c, :, at] = f(p[:, c * w : (c + 1) * w])
        out_out[:, at] = f(p[:, 3 * w :])


def after(x, *deps):
    return lax.optimization_barrier((x, *deps))[0]


def local(
    tokens,
    cotangent,
    route,
    lengths,
    clip_tau,
    attn_norm_gain,
    attn_norm_bias,
    qkv_weight,
    qv_bias,
    out_weight,
    out_bias,
    mlp_norm_gain,
    mlp_norm_bias,
    up_weight,
    up_bias,
    down_weight,
    down_bias,
):
    n_dp = lax.axis_size("dp")
    n_bits = n_dp.bit_length() - 1
    rs_bits = [b for b in range(n_bits) if b not in AG_BITS]
    masks = [1 << AG_BITS[0], 1 << AG_BITS[1], (1 << AG_BITS[0]) | (1 << AG_BITS[1])]
    me = lax.axis_index("dp")
    core = lax.axis_index("tensor")
    rows, width = tokens.shape
    group = 2 * rows
    cols = qkv_weight.shape[2]
    hidden = up_weight.shape[1]
    q_cols = cols // 4
    q_hidden = hidden // 4
    quarter = ((me >> AG_BITS[0]) & 1) + 2 * ((me >> AG_BITS[1]) & 1)
    sc = jnp.concatenate([jnp.stack([core, me, quarter, core]).astype(I32), lengths[0]])

    def swap(x):
        return lax.ppermute(x, "tensor", [(0, 1), (1, 0)])

    def hop(x, mask):
        return lax.ppermute(x, "dp", [(i, i ^ mask) for i in range(n_dp)])

    def exchange(x):
        return lax.all_to_all(x, "dp", split_axis=0, concat_axis=0, tiled=True)

    def share(own):
        got = [hop(own[:rows], m) for m in masks]
        return got + [swap(g) for g in got]

    w_qkv = jnp.transpose(qkv_weight, (1, 0, 2))
    vecs = jnp.concatenate(
        [attn_norm_gain, attn_norm_bias, out_bias, mlp_norm_gain, mlp_norm_bias, down_bias, up_bias]
    ).astype(F32).reshape(-1, width)

    msg, msg_cot, pick = kernel_call(
        functools.partial(route_kernel, n_dp),
        [((rows, width + PAD), BF16), ((rows, width), BF16), ((rows, rows), BF16)],
        [route.reshape(1, rows), lengths, tokens, cotangent],
        hbm={0: whole((1, rows)), 1: whole(lengths.shape), 2: whole(tokens.shape), 3: whole(tokens.shape)},
        flops=4 * rows * rows * width,
    )
    got = after(exchange(msg), vecs, sc)
    got_cot = exchange(msg_cot)
    other = swap(got)
    x, normed, qkv, lse, tops, part = kernel_call(
        attn_kernel,
        [
            ((group, width), BF16),
            ((group, width), BF16),
            ((group, 3 * cols), BF16),
            ((group, PAD), F32),
            ((cols // HD, PAD), F32),
            ((group, width), BF16),
        ],
        [sc, got, other, vecs, w_qkv, qv_bias, out_weight],
        smem=(0,),
        hbm={4: (w_qkv.shape, by_row(3)), 5: whole(qv_bias.shape), 6: whole(out_weight.shape)},
        flops=2 * group * width * 4 * cols * 3,
        scratch=[pltpu.VMEM((group, cols), BF16)],
        limit=20,
    )
    middle, mid, cot, msg_mlp = kernel_call(
        middle_kernel,
        [((group, width), F32), ((group, width), BF16), ((group, width), BF16), ((rows, 2 * width), BF16)],
        [x, part, swap(part), vecs, got, other, got_cot, swap(got_cot)],
        flops=1 << 28,
    )
    m1, m2 = (hop(msg_mlp, m) for m in masks[:2])
    gmid_part, mlp_mine, mlp_other, up_sums = kernel_call(
        mlp_kernel,
        [((group, width), BF16), ((rows, width), F32), ((rows, width), BF16), ((1, hidden), F32)],
        [mid, cot, vecs, up_weight, down_weight],
        hbm={3: (up_weight.shape, tiles(hidden // TILE, 1)), 4: (down_weight.shape, tiles(hidden // TILE, 0))},
        flops=2 * group * width * hidden * 4,
        scratch=[pltpu.VMEM((group, width), F32), pltpu.VMEM((group, width), F32)],
        limit=24,
    )
    gmid_part, m1, m2 = lax.optimization_barrier((gmid_part, m1, m2))
    m3 = hop(after(msg_mlp, gmid_part), masks[2])
    o1, o2 = swap(m1), swap(m2)
    gmid_recv = swap(gmid_part)
    gmid, gattn, mid_sums, msg_attn = kernel_call(
        gmid_kernel,
        [((rows, width), F32), ((group, width), BF16), ((8, width), F32), ((rows, 2 * width), BF16)],
        [gmid_part, gmid_recv, middle, cot, normed, vecs],
        flops=1 << 28,
    )
    gn_mine, gn_other, qkv_sums = kernel_call(
        attn_grad_kernel,
        [((rows, width), F32), ((rows, width), BF16), ((3, cols), F32)],
        [sc, gattn, out_weight, qkv, lse, w_qkv],
        smem=(0,),
        hbm={2: whole(out_weight.shape), 5: (w_qkv.shape, by_row(3))},
        flops=2 * group * width * 4 * cols * 3,
        scratch=[pltpu.VMEM((group, 3 * cols), BF16)],
        limit=20,
    )
    gn_other, m3, o1, o2 = lax.optimization_barrier((gn_other, m3, o1, o2))
    gn_recv = swap(gn_other)
    msg_attn = after(msg_attn, gn_other)
    a1, a2 = (hop(msg_attn, m) for m in masks[:2])
    mlp_shared = [m1, m2, m3, o1, o2, swap(m3)]
    back, norm_sums = kernel_call(
        last_kernel,
        [((rows, 2 * width), BF16), ((2, width), F32)],
        [gn_mine, gn_recv, x, gmid, middle, mlp_mine, swap(mlp_other), vecs, got],
        flops=1 << 28,
    )
    restored = exchange(back)

    block = width // n_dp
    first = rs_bits[0]
    def step(i, recv, keep):
        n, w = keep.shape
        left = [b for b in range(n_bits) if b not in rs_bits[:i]]
        run = run_lengths(left, block)[rs_bits[i]]
        return kernel_call(
            functools.partial(step_kernel, rs_bits[i], run),
            [((n // 2, w), BF16), ((n // 2, w), F32)],
            [sc, keep, recv],
            smem=(0,),
            flops=1 << 26,
            scratch=[pltpu.VMEM((n, w), F32)],
        )

    half = ((width // 2, q_hidden), BF16), ((width // 2, q_hidden), F32)
    send_down, keep_down, send_up, keep_up = kernel_call(
        functools.partial(mlp_weights_kernel, n_bits, first),
        [half[0], half[1], half[0], half[1]],
        [sc, after(mid, norm_sums), cot] + mlp_shared + [up_bias.reshape(1, hidden), up_weight, down_weight],
        smem=(0,),
        hbm={
            9: ((1, q_hidden), columns(q_hidden, 1)),
            10: ((width, q_hidden), columns(q_hidden, 1)),
            11: ((q_hidden, width), columns(q_hidden, 0)),
        },
        limit=28,
        flops=2 * 4 * group * width * q_hidden * 4,
        scratch=[
            pltpu.VMEM((4 * group, width), BF16),
            pltpu.VMEM((4 * group, width), BF16),
            pltpu.VMEM((width, q_hidden), F32),
        ],
    )
    send_down, send_up, a1, a2, restored = lax.optimization_barrier((send_down, send_up, a1, a2, restored))
    recv_down = hop(send_down, 1 << first)
    a3 = hop(after(msg_attn, send_up), masks[2])
    b1, b2 = swap(a1), swap(a2)
    a3, recv_down, b1, b2, send_up = lax.optimization_barrier((a3, recv_down, b1, b2, send_up))
    send_down, keep_down = step(1, recv_down, keep_down)
    recv_down, recv_up = hop(send_down, 1 << rs_bits[1]), hop(send_up, 1 << first)
    attn_shared = [a1, a2, a3, b1, b2, swap(a3)]
    out_tokens, grad_tokens = kernel_call(
        restore_kernel, [((rows, width), BF16)] * 2, [pick, restored], flops=1 << 27
    )

    send_attn, keep_attn = kernel_call(
        functools.partial(attn_weights_kernel, n_bits, first, n_dp),
        [((width // 2, 4 * q_cols), BF16), ((width // 2, 4 * q_cols), F32)],
        [sc, got, after(normed, send_up), gattn] + attn_shared + [qv_bias, w_qkv, out_weight],
        smem=(0,),
        hbm={
            10: ((2, q_cols), columns(q_cols, 1)),
            11: ((3, width, q_cols), columns(q_cols, 1)),
            12: ((q_cols, width), columns(q_cols, 0)),
        },
        limit=28,
        flops=2 * 4 * group * width * q_cols * 12,
        scratch=[
            pltpu.VMEM((4 * group, width), BF16),
            pltpu.VMEM((4 * group, width), BF16),
            pltpu.VMEM((4 * group, q_cols), BF16),
            pltpu.VMEM((4 * group, 3 * q_cols), BF16),
            pltpu.VMEM((width, 4 * q_cols), F32),
        ],
    )

    send_attn, recv_down, recv_up = lax.optimization_barrier((send_attn, recv_down, recv_up))
    attn_done = send_attn

    recv_attn = hop(send_attn, 1 << first)
    send_up, keep_up = step(1, recv_up, keep_up)
    recv_up = hop(send_up, 1 << rs_bits[1])
    send_attn, keep_attn = step(1, recv_attn, keep_attn)
    recv_attn = hop(send_attn, 1 << rs_bits[1])

    def rest(recv, keep):
        for i in range(2, len(rs_bits)):
            send, keep = step(i, recv, keep)
            recv = hop(send, 1 << rs_bits[i])
        return keep, recv

    def hand_out(*pairs):
        n, w = pairs[0][0].shape
        w *= len(pairs)
        pieces = kernel_call(
            functools.partial(pieces_kernel, len(pairs)),
            [((block, w), F32)] + [((block, w), BF16)] * 3,
            [sc] + [a for pair in pairs for a in pair],
            smem=(0,),
            flops=1 << 26,
            scratch=[pltpu.VMEM((n, w), F32)],
        )
        return [pieces[0]] + [hop(p, m) for p, m in zip(pieces[1:], masks)]

    mlp_pieces = hand_out(rest(recv_down, keep_down), rest(recv_up, keep_up))
    attn_pieces = hand_out(rest(recv_attn, keep_attn))
    grad_down, grad_up = kernel_call(
        join_mlp_kernel, [((block, hidden), F32), ((block, hidden), F32)], [sc] + mlp_pieces, smem=(0,)
    )
    grad_down = grad_down.T
    grad_qkv, grad_out = kernel_call(
        join_attn_kernel, [((3, block, cols), F32), ((block, cols), F32)], [sc] + attn_pieces, smem=(0,)
    )
    grad_qkv = jnp.transpose(grad_qkv, (1, 0, 2))
    grad_out = grad_out.T

    n_vec = 6 * width
    sums = jnp.concatenate(
        [
            norm_sums.reshape(-1),
            mid_sums[:4].reshape(-1),
            qkv_sums[0],
            qkv_sums[2],
            up_sums.reshape(-1),
        ]
    )
    n_sum = sums.size
    sums = after(sums, attn_done)
    msg = jnp.concatenate([sums, jnp.pad(tops[:, 0], (0, PAD - tops.shape[0]))]).reshape(-1, PAD)
    is_top = iota(msg.shape, 0) == n_sum // PAD
    for b in range(n_bits):
        came = hop(msg, 1 << b)
        msg = jnp.where(is_top, jnp.maximum(msg, came), msg + came)
    global_top = msg[-1, : tops.shape[0]]
    theirs = swap(msg).reshape(-1)
    msg = msg.reshape(-1)
    vector_sum = (msg[:n_vec] + theirs[:n_vec]).reshape(6, width)
    own, oth = msg[n_vec:n_sum], theirs[n_vec:n_sum]
    one = jnp.where(core == 0, own, oth)
    two = jnp.where(core == 0, oth, own)
    qv_sum = jnp.stack(
        [
            jnp.concatenate([one[:cols], two[:cols]]),
            jnp.concatenate([one[cols : 2 * cols], two[cols : 2 * cols]]),
        ]
    )
    up_sum = jnp.concatenate([one[2 * cols :], two[2 * cols :]])

    threshold = clip_tau[0].astype(F32)
    head_factor = jnp.sqrt(threshold / jnp.maximum(global_top, threshold))
    column_factor = jnp.repeat(head_factor, HD)
    clipped_qk = pl.pallas_call(
        clip_kernel,
        grid=(4,),
        out_shape=jax.ShapeDtypeStruct((width, 2, cols), BF16),
        in_specs=[
            pl.BlockSpec((2, width // 4, cols), lambda i: (0, i, 0)),
            pl.BlockSpec((1, cols), lambda i: (0, 0)),
        ],
        out_specs=pl.BlockSpec((width // 4, 2, cols), lambda i: (i, 0, 0)),
        name="clip_kernel",
    )(w_qkv, column_factor.reshape(1, cols))
    clipped_q_bias = (f(qv_bias[0]) * column_factor).astype(BF16)
    return (
        out_tokens,
        grad_tokens,
        grad_qkv,
        grad_out,
        grad_up,
        grad_down,
        qv_sum,
        up_sum,
        vector_sum,
        head_factor,
        clipped_qk,
        clipped_q_bias,
    )

def solution(mesh):
    placed = (
        P(("dp", "tensor"), None),
        P(("dp", "tensor"), None),
        P(("dp", "tensor")),
        P("dp", None),
        P(),
        P(),
        P(),
        P(None, None, "tensor"),
        P(None, "tensor"),
        P("tensor", None),
        P(),
        P(),
        P(),
        P(None, "tensor"),
        P("tensor"),
        P("tensor", None),
        P(),
    )
    return jax.shard_map(
        local,
        mesh=mesh,
        in_specs=placed,
        out_specs=(
            P(("dp", "tensor"), None),
            P(("dp", "tensor"), None),
            P("dp", None, "tensor"),
            P("tensor", "dp"),
            P("dp", "tensor"),
            P("tensor", "dp"),
            P(),
            P(),
            P(),
            P("tensor"),
            P(None, None, "tensor"),
            P("tensor"),
        ),
        check_vma=False,
    )
```

profile of v0, /device:TPU:0, one launch (start us, length us, event | category | flops | bytes accessed | tf_op | source)
XLA Modules:
  0.0 189.5 jit_solution(11837549611146011767)
XLA Ops:
  0.6 2.2 %route_kernel.1 = (bf16[128,1152]{1,0:T(8,128)(2,1)}, bf16[128,1024]{1,0:T(8,128)(2,1)}, bf16[128,128]{1,0:T(8,128)(2,1)S(1)}) custom-call(s32[1,128]{1,0:T(1,128)} %bitcast.69, s32[1,4]{1,0:T(1,128)} %refs_1_.1, bf16[128,1024]{1,0:T(8,128)(2,1)} %refs_2_.2, bf16[128,1024]{1,0:T(8,128)(2,1)} %refs_3_.2), custom_call_target="tpu_custom_call" | custom-call | flops 67108864 | bytes 524816 | tf_op jit(solution)/shard_map/route_kernel/pallas_call | solution.py:155
  2.8 8.4 %all-to-all-start = ((bf16[16,8,1152]{2,1,0:T(8,128)(2,1)}), bf16[16,8,1152]{2,1,0:T(8,128)(2,1)S(1)}, u32[]{:S(2)}, u32[]{:S(2)}) async-start(bf16[16,8,1152]{2,1,0:T(8,128)(2,1)} %bitcast.5), calls=%async_computation | async-start | bytes 589824 | tf_op jit(solution)/shard_map/all_to_all | solution.py:558
  16.8 5.1 %all-to-all-done = bf16[16,8,1152]{2,1,0:T(8,128)(2,1)S(1)} async-done(((bf16[16,8,1152]{2,1,0:T(8,128)(2,1)}), bf16[16,8,1152]{2,1,0:T(8,128)(2,1)S(1)}, u32[]{:S(2)}, u32[]{:S(2)}) %all-to-all-start) | async-done | bytes 294944 | tf_op jit(solution)/shard_map/all_to_all | solution.py:558
  21.9 3.5 %all-to-all-start.1 = ((bf16[16,8,1024]{2,1,0:T(8,128)(2,1)}), bf16[16,8,1024]{2,1,0:T(8,128)(2,1)S(1)}, u32[]{:S(2)}, u32[]{:S(2)}) async-start(bf16[16,8,1024]{2,1,0:T(8,128)(2,1)} %bitcast.8), calls=%async_computation.1 | async-start | bytes 524288 | tf_op jit(solution)/shard_map/all_to_all | solution.py:558
  25.4 5.3 %attn_kernel.1 = (bf16[256,1024]{1,0:T(8,128)(2,1)S(1)}, bf16[256,1024]{1,0:T(8,128)(2,1)S(1)}, bf16[256,1536]{1,0:T(8,128)(2,1)S(1)}, f32[256,128]{1,0:T(8,128)...) custom-call(s32[8]{0:T(128)S(1)} %concatenate.21.refs_0_, bf16[128,1152]{1,0:T(8,128)(2,1)S(1)} %bitcast.50, ...), custom_call_target="tpu_custom_call" | custom-call | flops 3221225472 | bytes 4818976 | tf_op jit(solution)/shard_map/attn_kernel/pallas_call | solution.py:155
  32.1 4.0 %all-to-all-done.1 = bf16[16,8,1024]{2,1,0:T(8,128)(2,1)S(1)} async-done(((bf16[16,8,1024]{2,1,0:T(8,128)(2,1)}), bf16[16,8,1024]{2,1,0:T(8,128)(2,1)S(1)}, u32[]{:S(2)}, u32[]{:S(2)}) %all-to-all-start.1) | async-done | bytes 262176 | tf_op jit(solution)/shard_map/all_to_all | solution.py:558
  40.0 8.9 %mlp_kernel.1 = (bf16[256,1024]{1,0:T(8,128)(2,1)S(1)}, f32[128,1024]{1,0:T(8,128)S(1)}, bf16[128,1024]{1,0:T(8,128)(2,1)S(1)}, f32[1,2048]{1,0:T(1,128)S(1)}) custom-call(bf16[256,1024]{1,0:T(8,128)(2,1)S(1)} %get-tuple-element.117.refs_0_.refs_1_, bf16[256,1024]{1,0:T(8,128)(2,1)S(1)} %get-tuple-element.98.refs_1_.refs_3_.refs_2_, ...), custom_call_target="tpu_custom_call" | custom-call | flops 4294967296 | bytes 9469952 | tf_op jit(solution)/shard_map/mlp_kernel/pallas_call | solution.py:155
  48.8 3.5 %collective-permute-done.3.refs_3_ = bf16[128,2048]{1,0:T(8,128)(2,1)S(1)} collective-permute-done((bf16[128,2048]{1,0:T(8,128)(2,1)S(1)}, bf16[128,2048]{1,0:T(8,128)(2,1)S(1)}, u32[]{:S(2)}, u32[]{:S(2)}) %collective-permute-start.3) | collective-permute-done | bytes 524320 | tf_op jit(solution)/shard_map/ppermute | solution.py:555
  53.0 1.6 collective-permute-start.6
  55.3 1.6 gmid_kernel.1
  56.9 7.7 %attn_grad_kernel.1 = (f32[128,1024]{1,0:T(8,128)S(1)}, bf16[128,1024]{1,0:T(8,128)(2,1)S(1)}, f32[3,512]{1,0:T(4,128)S(1)}) custom-call(s32[8]{0:T(128)S(1)} %concatenate.21.refs_0_, bf16[256,1024]{1,0:T(8,128)(2,1)S(1)} %get-tuple-element.104.refs_1_.refs_3_, bf16[512,1024]{1,0:T(8,128)(2,1)} %refs_12_.1, bf16[256,1536]{1,0:T(8,128)(2,1)S(1)} %copy-done.28, ...), custom_call_target="tpu_custom_call" | custom-call | flops 3221225472 | bytes 5636128 | tf_op jit(solution)/shard_map/attn_grad_kernel/pallas_call | solution.py:155
  64.7 3.5 %collective-permute-done.6.refs_5_ = bf16[128,2048]{1,0:T(8,128)(2,1)S(1)} collective-permute-done((bf16[128,2048]{1,0:T(8,128)(2,1)S(1)}, bf16[128,2048]{1,0:T(8,128)(2,1)S(1)}, u32[]{:S(2)}, u32[]{:S(2)}) %collective-permute-start.6) | collective-permute-done | bytes 524320 | tf_op jit(solution)/shard_map/ppermute | solution.py:555
  69.8 1.6 last_kernel.1
  71.4 4.2 %all-to-all-start.2 = ((bf16[16,8,2048]{2,1,0:T(8,128)(2,1)}), bf16[16,8,2048]{2,1,0:T(8,128)(2,1)S(1)}, u32[]{:S(2)}, u32[]{:S(2)}) async-start(bf16[16,8,2048]{2,1,0:T(8,128)(2,1)} %bitcast.10), calls=%async_computation.2 | async-start | bytes 1048576 | tf_op jit(solution)/shard_map/all_to_all | solution.py:558
  75.7 1.9 %collective-permute-start.12 = (bf16[128,2048]{1,0:T(8,128)(2,1)}, bf16[128,2048]{1,0:T(8,128)(2,1)S(1)}, u32[]{:S(2)}, u32[]{:S(2)}) collective-permute-start(bf16[128,2048]{1,0:T(8,128)(2,1)} %get-tuple-element.130), channel_id=1, source_target_pairs={{0,2},{2,0},{4,6},{6,4},{8,10},{10,8},{12,14},{14,12},{16,18},{18,... | collective-permute-start | bytes 1572872 | tf_op jit(solution)/shard_map/ppermute | solution.py:555
  87.1 7.9 %mlp_weights_kernel.1 = (bf16[512,512]{1,0:T(8,128)(2,1)S(1)}, f32[512,512]{1,0:T(8,128)S(1)}, bf16[512,512]{1,0:T(8,128)(2,1)S(1)}, f32[512,512]{1,0:T(8,128)S(1)}) custom-call(s32[8]{0:T(128)S(1)} %concatenate.21.refs_0_, bf16[256,1024]{1,0:T(8,128)(2,1)S(1)} %copy-done.12, bf16[256,1024]{1,0:T(8,128)(2,1)S(1)} %copy-done.1, ...), custom_call_target="tpu_custom_call" | custom-call | flops 4294967296 | bytes 12587040 | tf_op jit(solution)/shard_map/mlp_weights_kernel/pallas_call | solution.py:155
  100.2 12.1 %collective-permute-done.14.refs_6_ = bf16[128,2048]{1,0:T(8,128)(2,1)S(1)} collective-permute-done((bf16[128,2048]{1,0:T(8,128)(2,1)}, bf16[128,2048]{1,0:T(8,128)(2,1)S(1)}, u32[]{:S(2)}, u32[]{:S(2)}) %collective-permute-start.14) | collective-permute-done | bytes 524320 | tf_op jit(solution)/shard_map/ppermute | solution.py:555
  112.4 1.5 collective-permute-start.20
  115.5 2.4 %collective-permute-start.19 = (bf16[256,512]{1,0:T(8,128)(2,1)S(1)}, bf16[256,512]{1,0:T(8,128)(2,1)S(1)}, u32[]{:S(2)}, u32[]{:S(2)}) collective-permute-start(bf16[256,512]{1,0:T(8,128)(2,1)S(1)} %get-tuple-element.143), channel_id=1, source_target_pairs={{0,16},{2,18},{4,20},{6,22},{8,24},{10,26},{12,28},{14,30},{16,0},... | collective-permute-start | bytes 786440 | tf_op jit(solution)/shard_map/ppermute | solution.py:555
  120.0 12.2 %attn_weights_kernel.1 = (bf16[512,512]{1,0:T(8,128)(2,1)S(1)}, f32[512,512]{1,0:T(8,128)S(1)}) custom-call(s32[8]{0:T(128)S(1)} %concatenate.21.refs_0_, bf16[128,1152]{1,0:T(8,128)(2,1)S(1)} %bitcast.53, bf16[256,1024]{1,0:T(8,128)(2,1)S(1)} %get-tuple-element.135.refs_4_.refs_2_, bf16[256,1024]{1,0:T(8,128)(2,1)S(1)} %copy-done.9, ...), custom_call_target="tpu_custom_call" | custom-call | flops 3221225472 | bytes 8685600 | tf_op jit(solution)/shard_map/attn_weights_kernel/pallas_call | solution.py:155
  135.2 3.2 %collective-permute-done.30 = f32[73,128]{1,0:T(8,128)S(1)} collective-permute-done((f32[73,128]{1,0:T(8,128)S(1)}, f32[73,128]{1,0:T(8,128)S(1)}, u32[]{:S(2)}, u32[]{:S(2)}) %collective-permute-start.30) | collective-permute-done | bytes 37408 | tf_op jit(solution)/shard_map/ppermute | solution.py:555
  139.4 3.2 %collective-permute-done.31 = f32[73,128]{1,0:T(8,128)S(1)} collective-permute-done((f32[73,128]{1,0:T(8,128)S(1)}, f32[73,128]{1,0:T(8,128)S(1)}, u32[]{:S(2)}, u32[]{:S(2)}) %collective-permute-start.31) | collective-permute-done | bytes 37408 | tf_op jit(solution)/shard_map/ppermute | solution.py:555
  142.7 2.0 %collective-permute-start.32 = (f32[73,128]{1,0:T(8,128)S(1)}, f32[73,128]{1,0:T(8,128)S(1)}, u32[]{:S(2)}, u32[]{:S(2)}) collective-permute-start(f32[73,128]{1,0:T(8,128)S(1)} %add_select_fusion.2), channel_id=1, source_target_pairs={{0,8},{2,10},{4,12},{6,14},{8,0},{10,2},{12,4},{14,6},{16,24},{18,... | collective-permute-start | bytes 112136 | tf_op jit(solution)/shard_map/ppermute | solution.py:555
  144.7 2.0 %collective-permute-done.32 = f32[73,128]{1,0:T(8,128)S(1)} collective-permute-done((f32[73,128]{1,0:T(8,128)S(1)}, f32[73,128]{1,0:T(8,128)S(1)}, u32[]{:S(2)}, u32[]{:S(2)}) %collective-permute-start.32) | collective-permute-done | bytes 37408 | tf_op jit(solution)/shard_map/ppermute | solution.py:555
  146.8 2.3 %collective-permute-start.33 = (f32[73,128]{1,0:T(8,128)S(1)}, f32[73,128]{1,0:T(8,128)S(1)}, u32[]{:S(2)}, u32[]{:S(2)}) collective-permute-start(f32[73,128]{1,0:T(8,128)S(1)} %add_select_fusion.1), channel_id=1, source_target_pairs={{0,16},{2,18},{4,20},{6,22},{8,24},{10,26},{12,28},{14,30},{16,0},... | collective-permute-start | bytes 112136 | tf_op jit(solution)/shard_map/ppermute | solution.py:555
  154.3 1.7 collective-permute-start.26
  157.6 5.0 %clip_kernel.1 = bf16[1024,2,512]{2,1,0:T(2,128)(2,1)} custom-call(bf16[3,1024,512]{2,1,0:T(8,128)(2,1)} %bitcast.62, f32[1,512]{1,0:T(1,128)} %reshape_reshape.3.factor), custom_call_target="tpu_custom_call" | custom-call | tf_op jit(solution)/shard_map/clip_kernel/pallas_call | solution.py:787
  162.6 4.0 %collective-permute-done.21.refs_2_ = bf16[512,512]{1,0:T(8,128)(2,1)} collective-permute-done((bf16[512,512]{1,0:T(8,128)(2,1)}, bf16[512,512]{1,0:T(8,128)(2,1)}, u32[]{:S(2)}, u32[]{:S(2)}) %collective-permute-start.21) | collective-permute-done | bytes 524320 | tf_op jit(solution)/shard_map/ppermute | solution.py:555
  166.6 2.0 %step_kernel.4 = (bf16[256,512]{1,0:T(8,128)(2,1)}, f32[256,512]{1,0:T(8,128)S(1)}) custom-call(s32[8]{0:T(128)S(1)} %concatenate.21.refs_0_, f32[512,512]{1,0:T(8,128)S(1)} %get-tuple-element.139.refs_1_, bf16[512,512]{1,0:T(8,128)(2,1)} %collective-permute-done.21.refs_2_), custom_call_target="tpu_custom_call" | custom-call | flops 67108864 | bytes 1572896 | tf_op jit(solution)/shard_map/step_kernel/pallas_call | solution.py:155
  174.6 5.5 %collective-permute-done.22.refs_2_ = bf16[256,512]{1,0:T(8,128)(2,1)S(1)} collective-permute-done((bf16[256,512]{1,0:T(8,128)(2,1)}, bf16[256,512]{1,0:T(8,128)(2,1)S(1)}, u32[]{:S(2)}, u32[]{:S(2)}) %collective-permute-start.22) | collective-permute-done | bytes 262176 | tf_op jit(solution)/shard_map/ppermute | solution.py:555
  184.9 1.6 join_mlp_kernel.1
  186.4 1.7 collective-permute-done.25.refs_4_
  (165 shorter events, 54.5 us)
Async XLA Ops:
  2.8 19.0 %all-to-all-start = ((bf16[16,8,1152]{2,1,0:T(8,128)(2,1)}), bf16[16,8,1152]{2,1,0:T(8,128)(2,1)S(1)}, u32[]{:S(2)}, u32[]{:S(2)}) async-start(bf16[16,8,1152]{2,1,0:T(8,128)(2,1)} %bitcast.5), calls=%async_computation | async-start | bytes 589824 | tf_op jit(solution)/shard_map/all_to_all | solution.py:558
  21.9 14.2 %all-to-all-start.1 = ((bf16[16,8,1024]{2,1,0:T(8,128)(2,1)}), bf16[16,8,1024]{2,1,0:T(8,128)(2,1)S(1)}, u32[]{:S(2)}, u32[]{:S(2)}) async-start(bf16[16,8,1024]{2,1,0:T(8,128)(2,1)} %bitcast.8), calls=%async_computation.1 | async-start | bytes 524288 | tf_op jit(solution)/shard_map/all_to_all | solution.py:558
  31.6 6.1 %collective-permute-start.1 = (bf16[256,1024]{1,0:T(8,128)(2,1)S(1)}, bf16[256,1024]{1,0:T(8,128)(2,1)S(1)}, u32[]{:S(2)}, u32[]{:S(2)}) collective-permute-start(bf16[256,1024]{1,0:T(8,128)(2,1)S(1)} %get-tuple-element.95.refs_1_), channel_id=1, source_target_pairs={{0,1},{1,0},{2,3},{3,2},{4,5},{5,4},{6,7},{7,6},{8,9},{9,8},{10,11... | collective-permute-start | bytes 1572872 | tf_op jit(solution)/shard_map/ppermute | solution.py:552
  38.4 14.0 %collective-permute-start.3 = (bf16[128,2048]{1,0:T(8,128)(2,1)S(1)}, bf16[128,2048]{1,0:T(8,128)(2,1)S(1)}, u32[]{:S(2)}, u32[]{:S(2)}) collective-permute-start(bf16[128,2048]{1,0:T(8,128)(2,1)S(1)} %get-tuple-element.109), channel_id=1, source_target_pairs={{0,2},{2,0},{4,6},{6,4},{8,10},{10,8},{12,14},{14,12},{16,18},{18,... | collective-permute-start | bytes 1572872 | tf_op jit(solution)/shard_map/ppermute | solution.py:555
  39.3 13.7 %collective-permute-start.4 = (bf16[128,2048]{1,0:T(8,128)(2,1)S(1)}, bf16[128,2048]{1,0:T(8,128)(2,1)S(1)}, u32[]{:S(2)}, u32[]{:S(2)}) collective-permute-start(bf16[128,2048]{1,0:T(8,128)(2,1)S(1)} %get-tuple-element.109), channel_id=1, source_target_pairs={{0,4},{2,6},{4,0},{6,2},{8,12},{10,14},{12,8},{14,10},{16,20},{18,... | collective-permute-start | bytes 1572872 | tf_op jit(solution)/shard_map/ppermute | solution.py:555
  53.0 15.2 %collective-permute-start.6 = (bf16[128,2048]{1,0:T(8,128)(2,1)S(1)}, bf16[128,2048]{1,0:T(8,128)(2,1)S(1)}, u32[]{:S(2)}, u32[]{:S(2)}) collective-permute-start(bf16[128,2048]{1,0:T(8,128)(2,1)S(1)} %get-tuple-element.109), channel_id=1, source_target_pairs={{0,6},{2,4},{4,2},{6,0},{8,14},{10,12},{12,10},{14,8},{16,22},{18,... | collective-permute-start | bytes 1572872 | tf_op jit(solution)/shard_map/ppermute | solution.py:555
  54.6 13.6 %collective-permute-start.7 = (bf16[128,2048]{1,0:T(8,128)(2,1)S(1)}, bf16[128,2048]{1,0:T(8,128)(2,1)S(1)}, u32[]{:S(2)}, u32[]{:S(2)}) collective-permute-start(bf16[128,2048]{1,0:T(8,128)(2,1)S(1)} %collective-permute-done.3.refs_3_), channel_id=1, source_target_pairs={{0,1},{1,0},{2,3},{3,2},{4,5},{5,4},{6,7},{7,6},{8,9},{9,8},{10,11... | collective-permute-start | bytes 1572872 | tf_op jit(solution)/shard_map/ppermute | solution.py:552
  54.8 13.4 %collective-permute-start.8 = (bf16[128,2048]{1,0:T(8,128)(2,1)S(1)}, bf16[128,2048]{1,0:T(8,128)(2,1)S(1)}, u32[]{:S(2)}, u32[]{:S(2)}) collective-permute-start(bf16[128,2048]{1,0:T(8,128)(2,1)S(1)} %collective-permute-done.4.refs_4_), channel_id=1, source_target_pairs={{0,1},{1,0},{2,3},{3,2},{4,5},{5,4},{6,7},{7,6},{8,9},{9,8},{10,11... | collective-permute-start | bytes 1572872 | tf_op jit(solution)/shard_map/ppermute | solution.py:552
  55.1 13.2 %collective-permute-start.10 = (bf16[128,1024]{1,0:T(8,128)(2,1)S(1)}, bf16[128,1024]{1,0:T(8,128)(2,1)S(1)}, u32[]{:S(2)}, u32[]{:S(2)}) collective-permute-start(bf16[128,1024]{1,0:T(8,128)(2,1)S(1)} %get-tuple-element.115), channel_id=1, source_target_pairs={{0,1},{1,0},{2,3},{3,2},{4,5},{5,4},{6,7},{7,6},{8,9},{9,8},{10,11... | collective-permute-start | bytes 786440 | tf_op jit(solution)/shard_map/ppermute | solution.py:552
  71.4 26.0 %all-to-all-start.2 = ((bf16[16,8,2048]{2,1,0:T(8,128)(2,1)}), bf16[16,8,2048]{2,1,0:T(8,128)(2,1)S(1)}, u32[]{:S(2)}, u32[]{:S(2)}) async-start(bf16[16,8,2048]{2,1,0:T(8,128)(2,1)} %bitcast.10), calls=%async_computation.2 | async-start | bytes 1048576 | tf_op jit(solution)/shard_map/all_to_all | solution.py:558
  75.6 4.2 %collective-permute-start.11 = (bf16[128,2048]{1,0:T(8,128)(2,1)}, bf16[128,2048]{1,0:T(8,128)(2,1)S(1)}, u32[]{:S(2)}, u32[]{:S(2)}) collective-permute-start(bf16[128,2048]{1,0:T(8,128)(2,1)} %copy-done.20), channel_id=1, source_target_pairs={{0,1},{1,0},{2,3},{3,2},{4,5},{5,4},{6,7},{7,6},{8,9},{9,8},{10,11... | collective-permute-start | bytes 1572872 | tf_op jit(solution)/shard_map/ppermute | solution.py:552
  75.7 21.0 %collective-permute-start.12 = (bf16[128,2048]{1,0:T(8,128)(2,1)}, bf16[128,2048]{1,0:T(8,128)(2,1)S(1)}, u32[]{:S(2)}, u32[]{:S(2)}) collective-permute-start(bf16[128,2048]{1,0:T(8,128)(2,1)} %get-tuple-element.130), channel_id=1, source_target_pairs={{0,2},{2,0},{4,6},{6,4},{8,10},{10,8},{12,14},{14,12},{16,18},{18,... | collective-permute-start | bytes 1572872 | tf_op jit(solution)/shard_map/ppermute | solution.py:555
  77.6 19.8 %collective-permute-start.13 = (bf16[128,2048]{1,0:T(8,128)(2,1)}, bf16[128,2048]{1,0:T(8,128)(2,1)}, u32[]{:S(2)}, u32[]{:S(2)}) collective-permute-start(bf16[128,2048]{1,0:T(8,128)(2,1)} %get-tuple-element.130), channel_id=1, source_target_pairs={{0,4},{2,6},{4,0},{6,2},{8,12},{10,14},{12,8},{14,10},{16,20},{18,... | collective-permute-start | bytes 1572872 | tf_op jit(solution)/shard_map/ppermute | solution.py:555
  97.5 14.8 %collective-permute-start.14 = (bf16[128,2048]{1,0:T(8,128)(2,1)}, bf16[128,2048]{1,0:T(8,128)(2,1)S(1)}, u32[]{:S(2)}, u32[]{:S(2)}) collective-permute-start(bf16[128,2048]{1,0:T(8,128)(2,1)} %get-tuple-element.130), channel_id=1, source_target_pairs={{0,6},{2,4},{4,2},{6,0},{8,14},{10,12},{12,10},{14,8},{16,22},{18,... | collective-permute-start | bytes 1572872 | tf_op jit(solution)/shard_map/ppermute | solution.py:555
  98.2 14.1 %collective-permute-start.15 = (bf16[512,512]{1,0:T(8,128)(2,1)}, bf16[512,512]{1,0:T(8,128)(2,1)S(1)}, u32[]{:S(2)}, u32[]{:S(2)}) collective-permute-start(bf16[512,512]{1,0:T(8,128)(2,1)} %copy-done.26), channel_id=1, source_target_pairs={{0,8},{2,10},{4,12},{6,14},{8,0},{10,2},{12,4},{14,6},{16,24},{18,... | collective-permute-start | bytes 1572872 | tf_op jit(solution)/shard_map/ppermute | solution.py:555
  99.7 12.6 %collective-permute-start.16 = (bf16[128,2048]{1,0:T(8,128)(2,1)}, bf16[128,2048]{1,0:T(8,128)(2,1)S(1)}, u32[]{:S(2)}, u32[]{:S(2)}) collective-permute-start(bf16[128,2048]{1,0:T(8,128)(2,1)} %copy-done.15), channel_id=1, source_target_pairs={{0,1},{1,0},{2,3},{3,2},{4,5},{5,4},{6,7},{7,6},{8,9},{9,8},{10,11... | collective-permute-start | bytes 1572872 | tf_op jit(solution)/shard_map/ppermute | solution.py:552
  99.7 12.6 %collective-permute-start.17 = (bf16[128,2048]{1,0:T(8,128)(2,1)}, bf16[128,2048]{1,0:T(8,128)(2,1)S(1)}, u32[]{:S(2)}, u32[]{:S(2)}) collective-permute-start(bf16[128,2048]{1,0:T(8,128)(2,1)} %collective-permute-done.13.refs_5_), channel_id=1, source_target_pairs={{0,1},{1,0},{2,3},{3,2},{4,5},{5,4},{6,7},{7,6},{8,9},{9,8},{10,11... | collective-permute-start | bytes 1572872 | tf_op jit(solution)/shard_map/ppermute | solution.py:552
  112.3 5.6 %collective-permute-start.18 = (bf16[128,2048]{1,0:T(8,128)(2,1)S(1)}, bf16[128,2048]{1,0:T(8,128)(2,1)S(1)}, u32[]{:S(2)}, u32[]{:S(2)}) collective-permute-start(bf16[128,2048]{1,0:T(8,128)(2,1)S(1)} %collective-permute-done.14.refs_6_), channel_id=1, source_target_pairs={{0,1},{1,0},{2,3},{3,2},{4,5},{5,4},{6,7},{7,6},{8,9},{9,8},{10,11... | collective-permute-start | bytes 1572872 | tf_op jit(solution)/shard_map/ppermute | solution.py:552
  112.4 21.3 %collective-permute-start.20 = (bf16[512,512]{1,0:T(8,128)(2,1)}, bf16[512,512]{1,0:T(8,128)(2,1)S(1)}, u32[]{:S(2)}, u32[]{:S(2)}) collective-permute-start(bf16[512,512]{1,0:T(8,128)(2,1)} %copy-done.19), channel_id=1, source_target_pairs={{0,8},{2,10},{4,12},{6,14},{8,0},{10,2},{12,4},{14,6},{16,24},{18,... | collective-permute-start | bytes 1572872 | tf_op jit(solution)/shard_map/ppermute | solution.py:555
  115.5 17.4 %collective-permute-start.19 = (bf16[256,512]{1,0:T(8,128)(2,1)S(1)}, bf16[256,512]{1,0:T(8,128)(2,1)S(1)}, u32[]{:S(2)}, u32[]{:S(2)}) collective-permute-start(bf16[256,512]{1,0:T(8,128)(2,1)S(1)} %get-tuple-element.143), channel_id=1, source_target_pairs={{0,16},{2,18},{4,20},{6,22},{8,24},{10,26},{12,28},{14,30},{16,0},... | collective-permute-start | bytes 786440 | tf_op jit(solution)/shard_map/ppermute | solution.py:555
  138.5 4.1 %collective-permute-start.31 = (f32[73,128]{1,0:T(8,128)S(1)}, f32[73,128]{1,0:T(8,128)S(1)}, u32[]{:S(2)}, u32[]{:S(2)}) collective-permute-start(f32[73,128]{1,0:T(8,128)S(1)} %add_select_fusion.3), channel_id=1, source_target_pairs={{0,4},{2,6},{4,0},{6,2},{8,12},{10,14},{12,8},{14,10},{16,20},{18,... | collective-permute-start | bytes 112136 | tf_op jit(solution)/shard_map/ppermute | solution.py:555
  146.8 9.2 %collective-permute-start.33 = (f32[73,128]{1,0:T(8,128)S(1)}, f32[73,128]{1,0:T(8,128)S(1)}, u32[]{:S(2)}, u32[]{:S(2)}) collective-permute-start(f32[73,128]{1,0:T(8,128)S(1)} %add_select_fusion.1), channel_id=1, source_target_pairs={{0,16},{2,18},{4,20},{6,22},{8,24},{10,26},{12,28},{14,30},{16,0},... | collective-permute-start | bytes 112136 | tf_op jit(solution)/shard_map/ppermute | solution.py:555
  150.9 15.8 %collective-permute-start.21 = (bf16[512,512]{1,0:T(8,128)(2,1)}, bf16[512,512]{1,0:T(8,128)(2,1)}, u32[]{:S(2)}, u32[]{:S(2)}) collective-permute-start(bf16[512,512]{1,0:T(8,128)(2,1)} %copy-done.10), channel_id=1, source_target_pairs={{0,8},{2,10},{4,12},{6,14},{8,0},{10,2},{12,4},{14,6},{16,24},{18,... | collective-permute-start | bytes 1572872 | tf_op jit(solution)/shard_map/ppermute | solution.py:555
  154.3 15.4 %collective-permute-start.26 = (bf16[256,512]{1,0:T(8,128)(2,1)}, bf16[256,512]{1,0:T(8,128)(2,1)S(1)}, u32[]{:S(2)}, u32[]{:S(2)}) collective-permute-start(bf16[256,512]{1,0:T(8,128)(2,1)} %get-tuple-element.158), channel_id=1, source_target_pairs={{0,16},{2,18},{4,20},{6,22},{8,24},{10,26},{12,28},{14,30},{16,0},... | collective-permute-start | bytes 786440 | tf_op jit(solution)/shard_map/ppermute | solution.py:555
  156.1 6.5 %collective-permute-start.34 = (f32[73,128]{1,0:T(8,128)S(1)}, f32[73,128]{1,0:T(8,128)S(1)}, u32[]{:S(2)}, u32[]{:S(2)}) collective-permute-start(f32[73,128]{1,0:T(8,128)S(1)} %add_select_fusion), channel_id=1, source_target_pairs={{0,1},{1,0},{2,3},{3,2},{4,5},{5,4},{6,7},{7,6},{8,9},{9,8},{10,11... | collective-permute-start | bytes 112136 | tf_op jit(solution)/shard_map/ppermute | solution.py:552
  168.6 11.4 %collective-permute-start.22 = (bf16[256,512]{1,0:T(8,128)(2,1)}, bf16[256,512]{1,0:T(8,128)(2,1)S(1)}, u32[]{:S(2)}, u32[]{:S(2)}) collective-permute-start(bf16[256,512]{1,0:T(8,128)(2,1)} %get-tuple-element.146), channel_id=1, source_target_pairs={{0,16},{2,18},{4,20},{6,22},{8,24},{10,26},{12,28},{14,30},{16,0},... | collective-permute-start | bytes 786440 | tf_op jit(solution)/shard_map/ppermute | solution.py:555
  170.4 12.6 %collective-permute-start.27 = (bf16[64,1024]{1,0:T(8,128)(2,1)S(1)}, bf16[64,1024]{1,0:T(8,128)(2,1)S(1)}, u32[]{:S(2)}, u32[]{:S(2)}) collective-permute-start(bf16[64,1024]{1,0:T(8,128)(2,1)S(1)} %get-tuple-element.160), channel_id=1, source_target_pairs={{0,2},{2,0},{4,6},{6,4},{8,10},{10,8},{12,14},{14,12},{16,18},{18,... | collective-permute-start | bytes 393224 | tf_op jit(solution)/shard_map/ppermute | solution.py:555
  171.2 13.6 %collective-permute-start.28 = (bf16[64,1024]{1,0:T(8,128)(2,1)S(1)}, bf16[64,1024]{1,0:T(8,128)(2,1)S(1)}, u32[]{:S(2)}, u32[]{:S(2)}) collective-permute-start(bf16[64,1024]{1,0:T(8,128)(2,1)S(1)} %get-tuple-element.161), channel_id=1, source_target_pairs={{0,4},{2,6},{4,0},{6,2},{8,12},{10,14},{12,8},{14,10},{16,20},{18,... | collective-permute-start | bytes 393224 | tf_op jit(solution)/shard_map/ppermute | solution.py:555
  172.7 12.2 %collective-permute-start.29 = (bf16[64,1024]{1,0:T(8,128)(2,1)S(1)}, bf16[64,1024]{1,0:T(8,128)(2,1)S(1)}, u32[]{:S(2)}, u32[]{:S(2)}) collective-permute-start(bf16[64,1024]{1,0:T(8,128)(2,1)S(1)} %get-tuple-element.162), channel_id=1, source_target_pairs={{0,6},{2,4},{4,2},{6,0},{8,14},{10,12},{12,10},{14,8},{16,22},{18,... | collective-permute-start | bytes 393224 | tf_op jit(solution)/shard_map/ppermute | solution.py:555
  180.7 5.7 %collective-permute-start.23 = (bf16[64,512]{1,0:T(8,128)(2,1)S(1)}, bf16[64,512]{1,0:T(8,128)(2,1)S(1)}, u32[]{:S(2)}, u32[]{:S(2)}) collective-permute-start(bf16[64,512]{1,0:T(8,128)(2,1)S(1)} %get-tuple-element.148), channel_id=1, source_target_pairs={{0,2},{2,0},{4,6},{6,4},{8,10},{10,8},{12,14},{14,12},{16,18},{18,... | collective-permute-start | bytes 196616 | tf_op jit(solution)/shard_map/ppermute | solution.py:555
  181.5 4.9 %collective-permute-start.24 = (bf16[64,512]{1,0:T(8,128)(2,1)S(1)}, bf16[64,512]{1,0:T(8,128)(2,1)S(1)}, u32[]{:S(2)}, u32[]{:S(2)}) collective-permute-start(bf16[64,512]{1,0:T(8,128)(2,1)S(1)} %get-tuple-element.149), channel_id=1, source_target_pairs={{0,4},{2,6},{4,0},{6,2},{8,12},{10,14},{12,8},{14,10},{16,20},{18,... | collective-permute-start | bytes 196616 | tf_op jit(solution)/shard_map/ppermute | solution.py:555
  183.0 5.2 %collective-permute-start.25 = (bf16[64,512]{1,0:T(8,128)(2,1)S(1)}, bf16[64,512]{1,0:T(8,128)(2,1)S(1)}, u32[]{:S(2)}, u32[]{:S(2)}) collective-permute-start(bf16[64,512]{1,0:T(8,128)(2,1)S(1)} %get-tuple-element.150), channel_id=1, source_target_pairs={{0,6},{2,4},{4,2},{6,0},{8,14},{10,12},{12,10},{14,8},{16,22},{18,... | collective-permute-start | bytes 196616 | tf_op jit(solution)/shard_map/ppermute | solution.py:555
  (38 other events, 209.6 us)
where the time goes:
time: 191 us; the launch traced here: 190 us
  Pallas kernels  62.5 us (33%)
  waiting for transfers between devices  51.6 us (27%)
  starting transfers between devices  47 us (25%)
  local copies, waits for them, and re-layouts  24.5 us (13%)
  other arithmetic  2.14 us (1%)
    pallas_call x17, Pallas kernels, kernel_call(): pl.pallas_call(run, out_shape=shapes, in_specs=specs, out_specs=out_specs...  57.5 us
    ppermute x22, waiting for transfers between devices, hop(): return lax.ppermute(x, 'dp', [(i, i ^ mask) for i in range(n_dp)])  39.4 us
    ppermute x22, starting transfers between devices, hop(): return lax.ppermute(x, 'dp', [(i, i ^ mask) for i in range(n_dp)])  28.8 us
    unnamed x75, local copies, waits for them, and re-layouts  20.9 us
    all_to_all x3, starting transfers between devices, exchange(): return lax.all_to_all(x, 'dp', split_axis=0, concat_axis=0, tiled=True)  16.1 us
    all_to_all x3, waiting for transfers between devices, exchange(): return lax.all_to_all(x, 'dp', split_axis=0, concat_axis=0, tiled=True)  9.13 us
    pallas_call x1, Pallas kernels, local(): pl.pallas_call(clip_kernel, grid=(4,), out_shape=jax.ShapeDtypeStruct((wi...  4.99 us
  transfers between devices with their start and end apart: 38, of which 14 were waited for; matrix products, arithmetic and copies ran while one was open for 5% of the time, Pallas kernels for 30%

commit v1 on v0

--- a/solution.py
+++ b/solution.py
@@ -7,7 +7,7 @@
 from jax.sharding import PartitionSpec as P
 
 HD = 64
-AG_BITS = (0, 1)
+AG_BITS = (0, 2)
 PAD = 128
 COST = 1
 
@@ -106,7 +106,7 @@
 
 class Fetched:
     def __init__(self, ref, copies):
-        self.ref, self.copies, self.shape = ref, copies, ref.shape
+        self.ref, self.copies, self.shape = ref, copies, getattr(ref, "shape", None)
 
     def wait(self, k=None):
         for c in self.copies if k is None else [self.copies[k]]:
@@ -131,8 +131,9 @@
     args = [pltpu.with_memory_space_constraint(a, pltpu.HBM) if i in hbm else a for i, a in enumerate(args)]
     n_in, n_out, n_scratch = len(args), len(outs), len(scratch)
     extra = []
-    for i, (shape, chunks) in hbm.items():
-        extra.append(pltpu.VMEM(shape, args[i].dtype))
+    own = [i for i, (shape, _) in hbm.items() if shape is not None]
+    for i in own:
+        extra.append(pltpu.VMEM(hbm[i][0], args[i].dtype))
     n_chunks = {}
     for i, (shape, chunks) in hbm.items():
         n_chunks[i] = getattr(chunks, "count", 1)
@@ -143,7 +144,8 @@
         rest = refs[n_in + n_out + n_scratch :]
         sc = ins[0]
         for j, (i, (_, chunks)) in enumerate(hbm.items()):
-            dst, sem = rest[j], rest[len(hbm) + j]
+            dst = rest[own.index(i)] if i in own else refs[n_in + n_out :]
+            sem = rest[len(own) + j]
             copies = [
                 pltpu.make_async_copy(a, b, sem.at[k]) for k, (a, b) in enumerate(chunks(ins[i], dst, sc))
             ]
@@ -174,6 +176,20 @@
     return chunks
 
 
+def gathered(own_args, shared_args, rows):
+    spec = {}
+    for i, at in own_args:
+        spec[i] = (None, chunked(1, lambda src, dst, sc, k, at=at: (src, dst[at].at[pl.ds(0, 2 * rows), :])))
+    for j, i in enumerate(shared_args):
+
+        def make(src, dst, sc, k, j=j):
+            width = dst[0].shape[1]
+            return src.at[:, pl.ds(k * width, width)], dst[k].at[pl.ds((2 + j) * rows, rows), :]
+
+        spec[i] = (None, chunked(2, make))
+    return spec
+
+
 def by_row(count):
     return chunked(count, lambda src, dst, sc, k: (src.at[k], dst.at[k]))
 
@@ -196,7 +212,7 @@
     return chunks
 
 
-def route_kernel(n_dp, route, lens, tokens, cotangent, msg, msg_cot, pick_out):
+def route_kernel(n_dp, route, lens, tokens, cotangent, msg, pick_out):
     rows, width = tokens.shape
     row = jnp.broadcast_to(f(route.wait()[...]), (rows, rows))
     col = row.T
@@ -217,8 +233,8 @@
     pick_b = pick.astype(BF16)
     pick_out[...] = pick_b
     msg[:, :width] = nn(pick_b, tokens.wait()[...]).astype(BF16)
-    msg[:, width:] = extra.astype(BF16)
-    msg_cot[...] = nn(pick_b, cotangent.wait()[...]).astype(BF16)
+    msg[:, 2 * width :] = extra.astype(BF16)
+    msg[:, width : 2 * width] = nn(pick_b, cotangent.wait()[...]).astype(BF16)
 
 
 def ends_of(sc):
@@ -235,7 +251,7 @@
     width = w_out.shape[1]
     cols = w_out.shape[0]
     for i, half in enumerate((mine, other)):
-        put = place_matrix(f(half[:, width : width + 1]))
+        put = place_matrix(f(half[:, 2 * width : 2 * width + 1]))
         x = tn(put, half[:, :width])
         s = slice(i * rows, (i + 1) * rows)
         x_out[s, :] = x.astype(BF16)
@@ -273,13 +289,13 @@
     part_out[...] = nn(ctx_out[...], w_out.wait()[...]).astype(BF16)
 
 
-def middle_kernel(x, part, recv, vecs, mine, other, cot_mine, cot_other, middle_out, mid_out, cot_out, msg_out):
-    rows, width = cot_mine.shape
-    for i, (ids, c) in enumerate(((mine, cot_mine), (other, cot_other))):
+def middle_kernel(x, part, recv, vecs, mine, other, middle_out, mid_out, cot_out, msg_out):
+    rows, width = msg_out.shape[0], x.shape[1]
+    for i, half in enumerate((mine, other)):
         s = slice(i * rows, (i + 1) * rows)
         o = slice((1 - i) * rows, (2 - i) * rows)
-        put = place_matrix(f(ids[:, width : width + 1]))
-        cot = tn(put, c[...]).astype(BF16)
+        put = place_matrix(f(half[:, 2 * width : 2 * width + 1]))
+        cot = tn(put, half[:, width : 2 * width]).astype(BF16)
         cot_out[s, :] = cot
         middle = f(x[s, :]) + (f(part[s, :]) + f(recv[o, :])) + vecs[2:3, :]
         middle_out[s, :] = middle
@@ -367,7 +383,7 @@
 
 def last_kernel(part, recv, x, gmid, middle, y_mine, y_other, vecs, ids, msg_out, sums_out):
     rows, width = part.shape
-    put = place_matrix(f(ids[:, width : width + 1]))
+    put = place_matrix(f(ids[:, 2 * width : 2 * width + 1]))
     res = middle[:rows, :] + (y_mine[...] + f(y_other[...])) + vecs[5:6, :]
     msg_out[:, :width] = nn(put, res.astype(BF16)).astype(BF16)
     g = part[...] + f(recv[...])
@@ -404,24 +420,21 @@
         send_out[dst, at] = src[pl.ds(s, run), :].astype(BF16)
 
 
-def gather_rows(own, halves, dst, at):
-    n, width = own.shape
-    dst[:n, :] = own[...]
-    for h in halves:
-        r = h.shape[0]
-        dst[n : n + r, :] = h[:, at * width : (at + 1) * width]
-        n += r
-
-
 def mlp_weights_kernel(
-    n_bits, bit, sc, mid, cot, m1, m2, m3, o1, o2, o3, bias, up, down,
+    n_bits, bit, sc, mid, cot, m1, m2, m3, o1, o2, o3, vecs, up, down,
     send_down, keep_down, send_up, keep_up, mids, cots, grad,
 ):
-    gather_rows(mid, (m1, o1, m2, o2, m3, o3), mids, 0)
-    gather_rows(cot, (m1, o1, m2, o2, m3, o3), cots, 1)
+    for x in (mid, cot, m1, m2, m3, o1, o2, o3):
+        x.wait()
+    q_hidden = down.shape[0]
+    per_row = mids.shape[1] // q_hidden
+    bias = jnp.zeros((1, q_hidden), F32)
+    for k in range(4):
+        part = vecs[6 + k // per_row : 7 + k // per_row, (k % per_row) * q_hidden : (k % per_row + 1) * q_hidden]
+        bias = jnp.where(sc[2] == k, part, bias)
     mine = (sc[1] >> bit) & 1
     run = (mids.shape[1] >> n_bits) << bit
-    act, slope = gelu_parts(nn(mids[...], up.wait()[...]) + f(bias.wait()[...]))
+    act, slope = gelu_parts(nn(mids[...], up.wait()[...]) + bias)
     every = slice(None)
     grad[...] = tn(cots[...], act.astype(BF16))
     split_rows(grad, run, mine, send_down, keep_down, every)
@@ -432,11 +445,11 @@
 
 def attn_weights_kernel(
     n_bits, bit, n_dp, sc, ids, nrm, ga, m1, m2, m3, o1, o2, o3, qv_bias, w_qkv, w_out,
-    send_out, keep_out, norms, gattns, ctx, gqkv, grad,
+    send_out, keep_out, gattns, norms, ctx, gqkv, grad,
 ):
-    gather_rows(ga, (m1, o1, m2, o2, m3, o3), gattns, 0)
-    gather_rows(nrm, (m1, o1, m2, o2, m3, o3), norms, 1)
-    rows = nrm.shape[0] // 2
+    for x in (ga, nrm, m1, m2, m3, o1, o2, o3):
+        x.wait()
+    rows = gattns.shape[0] // 8
     group = 2 * rows
     me = sc[1]
     mine = (me >> bit) & 1
@@ -449,7 +462,7 @@
     v4 = (nn(norm4, w_qkv[2]) + f(qv_bias[1:2, :])).astype(BF16)
     gc4 = nt(gattns[...], w_out.wait()[...]).astype(BF16)
     lanes_b, lanes_f = half_lanes()
-    table = f(ids[:, norms.shape[1] :])
+    table = f(ids[:, 2 * norms.shape[1] :])
     from_dp = iota((rows, 1), 0) // (rows // n_dp)
     first = iota((rows, 1), 0) == from_dp * (rows // n_dp)
     for g in range(4):
@@ -566,15 +579,14 @@
         [attn_norm_gain, attn_norm_bias, out_bias, mlp_norm_gain, mlp_norm_bias, down_bias, up_bias]
     ).astype(F32).reshape(-1, width)
 
-    msg, msg_cot, pick = kernel_call(
+    msg, pick = kernel_call(
         functools.partial(route_kernel, n_dp),
-        [((rows, width + PAD), BF16), ((rows, width), BF16), ((rows, rows), BF16)],
+        [((rows, 2 * width + PAD), BF16), ((rows, rows), BF16)],
         [route.reshape(1, rows), lengths, tokens, cotangent],
         hbm={0: whole((1, rows)), 1: whole(lengths.shape), 2: whole(tokens.shape), 3: whole(tokens.shape)},
         flops=4 * rows * rows * width,
     )
     got = after(exchange(msg), vecs, sc)
-    got_cot = exchange(msg_cot)
     other = swap(got)
     x, normed, qkv, lse, tops, part = kernel_call(
         attn_kernel,
@@ -596,7 +608,7 @@
     middle, mid, cot, msg_mlp = kernel_call(
         middle_kernel,
         [((group, width), F32), ((group, width), BF16), ((group, width), BF16), ((rows, 2 * width), BF16)],
-        [x, part, swap(part), vecs, got, other, got_cot, swap(got_cot)],
+        [x, part, swap(part), vecs, got, other],
         flops=1 << 28,
     )
     m1, m2 = (hop(msg_mlp, m) for m in masks[:2])
@@ -640,6 +652,25 @@
         [gn_mine, gn_recv, x, gmid, middle, mlp_mine, swap(mlp_other), vecs, got],
         flops=1 << 28,
     )
+
+    n_vec = 6 * width
+    sums = jnp.concatenate(
+        [
+            norm_sums.reshape(-1),
+            mid_sums[:4].reshape(-1),
+            qkv_sums[0],
+            qkv_sums[2],
+            up_sums.reshape(-1),
+        ]
+    )
+    n_sum = sums.size
+    msg = jnp.concatenate([sums, jnp.pad(tops[:, 0], (0, PAD - tops.shape[0]))]).reshape(-1, PAD)
+    is_top = iota(msg.shape, 0) == n_sum // PAD
+
+    def combine(msg, *came):
+        return functools.reduce(lambda a, b: jnp.where(is_top, jnp.maximum(a, b), a + b), (msg, *came))
+
+    came = [hop(msg, m) for m in masks]
     restored = exchange(back)
 
     block = width // n_dp
@@ -661,10 +692,10 @@
     send_down, keep_down, send_up, keep_up = kernel_call(
         functools.partial(mlp_weights_kernel, n_bits, first),
         [half[0], half[1], half[0], half[1]],
-        [sc, after(mid, norm_sums), cot] + mlp_shared + [up_bias.reshape(1, hidden), up_weight, down_weight],
+        [sc, after(mid, norm_sums), cot] + mlp_shared + [vecs, up_weight, down_weight],
         smem=(0,),
         hbm={
-            9: ((1, q_hidden), columns(q_hidden, 1)),
+            **gathered([(1, 0), (2, 1)], [3, 6, 4, 7, 5, 8], rows),
             10: ((width, q_hidden), columns(q_hidden, 1)),
             11: ((q_hidden, width), columns(q_hidden, 0)),
         },
@@ -676,53 +707,21 @@
             pltpu.VMEM((width, q_hidden), F32),
         ],
     )
-    send_down, send_up, a1, a2, restored = lax.optimization_barrier((send_down, send_up, a1, a2, restored))
-    recv_down = hop(send_down, 1 << first)
+    send_down, send_up, a1, a2, restored, *came = lax.optimization_barrier(
+        (send_down, send_up, a1, a2, restored, *came)
+    )
+    msg = combine(msg, *came)
     a3 = hop(after(msg_attn, send_up), masks[2])
     b1, b2 = swap(a1), swap(a2)
-    a3, recv_down, b1, b2, send_up = lax.optimization_barrier((a3, recv_down, b1, b2, send_up))
-    send_down, keep_down = step(1, recv_down, keep_down)
-    recv_down, recv_up = hop(send_down, 1 << rs_bits[1]), hop(send_up, 1 << first)
-    attn_shared = [a1, a2, a3, b1, b2, swap(a3)]
+    recv_down = hop(send_down, 1 << first)
+
     out_tokens, grad_tokens = kernel_call(
         restore_kernel, [((rows, width), BF16)] * 2, [pick, restored], flops=1 << 27
     )
-
-    send_attn, keep_attn = kernel_call(
-        functools.partial(attn_weights_kernel, n_bits, first, n_dp),
-        [((width // 2, 4 * q_cols), BF16), ((width // 2, 4 * q_cols), F32)],
-        [sc, got, after(normed, send_up), gattn] + attn_shared + [qv_bias, w_qkv, out_weight],
-        smem=(0,),
-        hbm={
-            10: ((2, q_cols), columns(q_cols, 1)),
-            11: ((3, width, q_cols), columns(q_cols, 1)),
-            12: ((q_cols, width), columns(q_cols, 0)),
-        },
-        limit=28,
-        flops=2 * 4 * group * width * q_cols * 12,
-        scratch=[
-            pltpu.VMEM((4 * group, width), BF16),
-            pltpu.VMEM((4 * group, width), BF16),
-            pltpu.VMEM((4 * group, q_cols), BF16),
-            pltpu.VMEM((4 * group, 3 * q_cols), BF16),
-            pltpu.VMEM((width, 4 * q_cols), F32),
-        ],
-    )
-
-    send_attn, recv_down, recv_up = lax.optimization_barrier((send_attn, recv_down, recv_up))
-    attn_done = send_attn
-
-    recv_attn = hop(send_attn, 1 << first)
-    send_up, keep_up = step(1, recv_up, keep_up)
-    recv_up = hop(send_up, 1 << rs_bits[1])
-    send_attn, keep_attn = step(1, recv_attn, keep_attn)
-    recv_attn = hop(send_attn, 1 << rs_bits[1])
-
-    def rest(recv, keep):
-        for i in range(2, len(rs_bits)):
-            send, keep = step(i, recv, keep)
-            recv = hop(send, 1 << rs_bits[i])
-        return keep, recv
+    a3, b1, b2, recv_down, out_tokens, grad_tokens = lax.optimization_barrier(
+        (a3, b1, b2, recv_down, out_tokens, grad_tokens)
+    )
+    attn_shared = [a1, a2, a3, b1, b2, swap(a3)]
 
     def hand_out(*pairs):
         n, w = pairs[0][0].shape
@@ -737,11 +736,81 @@
         )
         return [pieces[0]] + [hop(p, m) for p, m in zip(pieces[1:], masks)]
 
-    mlp_pieces = hand_out(rest(recv_down, keep_down), rest(recv_up, keep_up))
-    attn_pieces = hand_out(rest(recv_attn, keep_attn))
+    def clip(msg):
+        threshold = clip_tau[0].astype(F32)
+        head_factor = jnp.sqrt(threshold / jnp.maximum(msg[-1, : tops.shape[0]], threshold))
+        column_factor = jnp.repeat(head_factor, HD)
+        clipped_qk = pl.pallas_call(
+            clip_kernel,
+            grid=(4,),
+            out_shape=jax.ShapeDtypeStruct((width, 2, cols), BF16),
+            in_specs=[
+                pl.BlockSpec((2, width // 4, cols), lambda i: (0, i, 0)),
+                pl.BlockSpec((1, cols), lambda i: (0, 0)),
+            ],
+            out_specs=pl.BlockSpec((width // 4, 2, cols), lambda i: (i, 0, 0)),
+            name="clip_kernel",
+        )(w_qkv, column_factor.reshape(1, cols))
+        return clipped_qk, head_factor, column_factor
+
+    n_steps = len(rs_bits)
+    recvs = {0: recv_down}
+    sends = {1: send_up}
+    keeps = {0: keep_down, 1: keep_up}
+    for t in range(1, n_steps + 2):
+        active = [i for i in range(3) if 0 <= t - i < n_steps]
+        gate = ()
+        for i in active:
+            if t > i:
+                sends[i], keeps[i] = step(t - i, recvs[i], keeps[i])
+                gate = (sends[i],)
+        for i in active:
+            recvs[i] = hop(after(sends[i], *gate), 1 << rs_bits[t - i])
+        extra = []
+        if t <= n_steps:
+            msg = after(msg, *gate)
+            came = hop(msg, 1 << rs_bits[t - 1])
+        if t == 1:
+            send_attn, keep_attn = kernel_call(
+                functools.partial(attn_weights_kernel, n_bits, first, n_dp),
+                [((width // 2, 4 * q_cols), BF16), ((width // 2, 4 * q_cols), F32)],
+                [sc, got, normed, gattn] + attn_shared + [qv_bias, w_qkv, out_weight],
+                smem=(0,),
+                hbm={
+                    **gathered([(2, 1), (3, 0)], [4, 7, 5, 8, 6, 9], rows),
+                    10: ((2, q_cols), columns(q_cols, 1)),
+                    11: ((3, width, q_cols), columns(q_cols, 1)),
+                    12: ((q_cols, width), columns(q_cols, 0)),
+                },
+                limit=28,
+                flops=2 * 4 * group * width * q_cols * 12,
+                scratch=[
+                    pltpu.VMEM((4 * group, width), BF16),
+                    pltpu.VMEM((4 * group, width), BF16),
+                    pltpu.VMEM((4 * group, q_cols), BF16),
+                    pltpu.VMEM((4 * group, 3 * q_cols), BF16),
+                    pltpu.VMEM((width, 4 * q_cols), F32),
+                ],
+            )
+            sends[2], keeps[2] = send_attn, keep_attn
+            extra = [sends[2]]
+        if t == n_steps + 1:
+            mlp_pieces = hand_out((after(keeps[0], *gate), recvs[0]), (keeps[1], recvs[1]))
+            clipped_qk, head_factor, column_factor = clip(msg)
+            extra = mlp_pieces[1:] + [clipped_qk]
+        done = lax.optimization_barrier([recvs[i] for i in active] + [came] + extra)
+        recvs.update(zip(active, done))
+        if t <= n_steps:
+            msg = combine(msg, done[len(active)])
+        if t == 1:
+            sends[2] = done[-1]
+        if t == n_steps + 1:
+            mlp_pieces[1:], clipped_qk = done[-4:-1], done[-1]
+    attn_pieces = hand_out((keeps[2], recvs[2]))
     grad_down, grad_up = kernel_call(
         join_mlp_kernel, [((block, hidden), F32), ((block, hidden), F32)], [sc] + mlp_pieces, smem=(0,)
     )
+    grad_down, grad_up, *attn_pieces[1:] = lax.optimization_barrier((grad_down, grad_up, *attn_pieces[1:]))
     grad_down = grad_down.T
     grad_qkv, grad_out = kernel_call(
         join_attn_kernel, [((3, block, cols), F32), ((block, cols), F32)], [sc] + attn_pieces, smem=(0,)
@@ -749,24 +818,6 @@
     grad_qkv = jnp.transpose(grad_qkv, (1, 0, 2))
     grad_out = grad_out.T
 
-    n_vec = 6 * width
-    sums = jnp.concatenate(
-        [
-            norm_sums.reshape(-1),
-            mid_sums[:4].reshape(-1),
-            qkv_sums[0],
-            qkv_sums[2],
-            up_sums.reshape(-1),
-        ]
-    )
-    n_sum = sums.size
-    sums = after(sums, attn_done)
-    msg = jnp.concatenate([sums, jnp.pad(tops[:, 0], (0, PAD - tops.shape[0]))]).reshape(-1, PAD)
-    is_top = iota(msg.shape, 0) == n_sum // PAD
-    for b in range(n_bits):
-        came = hop(msg, 1 << b)
-        msg = jnp.where(is_top, jnp.maximum(msg, came), msg + came)
-    global_top = msg[-1, : tops.shape[0]]
     theirs = swap(msg).reshape(-1)
     msg = msg.reshape(-1)
     vector_sum = (msg[:n_vec] + theirs[:n_vec]).reshape(6, width)
@@ -781,20 +832,6 @@
     )
     up_sum = jnp.concatenate([one[2 * cols :], two[2 * cols :]])
 
-    threshold = clip_tau[0].astype(F32)
-    head_factor = jnp.sqrt(threshold / jnp.maximum(global_top, threshold))
-    column_factor = jnp.repeat(head_factor, HD)
-    clipped_qk = pl.pallas_call(
-        clip_kernel,
-        grid=(4,),
-        out_shape=jax.ShapeDtypeStruct((width, 2, cols), BF16),
-        in_specs=[
-            pl.BlockSpec((2, width // 4, cols), lambda i: (0, i, 0)),
-            pl.BlockSpec((1, cols), lambda i: (0, 0)),
-        ],
-        out_specs=pl.BlockSpec((width // 4, 2, cols), lambda i: (i, 0, 0)),
-        name="clip_kernel",
-    )(w_qkv, column_factor.reshape(1, cols))
     clipped_q_bias = (f(qv_bias[0]) * column_factor).astype(BF16)
     return (
         out_tokens,

time: 191 us -> 175 us (0.916)
  local copies, waits for them, and re-layouts: 24.5 us -> 12.2 us
  starting transfers between devices: 47 us -> 43.4 us
  Pallas kernels: 62.5 us -> 65.2 us
    unnamed x75 -> x52, local copies, waits for them, and re-layouts: 20.9 us -> 9.21 us
    all_to_all x3 -> x2, starting transfers between devices: 16.1 us -> 11.9 us  [exchange(): return lax.all_to_all(x, 'dp', split_axis=0, concat_axis=0, tiled=True)]
    ppermute x22 -> x23, waiting for transfers between devices: 39.4 us -> 35.9 us  [hop(): return lax.ppermute(x, 'dp', [(i, i ^ mask) for i in range(n_dp)])]
    pallas_call x17, Pallas kernels: 57.5 us -> 60.2 us  [kernel_call(): pl.pallas_call(run, out_shape=shapes, in_specs=specs, out_specs=out_specs...]
    all_to_all x3 -> x2, waiting for transfers between devices: 9.13 us -> 10.1 us  [exchange(): return lax.all_to_all(x, 'dp', split_axis=0, concat_axis=0, tiled=True)]
    ppermute x22 -> x23, starting transfers between devices: 28.8 us -> 29.8 us  [hop(): return lax.ppermute(x, 'dp', [(i, i ^ mask) for i in range(n_dp)])]
  transfers between devices with their start and end apart: 38 -> 37, of which waited for: 14 -> 14; matrix products, arithmetic and copies ran while one was open for 5% -> 5% of each run, Pallas kernels for 30% -> 30%
where the time goes in v1:
time: 175 us; the launch traced here: 174 us
  Pallas kernels  65.2 us (37%)
  waiting for transfers between devices  49.8 us (28%)
  starting transfers between devices  43.4 us (25%)
  local copies, waits for them, and re-layouts  12.2 us (7%)
  other arithmetic  2.07 us (1%)
  between operations  1.76 us (1%)
    pallas_call x17, Pallas kernels, kernel_call(): pl.pallas_call(run, out_shape=shapes, in_specs=specs, out_specs=out_specs...  60.2 us
    ppermute x23, waiting for transfers between devices, hop(): return lax.ppermute(x, 'dp', [(i, i ^ mask) for i in range(n_dp)])  35.9 us
    ppermute x23, starting transfers between devices, hop(): return lax.ppermute(x, 'dp', [(i, i ^ mask) for i in range(n_dp)])  29.8 us
    all_to_all x2, starting transfers between devices, exchange(): return lax.all_to_all(x, 'dp', split_axis=0, concat_axis=0, tiled=True)  11.9 us
    all_to_all x2, waiting for transfers between devices, exchange(): return lax.all_to_all(x, 'dp', split_axis=0, concat_axis=0, tiled=True)  10.1 us
    unnamed x52, local copies, waits for them, and re-layouts  9.21 us
    pallas_call x1, Pallas kernels, clip(): pl.pallas_call(clip_kernel, grid=(4,), out_shape=jax.ShapeDtypeStruct((wi...  4.99 us
    ppermute x12, waiting for transfers between devices, swap(): return lax.ppermute(x, 'tensor', [(0, 1), (1, 0)])  3.75 us
  transfers between devices with their start and end apart: 37, of which 14 were waited for; matrix products, arithmetic and copies ran while one was open for 5% of the time, Pallas kernels for 30%

profile of v1, /device:TPU:0, one launch (start us, length us, event | category | flops | bytes accessed | tf_op | source)
XLA Modules:
  0.0 174.3 jit_solution(16600552964643044809)
XLA Ops:
  0.6 2.3 %route_kernel.1 = (bf16[128,2176]{1,0:T(8,128)(2,1)}, bf16[128,128]{1,0:T(8,128)(2,1)S(1)}) custom-call(s32[1,128]{1,0:T(1,128)} %bitcast.64, s32[1,4]{1,0:T(1,128)} %refs_1_.1, bf16[128,1024]{1,0:T(8,128)(2,1)} %refs_2_.2, bf16[128,1024]{1,0:T(8,128)(2,1)} %refs_3_.2), custom_call_target="tpu_custom_call" | custom-call | flops 67108864 | bytes 524816 | tf_op jit(solution)/shard_map/route_kernel/pallas_call | solution.py:157
  2.9 8.4 %all-to-all-start = ((bf16[16,8,2176]{2,1,0:T(8,128)(2,1)}), bf16[16,8,2176]{2,1,0:T(8,128)(2,1)S(1)}, u32[]{:S(2)}, u32[]{:S(2)}) async-start(bf16[16,8,2176]{2,1,0:T(8,128)(2,1)} %bitcast.5), calls=%async_computation | async-start | bytes 1114112 | tf_op jit(solution)/shard_map/all_to_all | solution.py:571
  16.9 10.1 %all-to-all-done = bf16[16,8,2176]{2,1,0:T(8,128)(2,1)S(1)} async-done(((bf16[16,8,2176]{2,1,0:T(8,128)(2,1)}), bf16[16,8,2176]{2,1,0:T(8,128)(2,1)S(1)}, u32[]{:S(2)}, u32[]{:S(2)}) %all-to-all-start) | async-done | bytes 557088 | tf_op jit(solution)/shard_map/all_to_all | solution.py:571
  26.9 2.0 %collective-permute-done.refs_2_.refs_5_ = bf16[128,2176]{1,0:T(8,128)(2,1)S(1)} collective-permute-done((bf16[128,2176]{1,0:T(8,128)(2,1)S(1)}, bf16[128,2176]{1,0:T(8,128)(2,1)S(1)}, u32[]{:S(2)}, u32[]{:S(2)}) %collective-permute-start) | collective-permute-done | bytes 557088 | tf_op jit(solution)/shard_map/ppermute | solution.py:565
  28.9 5.2 %attn_kernel.1 = (bf16[256,1024]{1,0:T(8,128)(2,1)S(1)}, bf16[256,1024]{1,0:T(8,128)(2,1)S(1)}, bf16[256,1536]{1,0:T(8,128)(2,1)S(1)}, f32[256,128]{1,0:T(8,128)...) custom-call(s32[8]{0:T(128)S(1)} %concatenate.18.refs_0_, bf16[128,2176]{1,0:T(8,128)(2,1)S(1)} %bitcast.44, ...), custom_call_target="tpu_custom_call" | custom-call | flops 3221225472 | bytes 5343264 | tf_op jit(solution)/shard_map/attn_kernel/pallas_call | solution.py:157
  34.3 1.8 %collective-permute-done.1.refs_2_ = bf16[256,1024]{1,0:T(8,128)(2,1)S(1)} collective-permute-done((bf16[256,1024]{1,0:T(8,128)(2,1)S(1)}, bf16[256,1024]{1,0:T(8,128)(2,1)S(1)}, u32[]{:S(2)}, u32[]{:S(2)}) %collective-permute-start.1) | collective-permute-done | bytes 524320 | tf_op jit(solution)/shard_map/ppermute | solution.py:565
  38.8 8.8 %mlp_kernel.1 = (bf16[256,1024]{1,0:T(8,128)(2,1)S(1)}, f32[128,1024]{1,0:T(8,128)S(1)}, bf16[128,1024]{1,0:T(8,128)(2,1)S(1)}, f32[1,2048]{1,0:T(1,128)S(1)}) custom-call(bf16[256,1024]{1,0:T(8,128)(2,1)S(1)} %get-tuple-element.140.refs_0_.refs_1_, bf16[256,1024]{1,0:T(8,128)(2,1)S(1)} %get-tuple-element.119.refs_1_.refs_3_.refs_2_, ...), custom_call_target="tpu_custom_call" | custom-call | flops 4294967296 | bytes 9469952 | tf_op jit(solution)/shard_map/mlp_kernel/pallas_call | solution.py:157
  47.6 3.2 %collective-permute-done.2.refs_3_ = bf16[128,2048]{1,0:T(8,128)(2,1)S(1)} collective-permute-done((bf16[128,2048]{1,0:T(8,128)(2,1)S(1)}, bf16[128,2048]{1,0:T(8,128)(2,1)S(1)}, u32[]{:S(2)}, u32[]{:S(2)}) %collective-permute-start.2) | collective-permute-done | bytes 524320 | tf_op jit(solution)/shard_map/ppermute | solution.py:568
  51.1 2.3 %collective-permute-start.5 = (bf16[128,2048]{1,0:T(8,128)(2,1)S(1)}, bf16[128,2048]{1,0:T(8,128)(2,1)S(1)}, u32[]{:S(2)}, u32[]{:S(2)}) collective-permute-start(bf16[128,2048]{1,0:T(8,128)(2,1)S(1)} %get-tuple-element.130), channel_id=1, source_target_pairs={{0,10},{2,8},{4,14},{6,12},{8,2},{10,0},{12,6},{14,4},{16,26},{18,... | collective-permute-start | bytes 1572872 | tf_op jit(solution)/shard_map/ppermute | solution.py:568
  54.4 1.6 gmid_kernel.1
  56.0 7.7 %attn_grad_kernel.1 = (f32[128,1024]{1,0:T(8,128)S(1)}, bf16[128,1024]{1,0:T(8,128)(2,1)S(1)}, f32[3,512]{1,0:T(4,128)S(1)}) custom-call(s32[8]{0:T(128)S(1)} %concatenate.18.refs_0_, bf16[256,1024]{1,0:T(8,128)(2,1)S(1)} %get-tuple-element.126.refs_1_.refs_3_, bf16[512,1024]{1,0:T(8,128)(2,1)} %refs_12_.1, ...), custom_call_target="tpu_custom_call" | custom-call | flops 3221225472 | bytes 5636128 | tf_op jit(solution)/shard_map/attn_grad_kernel/pallas_call | solution.py:157
  63.7 2.6 %collective-permute-done.5.refs_5_ = bf16[128,2048]{1,0:T(8,128)(2,1)S(1)} collective-permute-done((bf16[128,2048]{1,0:T(8,128)(2,1)S(1)}, bf16[128,2048]{1,0:T(8,128)(2,1)S(1)}, u32[]{:S(2)}, u32[]{:S(2)}) %collective-permute-start.5) | collective-permute-done | bytes 524320 | tf_op jit(solution)/shard_map/ppermute | solution.py:568
  66.4 1.5 collective-permute-start.11
  69.4 1.6 last_kernel.1
  71.0 3.6 %all-to-all-start.1 = ((bf16[16,8,2048]{2,1,0:T(8,128)(2,1)}), bf16[16,8,2048]{2,1,0:T(8,128)(2,1)S(1)}, u32[]{:S(2)}, u32[]{:S(2)}) async-start(bf16[16,8,2048]{2,1,0:T(8,128)(2,1)} %bitcast.8), calls=%async_computation.1 | async-start | bytes 1048576 | tf_op jit(solution)/shard_map/all_to_all | solution.py:571
  74.7 1.9 %collective-permute-start.13 = (f32[73,128]{1,0:T(8,128)S(1)}, f32[73,128]{1,0:T(8,128)S(1)}, u32[]{:S(2)}, u32[]{:S(2)}) collective-permute-start(f32[73,128]{1,0:T(8,128)S(1)} %bitcast.55), channel_id=1, source_target_pairs={{0,2},{2,0},{4,6},{6,4},{8,10},{10,8},{12,14},{14,12},{16,18},{18,... | collective-permute-start | bytes 112136 | tf_op jit(solution)/shard_map/ppermute | solution.py:568
  79.1 9.5 %mlp_weights_kernel.1 = (bf16[512,512]{1,0:T(8,128)(2,1)S(1)}, f32[512,512]{1,0:T(8,128)S(1)}, bf16[512,512]{1,0:T(8,128)(2,1)S(1)}, f32[512,512]{1,0:T(8,128)S(1)}) custom-call(s32[8]{0:T(128)S(1)} %concatenate.18.refs_0_, bf16[256,1024]{1,0:T(8,128)(2,1)} %copy-done.5, bf16[256,1024]{1,0:T(8,128)(2,1)} %copy-done.1, bf16[128,2048]{1,0:T(8,128)(2,1)} %copy-done.10, ...), custom_call_target="tpu_custom_call" | custom-call | flops 4294967296 | bytes 12615712 | tf_op jit(solution)/shard_map/mlp_weights_kernel/pallas_call | solution.py:157
  90.1 1.8 %collective-permute-done.14 = f32[73,128]{1,0:T(8,128)S(1)} collective-permute-done((f32[73,128]{1,0:T(8,128)S(1)}, f32[73,128]{1,0:T(8,128)S(1)}, u32[]{:S(2)}, u32[]{:S(2)}) %collective-permute-start.14) | collective-permute-done | bytes 37408 | tf_op jit(solution)/shard_map/ppermute | solution.py:568
  92.4 2.4 %collective-permute-start.16 = (bf16[128,2048]{1,0:T(8,128)(2,1)}, bf16[128,2048]{1,0:T(8,128)(2,1)S(1)}, u32[]{:S(2)}, u32[]{:S(2)}) collective-permute-start(bf16[128,2048]{1,0:T(8,128)(2,1)} %get-tuple-element.152), channel_id=1, source_target_pairs={{0,10},{2,8},{4,14},{6,12},{8,2},{10,0},{12,6},{14,4},{16,26},{18,... | collective-permute-start | bytes 1572872 | tf_op jit(solution)/shard_map/ppermute | solution.py:568
  97.3 9.4 %collective-permute-done.16.refs_6_ = bf16[128,2048]{1,0:T(8,128)(2,1)S(1)} collective-permute-done((bf16[128,2048]{1,0:T(8,128)(2,1)}, bf16[128,2048]{1,0:T(8,128)(2,1)S(1)}, u32[]{:S(2)}, u32[]{:S(2)}) %collective-permute-start.16) | collective-permute-done | bytes 524320 | tf_op jit(solution)/shard_map/ppermute | solution.py:568
  106.7 2.6 %collective-permute-done.19.refs_2_ = bf16[512,512]{1,0:T(8,128)(2,1)S(1)} collective-permute-done((bf16[512,512]{1,0:T(8,128)(2,1)}, bf16[512,512]{1,0:T(8,128)(2,1)S(1)}, u32[]{:S(2)}, u32[]{:S(2)}) %collective-permute-start.19) | collective-permute-done | bytes 524320 | tf_op jit(solution)/shard_map/ppermute | solution.py:568
  111.2 1.9 %collective-permute-start.21 = (bf16[256,512]{1,0:T(8,128)(2,1)S(1)}, bf16[256,512]{1,0:T(8,128)(2,1)S(1)}, u32[]{:S(2)}, u32[]{:S(2)}) collective-permute-start(bf16[256,512]{1,0:T(8,128)(2,1)S(1)} %get-tuple-element.170), channel_id=1, source_target_pairs={{0,16},{2,18},{4,20},{6,22},{8,24},{10,26},{12,28},{14,30},{16,0},... | collective-permute-start | bytes 786440 | tf_op jit(solution)/shard_map/ppermute | solution.py:568
  114.2 13.9 %attn_weights_kernel.1 = (bf16[512,512]{1,0:T(8,128)(2,1)}, f32[512,512]{1,0:T(8,128)S(1)}) custom-call(s32[8]{0:T(128)S(1)} %concatenate.18.refs_0_, bf16[128,2176]{1,0:T(8,128)(2,1)S(1)} %bitcast.47, bf16[256,1024]{1,0:T(8,128)(2,1)} %copy-done, bf16[256,1024]{1,0:T(8,128)(2,1)} %copy-done.4, bf16[128,2048]{1,0:T(8,128)(2,1)} %collective-permute-done.11.refs_4_, ...), custom_call_target="tpu_custom_call" | custom-call | flops 3221225472 | bytes 8947744 | tf_op jit(solution)/shard_map/attn_weights_kernel/pallas_call | solution.py:157
  130.4 1.8 %collective-permute-start.25 = (bf16[512,512]{1,0:T(8,128)(2,1)}, bf16[512,512]{1,0:T(8,128)(2,1)S(1)}, u32[]{:S(2)}, u32[]{:S(2)}) collective-permute-start(bf16[512,512]{1,0:T(8,128)(2,1)} %get-tuple-element.181), channel_id=1, source_target_pairs={{0,4},{2,6},{4,0},{6,2},{8,12},{10,14},{12,8},{14,10},{16,20},{18,... | collective-permute-start | bytes 1572872 | tf_op jit(solution)/shard_map/ppermute | solution.py:568
  133.3 1.9 %collective-permute-start.26 = (f32[73,128]{1,0:T(8,128)S(1)}, f32[73,128]{1,0:T(8,128)S(1)}, u32[]{:S(2)}, u32[]{:S(2)}) collective-permute-start(f32[73,128]{1,0:T(8,128)S(1)} %add_select_fusion.1), channel_id=1, source_target_pairs={{0,16},{2,18},{4,20},{6,22},{8,24},{10,26},{12,28},{14,30},{16,0},... | collective-permute-start | bytes 112136 | tf_op jit(solution)/shard_map/ppermute | solution.py:568
  135.9 11.7 %collective-permute-done.26 = f32[73,128]{1,0:T(8,128)S(1)} collective-permute-done((f32[73,128]{1,0:T(8,128)S(1)}, f32[73,128]{1,0:T(8,128)S(1)}, u32[]{:S(2)}, u32[]{:S(2)}) %collective-permute-start.26) | collective-permute-done | bytes 37408 | tf_op jit(solution)/shard_map/ppermute | solution.py:568
  147.6 1.5 step_kernel.5
  151.6 2.3 %collective-permute-start.29 = (bf16[64,1024]{1,0:T(8,128)(2,1)S(1)}, bf16[64,1024]{1,0:T(8,128)(2,1)S(1)}, u32[]{:S(2)}, u32[]{:S(2)}) collective-permute-start(bf16[64,1024]{1,0:T(8,128)(2,1)S(1)} %get-tuple-element.194), channel_id=1, source_target_pairs={{0,8},{2,10},{4,12},{6,14},{8,0},{10,2},{12,4},{14,6},{16,24},{18,... | collective-permute-start | bytes 393224 | tf_op jit(solution)/shard_map/ppermute | solution.py:568
  156.4 5.0 %clip_kernel.1 = bf16[1024,2,512]{2,1,0:T(2,128)(2,1)} custom-call(bf16[3,1024,512]{2,1,0:T(8,128)(2,1)} %bitcast.54, f32[1,512]{1,0:T(1,128)} %reshape_reshape.3.factor), custom_call_target="tpu_custom_call" | custom-call | tf_op jit(solution)/shard_map/clip_kernel/pallas_call | solution.py:743
  163.4 2.4 %collective-permute-done.30.refs_4_ = bf16[64,1024]{1,0:T(8,128)(2,1)S(1)} collective-permute-done((bf16[64,1024]{1,0:T(8,128)(2,1)S(1)}, bf16[64,1024]{1,0:T(8,128)(2,1)S(1)}, u32[]{:S(2)}, u32[]{:S(2)}) %collective-permute-start.30) | collective-permute-done | bytes 131104 | tf_op jit(solution)/shard_map/ppermute | solution.py:568
  167.3 2.7 %collective-permute-start.33 = (bf16[64,512]{1,0:T(8,128)(2,1)S(1)}, bf16[64,512]{1,0:T(8,128)(2,1)S(1)}, u32[]{:S(2)}, u32[]{:S(2)}) collective-permute-start(bf16[64,512]{1,0:T(8,128)(2,1)S(1)} %get-tuple-element.207), channel_id=1, source_target_pairs={{0,10},{2,8},{4,14},{6,12},{8,2},{10,0},{12,6},{14,4},{16,26},{18,... | collective-permute-start | bytes 196616 | tf_op jit(solution)/shard_map/ppermute | solution.py:568
  170.6 1.6 join_mlp_kernel.1
  (137 shorter events, 36.1 us)
Async XLA Ops:
  2.9 24.0 %all-to-all-start = ((bf16[16,8,2176]{2,1,0:T(8,128)(2,1)}), bf16[16,8,2176]{2,1,0:T(8,128)(2,1)S(1)}, u32[]{:S(2)}, u32[]{:S(2)}) async-start(bf16[16,8,2176]{2,1,0:T(8,128)(2,1)} %bitcast.5), calls=%async_computation | async-start | bytes 1114112 | tf_op jit(solution)/shard_map/all_to_all | solution.py:571
  36.8 14.0 %collective-permute-start.2 = (bf16[128,2048]{1,0:T(8,128)(2,1)S(1)}, bf16[128,2048]{1,0:T(8,128)(2,1)S(1)}, u32[]{:S(2)}, u32[]{:S(2)}) collective-permute-start(bf16[128,2048]{1,0:T(8,128)(2,1)S(1)} %get-tuple-element.130), channel_id=1, source_target_pairs={{0,2},{2,0},{4,6},{6,4},{8,10},{10,8},{12,14},{14,12},{16,18},{18,... | collective-permute-start | bytes 1572872 | tf_op jit(solution)/shard_map/ppermute | solution.py:568
  37.4 13.7 %collective-permute-start.3 = (bf16[128,2048]{1,0:T(8,128)(2,1)S(1)}, bf16[128,2048]{1,0:T(8,128)(2,1)S(1)}, u32[]{:S(2)}, u32[]{:S(2)}) collective-permute-start(bf16[128,2048]{1,0:T(8,128)(2,1)S(1)} %get-tuple-element.130), channel_id=1, source_target_pairs={{0,8},{2,10},{4,12},{6,14},{8,0},{10,2},{12,4},{14,6},{16,24},{18,... | collective-permute-start | bytes 1572872 | tf_op jit(solution)/shard_map/ppermute | solution.py:568
  51.1 15.2 %collective-permute-start.5 = (bf16[128,2048]{1,0:T(8,128)(2,1)S(1)}, bf16[128,2048]{1,0:T(8,128)(2,1)S(1)}, u32[]{:S(2)}, u32[]{:S(2)}) collective-permute-start(bf16[128,2048]{1,0:T(8,128)(2,1)S(1)} %get-tuple-element.130), channel_id=1, source_target_pairs={{0,10},{2,8},{4,14},{6,12},{8,2},{10,0},{12,6},{14,4},{16,26},{18,... | collective-permute-start | bytes 1572872 | tf_op jit(solution)/shard_map/ppermute | solution.py:568
  53.4 12.9 %collective-permute-start.6 = (bf16[128,2048]{1,0:T(8,128)(2,1)S(1)}, bf16[128,2048]{1,0:T(8,128)(2,1)S(1)}, u32[]{:S(2)}, u32[]{:S(2)}) collective-permute-start(bf16[128,2048]{1,0:T(8,128)(2,1)S(1)} %collective-permute-done.2.refs_3_), channel_id=1, source_target_pairs={{0,1},{1,0},{2,3},{3,2},{4,5},{5,4},{6,7},{7,6},{8,9},{9,8},{10,11... | collective-permute-start | bytes 1572872 | tf_op jit(solution)/shard_map/ppermute | solution.py:565
  53.7 12.7 %collective-permute-start.7 = (bf16[128,2048]{1,0:T(8,128)(2,1)S(1)}, bf16[128,2048]{1,0:T(8,128)(2,1)S(1)}, u32[]{:S(2)}, u32[]{:S(2)}) collective-permute-start(bf16[128,2048]{1,0:T(8,128)(2,1)S(1)} %collective-permute-done.3.refs_4_), channel_id=1, source_target_pairs={{0,1},{1,0},{2,3},{3,2},{4,5},{5,4},{6,7},{7,6},{8,9},{9,8},{10,11... | collective-permute-start | bytes 1572872 | tf_op jit(solution)/shard_map/ppermute | solution.py:565
  54.1 15.4 %collective-permute-start.9 = (bf16[128,1024]{1,0:T(8,128)(2,1)S(1)}, bf16[128,1024]{1,0:T(8,128)(2,1)S(1)}, u32[]{:S(2)}, u32[]{:S(2)}) collective-permute-start(bf16[128,1024]{1,0:T(8,128)(2,1)S(1)} %get-tuple-element.138), channel_id=1, source_target_pairs={{0,1},{1,0},{2,3},{3,2},{4,5},{5,4},{6,7},{7,6},{8,9},{9,8},{10,11... | collective-permute-start | bytes 786440 | tf_op jit(solution)/shard_map/ppermute | solution.py:565
  66.4 25.9 %collective-permute-start.11 = (bf16[128,2048]{1,0:T(8,128)(2,1)}, bf16[128,2048]{1,0:T(8,128)(2,1)}, u32[]{:S(2)}, u32[]{:S(2)}) collective-permute-start(bf16[128,2048]{1,0:T(8,128)(2,1)} %get-tuple-element.152), channel_id=1, source_target_pairs={{0,2},{2,0},{4,6},{6,4},{8,10},{10,8},{12,14},{14,12},{16,18},{18,... | collective-permute-start | bytes 1572872 | tf_op jit(solution)/shard_map/ppermute | solution.py:568
  68.0 24.4 %collective-permute-start.12 = (bf16[128,2048]{1,0:T(8,128)(2,1)}, bf16[128,2048]{1,0:T(8,128)(2,1)}, u32[]{:S(2)}, u32[]{:S(2)}) collective-permute-start(bf16[128,2048]{1,0:T(8,128)(2,1)} %get-tuple-element.152), channel_id=1, source_target_pairs={{0,8},{2,10},{4,12},{6,14},{8,0},{10,2},{12,4},{14,6},{16,24},{18,... | collective-permute-start | bytes 1572872 | tf_op jit(solution)/shard_map/ppermute | solution.py:568
  69.4 8.7 %collective-permute-start.10 = (bf16[128,2048]{1,0:T(8,128)(2,1)S(1)}, bf16[128,2048]{1,0:T(8,128)(2,1)S(1)}, u32[]{:S(2)}, u32[]{:S(2)}) collective-permute-start(bf16[128,2048]{1,0:T(8,128)(2,1)S(1)} %collective-permute-done.5.refs_5_), channel_id=1, source_target_pairs={{0,1},{1,0},{2,3},{3,2},{4,5},{5,4},{6,7},{7,6},{8,9},{9,8},{10,11... | collective-permute-start | bytes 1572872 | tf_op jit(solution)/shard_map/ppermute | solution.py:565
  71.0 21.3 %all-to-all-start.1 = ((bf16[16,8,2048]{2,1,0:T(8,128)(2,1)}), bf16[16,8,2048]{2,1,0:T(8,128)(2,1)S(1)}, u32[]{:S(2)}, u32[]{:S(2)}) async-start(bf16[16,8,2048]{2,1,0:T(8,128)(2,1)} %bitcast.8), calls=%async_computation.1 | async-start | bytes 1048576 | tf_op jit(solution)/shard_map/all_to_all | solution.py:571
  74.7 15.4 %collective-permute-start.13 = (f32[73,128]{1,0:T(8,128)S(1)}, f32[73,128]{1,0:T(8,128)S(1)}, u32[]{:S(2)}, u32[]{:S(2)}) collective-permute-start(f32[73,128]{1,0:T(8,128)S(1)} %bitcast.55), channel_id=1, source_target_pairs={{0,2},{2,0},{4,6},{6,4},{8,10},{10,8},{12,14},{14,12},{16,18},{18,... | collective-permute-start | bytes 112136 | tf_op jit(solution)/shard_map/ppermute | solution.py:568
  76.6 15.3 %collective-permute-start.14 = (f32[73,128]{1,0:T(8,128)S(1)}, f32[73,128]{1,0:T(8,128)S(1)}, u32[]{:S(2)}, u32[]{:S(2)}) collective-permute-start(f32[73,128]{1,0:T(8,128)S(1)} %bitcast.56), channel_id=1, source_target_pairs={{0,8},{2,10},{4,12},{6,14},{8,0},{10,2},{12,4},{14,6},{16,24},{18,... | collective-permute-start | bytes 112136 | tf_op jit(solution)/shard_map/ppermute | solution.py:568
  78.9 13.5 %collective-permute-start.15 = (f32[73,128]{1,0:T(8,128)S(1)}, f32[73,128]{1,0:T(8,128)S(1)}, u32[]{:S(2)}, u32[]{:S(2)}) collective-permute-start(f32[73,128]{1,0:T(8,128)S(1)} %bitcast.57), channel_id=1, source_target_pairs={{0,10},{2,8},{4,14},{6,12},{8,2},{10,0},{12,6},{14,4},{16,26},{18,... | collective-permute-start | bytes 112136 | tf_op jit(solution)/shard_map/ppermute | solution.py:568
  92.4 14.3 %collective-permute-start.16 = (bf16[128,2048]{1,0:T(8,128)(2,1)}, bf16[128,2048]{1,0:T(8,128)(2,1)S(1)}, u32[]{:S(2)}, u32[]{:S(2)}) collective-permute-start(bf16[128,2048]{1,0:T(8,128)(2,1)} %get-tuple-element.152), channel_id=1, source_target_pairs={{0,10},{2,8},{4,14},{6,12},{8,2},{10,0},{12,6},{14,4},{16,26},{18,... | collective-permute-start | bytes 1572872 | tf_op jit(solution)/shard_map/ppermute | solution.py:568
  94.8 11.9 %collective-permute-start.17 = (bf16[128,2048]{1,0:T(8,128)(2,1)}, bf16[128,2048]{1,0:T(8,128)(2,1)S(1)}, u32[]{:S(2)}, u32[]{:S(2)}) collective-permute-start(bf16[128,2048]{1,0:T(8,128)(2,1)} %collective-permute-done.11.refs_4_), channel_id=1, source_target_pairs={{0,1},{1,0},{2,3},{3,2},{4,5},{5,4},{6,7},{7,6},{8,9},{9,8},{10,11... | collective-permute-start | bytes 1572872 | tf_op jit(solution)/shard_map/ppermute | solution.py:565
  94.8 11.9 %collective-permute-start.18 = (bf16[128,2048]{1,0:T(8,128)(2,1)}, bf16[128,2048]{1,0:T(8,128)(2,1)S(1)}, u32[]{:S(2)}, u32[]{:S(2)}) collective-permute-start(bf16[128,2048]{1,0:T(8,128)(2,1)} %collective-permute-done.12.refs_5_), channel_id=1, source_target_pairs={{0,1},{1,0},{2,3},{3,2},{4,5},{5,4},{6,7},{7,6},{8,9},{9,8},{10,11... | collective-permute-start | bytes 1572872 | tf_op jit(solution)/shard_map/ppermute | solution.py:565
  95.3 14.0 %collective-permute-start.19 = (bf16[512,512]{1,0:T(8,128)(2,1)}, bf16[512,512]{1,0:T(8,128)(2,1)S(1)}, u32[]{:S(2)}, u32[]{:S(2)}) collective-permute-start(bf16[512,512]{1,0:T(8,128)(2,1)} %copy-done.7), channel_id=1, source_target_pairs={{0,4},{2,6},{4,0},{6,2},{8,12},{10,14},{12,8},{14,10},{16,20},{18,... | collective-permute-start | bytes 1572872 | tf_op jit(solution)/shard_map/ppermute | solution.py:568
  110.1 18.0 %collective-permute-start.22 = (bf16[512,512]{1,0:T(8,128)(2,1)}, bf16[512,512]{1,0:T(8,128)(2,1)S(1)}, u32[]{:S(2)}, u32[]{:S(2)}) collective-permute-start(bf16[512,512]{1,0:T(8,128)(2,1)} %copy-done.6), channel_id=1, source_target_pairs={{0,4},{2,6},{4,0},{6,2},{8,12},{10,14},{12,8},{14,10},{16,20},{18,... | collective-permute-start | bytes 1572872 | tf_op jit(solution)/shard_map/ppermute | solution.py:568
  111.2 16.9 %collective-permute-start.21 = (bf16[256,512]{1,0:T(8,128)(2,1)S(1)}, bf16[256,512]{1,0:T(8,128)(2,1)S(1)}, u32[]{:S(2)}, u32[]{:S(2)}) collective-permute-start(bf16[256,512]{1,0:T(8,128)(2,1)S(1)} %get-tuple-element.170), channel_id=1, source_target_pairs={{0,16},{2,18},{4,20},{6,22},{8,24},{10,26},{12,28},{14,30},{16,0},... | collective-permute-start | bytes 786440 | tf_op jit(solution)/shard_map/ppermute | solution.py:568
  113.1 15.0 %collective-permute-start.23 = (f32[73,128]{1,0:T(8,128)S(1)}, f32[73,128]{1,0:T(8,128)S(1)}, u32[]{:S(2)}, u32[]{:S(2)}) collective-permute-start(f32[73,128]{1,0:T(8,128)S(1)} %add_select_fusion.2), channel_id=1, source_target_pairs={{0,4},{2,6},{4,0},{6,2},{8,12},{10,14},{12,8},{14,10},{16,20},{18,... | collective-permute-start | bytes 112136 | tf_op jit(solution)/shard_map/ppermute | solution.py:568
  130.4 17.2 %collective-permute-start.25 = (bf16[512,512]{1,0:T(8,128)(2,1)}, bf16[512,512]{1,0:T(8,128)(2,1)S(1)}, u32[]{:S(2)}, u32[]{:S(2)}) collective-permute-start(bf16[512,512]{1,0:T(8,128)(2,1)} %get-tuple-element.181), channel_id=1, source_target_pairs={{0,4},{2,6},{4,0},{6,2},{8,12},{10,14},{12,8},{14,10},{16,20},{18,... | collective-permute-start | bytes 1572872 | tf_op jit(solution)/shard_map/ppermute | solution.py:568
  132.2 15.4 %collective-permute-start.24 = (bf16[256,512]{1,0:T(8,128)(2,1)}, bf16[256,512]{1,0:T(8,128)(2,1)S(1)}, u32[]{:S(2)}, u32[]{:S(2)}) collective-permute-start(bf16[256,512]{1,0:T(8,128)(2,1)} %get-tuple-element.179), channel_id=1, source_target_pairs={{0,16},{2,18},{4,20},{6,22},{8,24},{10,26},{12,28},{14,30},{16,0},... | collective-permute-start | bytes 786440 | tf_op jit(solution)/shard_map/ppermute | solution.py:568
  133.3 14.2 %collective-permute-start.26 = (f32[73,128]{1,0:T(8,128)S(1)}, f32[73,128]{1,0:T(8,128)S(1)}, u32[]{:S(2)}, u32[]{:S(2)}) collective-permute-start(f32[73,128]{1,0:T(8,128)S(1)} %add_select_fusion.1), channel_id=1, source_target_pairs={{0,16},{2,18},{4,20},{6,22},{8,24},{10,26},{12,28},{14,30},{16,0},... | collective-permute-start | bytes 112136 | tf_op jit(solution)/shard_map/ppermute | solution.py:568
  149.1 16.8 %collective-permute-start.27 = (bf16[256,512]{1,0:T(8,128)(2,1)}, bf16[256,512]{1,0:T(8,128)(2,1)S(1)}, u32[]{:S(2)}, u32[]{:S(2)}) collective-permute-start(bf16[256,512]{1,0:T(8,128)(2,1)} %get-tuple-element.187), channel_id=1, source_target_pairs={{0,16},{2,18},{4,20},{6,22},{8,24},{10,26},{12,28},{14,30},{16,0},... | collective-permute-start | bytes 786440 | tf_op jit(solution)/shard_map/ppermute | solution.py:568
  150.8 11.8 %collective-permute-start.28 = (bf16[64,1024]{1,0:T(8,128)(2,1)S(1)}, bf16[64,1024]{1,0:T(8,128)(2,1)S(1)}, u32[]{:S(2)}, u32[]{:S(2)}) collective-permute-start(bf16[64,1024]{1,0:T(8,128)(2,1)S(1)} %get-tuple-element.193), channel_id=1, source_target_pairs={{0,2},{2,0},{4,6},{6,4},{8,10},{10,8},{12,14},{14,12},{16,18},{18,... | collective-permute-start | bytes 393224 | tf_op jit(solution)/shard_map/ppermute | solution.py:568
  151.6 11.8 %collective-permute-start.29 = (bf16[64,1024]{1,0:T(8,128)(2,1)S(1)}, bf16[64,1024]{1,0:T(8,128)(2,1)S(1)}, u32[]{:S(2)}, u32[]{:S(2)}) collective-permute-start(bf16[64,1024]{1,0:T(8,128)(2,1)S(1)} %get-tuple-element.194), channel_id=1, source_target_pairs={{0,8},{2,10},{4,12},{6,14},{8,0},{10,2},{12,4},{14,6},{16,24},{18,... | collective-permute-start | bytes 393224 | tf_op jit(solution)/shard_map/ppermute | solution.py:568
  153.9 11.9 %collective-permute-start.30 = (bf16[64,1024]{1,0:T(8,128)(2,1)S(1)}, bf16[64,1024]{1,0:T(8,128)(2,1)S(1)}, u32[]{:S(2)}, u32[]{:S(2)}) collective-permute-start(bf16[64,1024]{1,0:T(8,128)(2,1)S(1)} %get-tuple-element.195), channel_id=1, source_target_pairs={{0,10},{2,8},{4,14},{6,12},{8,2},{10,0},{12,6},{14,4},{16,26},{18,... | collective-permute-start | bytes 393224 | tf_op jit(solution)/shard_map/ppermute | solution.py:568
  154.9 6.5 %collective-permute-start.34 = (f32[73,128]{1,0:T(8,128)S(1)}, f32[73,128]{1,0:T(8,128)S(1)}, u32[]{:S(2)}, u32[]{:S(2)}) collective-permute-start(f32[73,128]{1,0:T(8,128)S(1)} %add_select_fusion), channel_id=1, source_target_pairs={{0,1},{1,0},{2,3},{3,2},{4,5},{5,4},{6,7},{7,6},{8,9},{9,8},{10,11... | collective-permute-start | bytes 112136 | tf_op jit(solution)/shard_map/ppermute | solution.py:565
  166.5 5.7 %collective-permute-start.31 = (bf16[64,512]{1,0:T(8,128)(2,1)S(1)}, bf16[64,512]{1,0:T(8,128)(2,1)S(1)}, u32[]{:S(2)}, u32[]{:S(2)}) collective-permute-start(bf16[64,512]{1,0:T(8,128)(2,1)S(1)} %get-tuple-element.205), channel_id=1, source_target_pairs={{0,2},{2,0},{4,6},{6,4},{8,10},{10,8},{12,14},{14,12},{16,18},{18,... | collective-permute-start | bytes 196616 | tf_op jit(solution)/shard_map/ppermute | solution.py:568
  167.3 4.9 %collective-permute-start.32 = (bf16[64,512]{1,0:T(8,128)(2,1)S(1)}, bf16[64,512]{1,0:T(8,128)(2,1)S(1)}, u32[]{:S(2)}, u32[]{:S(2)}) collective-permute-start(bf16[64,512]{1,0:T(8,128)(2,1)S(1)} %get-tuple-element.206), channel_id=1, source_target_pairs={{0,8},{2,10},{4,12},{6,14},{8,0},{10,2},{12,4},{14,6},{16,24},{18,... | collective-permute-start | bytes 196616 | tf_op jit(solution)/shard_map/ppermute | solution.py:568
  167.3 5.6 %collective-permute-start.33 = (bf16[64,512]{1,0:T(8,128)(2,1)S(1)}, bf16[64,512]{1,0:T(8,128)(2,1)S(1)}, u32[]{:S(2)}, u32[]{:S(2)}) collective-permute-start(bf16[64,512]{1,0:T(8,128)(2,1)S(1)} %get-tuple-element.207), channel_id=1, source_target_pairs={{0,10},{2,8},{4,14},{6,12},{8,2},{10,0},{12,6},{14,4},{16,26},{18,... | collective-permute-start | bytes 196616 | tf_op jit(solution)/shard_map/ppermute | solution.py:568
  (25 other events, 186.1 us)

commit v2 on v1

--- a/solution.py
+++ b/solution.py
@@ -118,17 +118,17 @@
     return shape, lambda src, dst, sc: [(src, dst)]
 
 
-def kernel_call(body, outs, args, smem=(), hbm=None, flops=0, scratch=(), limit=12):
+def kernel_call(body, outs, args, smem=(), hbm=None, flops=0, scratch=(), limit=12, loose=()):
     hbm = hbm or {}
     specs = []
     n_bytes = 0
     for i, a in enumerate(args):
         n_bytes += a.size * a.dtype.itemsize
-        space = pltpu.HBM if i in hbm else pltpu.SMEM if i in smem else pltpu.VMEM
+        space = pl.ANY if i in loose else pltpu.HBM if i in hbm else pltpu.SMEM if i in smem else pltpu.VMEM
         specs.append(pl.BlockSpec(memory_space=space))
     shapes = [jax.ShapeDtypeStruct(s, d) for s, d in outs]
     out_specs = [pl.BlockSpec(memory_space=pltpu.VMEM) for _ in outs]
-    args = [pltpu.with_memory_space_constraint(a, pltpu.HBM) if i in hbm else a for i, a in enumerate(args)]
+    args = [pltpu.with_memory_space_constraint(a, pltpu.HBM) if i in hbm and i not in loose else a for i, a in enumerate(args)]
     n_in, n_out, n_scratch = len(args), len(outs), len(scratch)
     extra = []
     own = [i for i, (shape, _) in hbm.items() if shape is not None]
@@ -176,7 +176,7 @@
     return chunks
 
 
-def gathered(own_args, shared_args, rows):
+def gathered(own_args, shared_args, rows, start=2):
     spec = {}
     for i, at in own_args:
         spec[i] = (None, chunked(1, lambda src, dst, sc, k, at=at: (src, dst[at].at[pl.ds(0, 2 * rows), :])))
@@ -184,7 +184,7 @@
 
         def make(src, dst, sc, k, j=j):
             width = dst[0].shape[1]
-            return src.at[:, pl.ds(k * width, width)], dst[k].at[pl.ds((2 + j) * rows, rows), :]
+            return src.at[:, pl.ds(k * width, width)], dst[k].at[pl.ds((start + j) * rows, rows), :]
 
         spec[i] = (None, chunked(2, make))
     return spec
@@ -307,7 +307,7 @@
             msg_out[:, width:] = cot
 
 
-TILE = 512
+TILE = 1024
 
 
 def mlp_kernel(mid, cot, vecs, up, down, gmid_out, mine_out, other_out, sums_out, acc, acc_y):
@@ -443,18 +443,10 @@
     split_rows(grad, run, mine, send_up, keep_up, every)
 
 
-def attn_weights_kernel(
-    n_bits, bit, n_dp, sc, ids, nrm, ga, m1, m2, m3, o1, o2, o3, qv_bias, w_qkv, w_out,
-    send_out, keep_out, gattns, norms, ctx, gqkv, grad,
-):
-    for x in (ga, nrm, m1, m2, m3, o1, o2, o3):
-        x.wait()
-    rows = gattns.shape[0] // 8
-    group = 2 * rows
+def attn_quarter(n_dp, masks, sc, ids, qv_bias, w_qkv, w_out, gattns, norms, ctx, gqkv):
+    group = norms.shape[0] // len(masks)
+    rows = group // 2
     me = sc[1]
-    mine = (me >> bit) & 1
-    run = (norms.shape[1] >> n_bits) << bit
-    masks = (0, 1 << AG_BITS[0], 1 << AG_BITS[1], (1 << AG_BITS[0]) | (1 << AG_BITS[1]))
     norm4 = norms[...]
     w_qkv, qv_bias = w_qkv.wait(), qv_bias.wait()
     q4 = (nn(norm4, w_qkv[0]) + f(qv_bias[0:1, :])).astype(BF16)
@@ -465,8 +457,8 @@
     table = f(ids[:, 2 * norms.shape[1] :])
     from_dp = iota((rows, 1), 0) // (rows // n_dp)
     first = iota((rows, 1), 0) == from_dp * (rows // n_dp)
-    for g in range(4):
-        chosen = jnp.where((from_dp == (me ^ masks[g])) & first, table, 0.0)
+    for g, bits in enumerate(masks):
+        chosen = jnp.where((from_dp == (me ^ bits)) & first, table, 0.0)
         lens = jnp.sum(chosen, axis=0, keepdims=True)
         ends = [lens[:, 1:2]]
         for i in range(2, 5):
@@ -485,9 +477,29 @@
         ctx[s, :] = out.astype(BF16)
         for c in range(3):
             gqkv[s, c * PAD : (c + 1) * PAD] = total[c].astype(BF16)
-    grad[:, : 3 * PAD] = tn(norm4, gqkv[...])
+
+
+def attn_first_kernel(
+    n_dp, masks, sc, ids, nrm, ga, m1, m2, o1, o2, qv_bias, w_qkv, w_out, grad, gattns, norms, ctx, gqkv
+):
+    for x in (ga, nrm, m1, m2, o1, o2):
+        x.wait()
+    attn_quarter(n_dp, masks, sc, ids, qv_bias, w_qkv, w_out, gattns, norms, ctx, gqkv)
+    grad[:, : 3 * PAD] = tn(norms[...], gqkv[...])
     grad[:, 3 * PAD :] = tn(gattns[...], ctx[...])
-    split_rows(grad, run, mine, send_out, keep_out, slice(None))
+
+
+def attn_weights_kernel(
+    n_bits, bit, n_dp, masks, sc, ids, base, m3, o3, qv_bias, w_qkv, w_out,
+    send_out, keep_out, gattns, norms, ctx, gqkv, grad,
+):
+    m3.wait()
+    o3.wait()
+    run = (norms.shape[1] >> n_bits) << bit
+    attn_quarter(n_dp, masks, sc, ids, qv_bias, w_qkv, w_out, gattns, norms, ctx, gqkv)
+    grad[:, : 3 * PAD] = base[:, : 3 * PAD] + tn(norms[...], gqkv[...])
+    grad[:, 3 * PAD :] = base[:, 3 * PAD :] + tn(gattns[...], ctx[...])
+    split_rows(grad, run, (sc[1] >> bit) & 1, send_out, keep_out, slice(None))
 
 
 def step_kernel(bit, run, sc, keep, recv, send_out, keep_out, cur):
@@ -622,7 +634,7 @@
         limit=24,
     )
     gmid_part, m1, m2 = lax.optimization_barrier((gmid_part, m1, m2))
-    m3 = hop(after(msg_mlp, gmid_part), masks[2])
+    m3 = hop(m2, masks[0])
     o1, o2 = swap(m1), swap(m2)
     gmid_recv = swap(gmid_part)
     gmid, gattn, mid_sums, msg_attn = kernel_call(
@@ -670,7 +682,9 @@
     def combine(msg, *came):
         return functools.reduce(lambda a, b: jnp.where(is_top, jnp.maximum(a, b), a + b), (msg, *came))
 
-    came = [hop(msg, m) for m in masks]
+    near = [1 << b for b in rs_bits[:2]]
+    came = [hop(msg, m) for m in near + [near[0] | near[1]]]
+    later = [b for b in range(n_bits) if b not in rs_bits[:2]]
     restored = exchange(back)
 
     block = width // n_dp
@@ -711,17 +725,37 @@
         (send_down, send_up, a1, a2, restored, *came)
     )
     msg = combine(msg, *came)
-    a3 = hop(after(msg_attn, send_up), masks[2])
+    a3 = hop(a1, masks[1])
     b1, b2 = swap(a1), swap(a2)
     recv_down = hop(send_down, 1 << first)
 
-    out_tokens, grad_tokens = kernel_call(
-        restore_kernel, [((rows, width), BF16)] * 2, [pick, restored], flops=1 << 27
-    )
-    a3, b1, b2, recv_down, out_tokens, grad_tokens = lax.optimization_barrier(
-        (a3, b1, b2, recv_down, out_tokens, grad_tokens)
-    )
-    attn_shared = [a1, a2, a3, b1, b2, swap(a3)]
+    def attn_scratch(n):
+        return [
+            pltpu.VMEM((n * group, width), BF16),
+            pltpu.VMEM((n * group, width), BF16),
+            pltpu.VMEM((n * group, q_cols), BF16),
+            pltpu.VMEM((n * group, 3 * q_cols), BF16),
+        ]
+
+    def quarter_weights(i):
+        return {
+            i: ((2, q_cols), columns(q_cols, 1)),
+            i + 1: ((3, width, q_cols), columns(q_cols, 1)),
+            i + 2: ((q_cols, width), columns(q_cols, 0)),
+        }
+
+    (part_attn,) = kernel_call(
+        functools.partial(attn_first_kernel, n_dp, [0] + masks[:2]),
+        [((width, 4 * q_cols), F32)],
+        [sc, got, normed, gattn, a1, a2, b1, b2, qv_bias, w_qkv, out_weight],
+        smem=(0,),
+        hbm={**gathered([(2, 1), (3, 0)], [4, 6, 5, 7], rows), **quarter_weights(8)},
+        limit=24,
+        loose=(6, 7),
+        flops=2 * 3 * group * width * q_cols * 12,
+        scratch=attn_scratch(3),
+    )
+    a3, recv_down, part_attn = lax.optimization_barrier((a3, recv_down, part_attn))
 
     def hand_out(*pairs):
         n, w = pairs[0][0].shape
@@ -769,31 +803,27 @@
         extra = []
         if t <= n_steps:
             msg = after(msg, *gate)
-            came = hop(msg, 1 << rs_bits[t - 1])
+            came = hop(msg, 1 << later[t - 1])
         if t == 1:
             send_attn, keep_attn = kernel_call(
-                functools.partial(attn_weights_kernel, n_bits, first, n_dp),
+                functools.partial(attn_weights_kernel, n_bits, first, n_dp, masks[2:]),
                 [((width // 2, 4 * q_cols), BF16), ((width // 2, 4 * q_cols), F32)],
-                [sc, got, normed, gattn] + attn_shared + [qv_bias, w_qkv, out_weight],
+                [sc, got, part_attn, a3, swap(a3), qv_bias, w_qkv, out_weight],
                 smem=(0,),
-                hbm={
-                    **gathered([(2, 1), (3, 0)], [4, 7, 5, 8, 6, 9], rows),
-                    10: ((2, q_cols), columns(q_cols, 1)),
-                    11: ((3, width, q_cols), columns(q_cols, 1)),
-                    12: ((q_cols, width), columns(q_cols, 0)),
-                },
-                limit=28,
-                flops=2 * 4 * group * width * q_cols * 12,
-                scratch=[
-                    pltpu.VMEM((4 * group, width), BF16),
-                    pltpu.VMEM((4 * group, width), BF16),
-                    pltpu.VMEM((4 * group, q_cols), BF16),
-                    pltpu.VMEM((4 * group, 3 * q_cols), BF16),
-                    pltpu.VMEM((width, 4 * q_cols), F32),
-                ],
+                hbm={**gathered([], [3, 4], rows, 0), **quarter_weights(5)},
+                limit=20,
+                loose=(4,),
+                flops=2 * group * width * q_cols * 12,
+                scratch=attn_scratch(1) + [pltpu.VMEM((width, 4 * q_cols), F32)],
             )
             sends[2], keeps[2] = send_attn, keep_attn
-            extra = [sends[2]]
+            out_tokens, grad_tokens = kernel_call(
+                restore_kernel,
+                [((rows, width), BF16)] * 2,
+                [pick, after(restored, *gate)],
+                flops=1 << 27,
+            )
+            extra = [out_tokens, grad_tokens, sends[2]]
         if t == n_steps + 1:
             mlp_pieces = hand_out((after(keeps[0], *gate), recvs[0]), (keeps[1], recvs[1]))
             clipped_qk, head_factor, column_factor = clip(msg)
@@ -803,7 +833,7 @@
         if t <= n_steps:
             msg = combine(msg, done[len(active)])
         if t == 1:
-            sends[2] = done[-1]
+            out_tokens, grad_tokens, sends[2] = done[-3:]
         if t == n_steps + 1:
             mlp_pieces[1:], clipped_qk = done[-4:-1], done[-1]
     attn_pieces = hand_out((keeps[2], recvs[2]))

time: 175 us -> 170 us (0.971)
  starting transfers between devices: 43.4 us -> 40.1 us
  waiting for transfers between devices: 49.8 us -> 47.8 us
    ppermute x23, waiting for transfers between devices: 35.9 us -> 32.3 us  [hop(): return lax.ppermute(x, 'dp', [(i, i ^ mask) for i in range(n_dp)])]
    ppermute x23, starting transfers between devices: 29.8 us -> 26.4 us  [hop(): return lax.ppermute(x, 'dp', [(i, i ^ mask) for i in range(n_dp)])]
    unnamed x52 -> x56, local copies, waits for them, and re-layouts: 9.21 us -> 8.45 us
    pallas_call x17 -> x18, Pallas kernels: 60.2 us -> 60.2 us  [kernel_call(): pl.pallas_call(run, out_shape=shapes, in_specs=specs, out_specs=out_specs...]
  transfers between devices with their start and end apart: 37 -> 37, of which waited for: 14 -> 17; matrix products, arithmetic and copies ran while one was open for 5% -> 6% of each run, Pallas kernels for 30% -> 31%
where the time goes in v2:
time: 170 us; the launch traced here: 169 us
  Pallas kernels  65.2 us (38%)
  waiting for transfers between devices  47.8 us (28%)
  starting transfers between devices  40.1 us (24%)
  local copies, waits for them, and re-layouts  11.4 us (7%)
  other arithmetic  2.88 us (2%)
  between operations  1.8 us (1%)
    pallas_call x18, Pallas kernels, kernel_call(): pl.pallas_call(run, out_shape=shapes, in_specs=specs, out_specs=out_specs...  60.2 us
    ppermute x23, waiting for transfers between devices, hop(): return lax.ppermute(x, 'dp', [(i, i ^ mask) for i in range(n_dp)])  32.3 us
    ppermute x23, starting transfers between devices, hop(): return lax.ppermute(x, 'dp', [(i, i ^ mask) for i in range(n_dp)])  26.4 us
    all_to_all x2, starting transfers between devices, exchange(): return lax.all_to_all(x, 'dp', split_axis=0, concat_axis=0, tiled=True)  11.9 us
    all_to_all x2, waiting for transfers between devices, exchange(): return lax.all_to_all(x, 'dp', split_axis=0, concat_axis=0, tiled=True)  10.1 us
    unnamed x56, local copies, waits for them, and re-layouts  8.45 us
    ppermute x12, waiting for transfers between devices, swap(): return lax.ppermute(x, 'tensor', [(0, 1), (1, 0)])  5.47 us
    pallas_call x1, Pallas kernels, clip(): pl.pallas_call(clip_kernel, grid=(4,), out_shape=jax.ShapeDtypeStruct((wi...  4.99 us
  transfers between devices with their start and end apart: 37, of which 17 were waited for; matrix products, arithmetic and copies ran while one was open for 6% of the time, Pallas kernels for 31%

profile of v2, /device:TPU:0, one launch (start us, length us, event | category | flops | bytes accessed | tf_op | source)
XLA Modules:
  0.0 169.2 jit_solution(18375303015823565617)
XLA Ops:
  0.6 2.3 %route_kernel.1 = (bf16[128,2176]{1,0:T(8,128)(2,1)}, bf16[128,128]{1,0:T(8,128)(2,1)S(1)}) custom-call(s32[1,128]{1,0:T(1,128)} %bitcast.66, s32[1,4]{1,0:T(1,128)} %refs_1_.1, bf16[128,1024]{1,0:T(8,128)(2,1)} %refs_2_.2, bf16[128,1024]{1,0:T(8,128)(2,1)} %refs_3_.2), custom_call_target="tpu_custom_call" | custom-call | flops 67108864 | bytes 524816 | tf_op jit(solution)/shard_map/route_kernel/pallas_call | solution.py:157
  2.9 8.4 %all-to-all-start = ((bf16[16,8,2176]{2,1,0:T(8,128)(2,1)}), bf16[16,8,2176]{2,1,0:T(8,128)(2,1)S(1)}, u32[]{:S(2)}, u32[]{:S(2)}) async-start(bf16[16,8,2176]{2,1,0:T(8,128)(2,1)} %bitcast.5), calls=%async_computation | async-start | bytes 1114112 | tf_op jit(solution)/shard_map/all_to_all | solution.py:583
  16.9 10.1 %all-to-all-done = bf16[16,8,2176]{2,1,0:T(8,128)(2,1)S(1)} async-done(((bf16[16,8,2176]{2,1,0:T(8,128)(2,1)}), bf16[16,8,2176]{2,1,0:T(8,128)(2,1)S(1)}, u32[]{:S(2)}, u32[]{:S(2)}) %all-to-all-start) | async-done | bytes 557088 | tf_op jit(solution)/shard_map/all_to_all | solution.py:583
  26.9 2.0 %collective-permute-done.refs_2_.refs_5_ = bf16[128,2176]{1,0:T(8,128)(2,1)S(1)} collective-permute-done((bf16[128,2176]{1,0:T(8,128)(2,1)S(1)}, bf16[128,2176]{1,0:T(8,128)(2,1)S(1)}, u32[]{:S(2)}, u32[]{:S(2)}) %collective-permute-start) | collective-permute-done | bytes 557088 | tf_op jit(solution)/shard_map/ppermute | solution.py:577
  28.9 5.2 %attn_kernel.1 = (bf16[256,1024]{1,0:T(8,128)(2,1)S(1)}, bf16[256,1024]{1,0:T(8,128)(2,1)S(1)}, bf16[256,1536]{1,0:T(8,128)(2,1)S(1)}, f32[256,128]{1,0:T(8,128)...) custom-call(s32[8]{0:T(128)S(1)} %concatenate.18.refs_0_, bf16[128,2176]{1,0:T(8,128)(2,1)S(1)} %bitcast.44, ...), custom_call_target="tpu_custom_call" | custom-call | flops 3221225472 | bytes 5343264 | tf_op jit(solution)/shard_map/attn_kernel/pallas_call | solution.py:157
  34.3 1.8 %collective-permute-done.1.refs_2_ = bf16[256,1024]{1,0:T(8,128)(2,1)S(1)} collective-permute-done((bf16[256,1024]{1,0:T(8,128)(2,1)S(1)}, bf16[256,1024]{1,0:T(8,128)(2,1)S(1)}, u32[]{:S(2)}, u32[]{:S(2)}) %collective-permute-start.1) | collective-permute-done | bytes 524320 | tf_op jit(solution)/shard_map/ppermute | solution.py:577
  38.8 8.0 %mlp_kernel.1 = (bf16[256,1024]{1,0:T(8,128)(2,1)S(1)}, f32[128,1024]{1,0:T(8,128)S(1)}, bf16[128,1024]{1,0:T(8,128)(2,1)S(1)}, f32[1,2048]{1,0:T(1,128)S(1)}) custom-call(bf16[256,1024]{1,0:T(8,128)(2,1)S(1)} %get-tuple-element.135.refs_0_.refs_1_, bf16[256,1024]{1,0:T(8,128)(2,1)S(1)} %get-tuple-element.117.refs_1_.refs_3_.refs_2_, ...), custom_call_target="tpu_custom_call" | custom-call | flops 4294967296 | bytes 9469952 | tf_op jit(solution)/shard_map/mlp_kernel/pallas_call | solution.py:157
  46.8 4.0 %collective-permute-done.2.refs_3_ = bf16[128,2048]{1,0:T(8,128)(2,1)S(1)} collective-permute-done((bf16[128,2048]{1,0:T(8,128)(2,1)S(1)}, bf16[128,2048]{1,0:T(8,128)(2,1)S(1)}, u32[]{:S(2)}, u32[]{:S(2)}) %collective-permute-start.2) | collective-permute-done | bytes 524320 | tf_op jit(solution)/shard_map/ppermute | solution.py:580
  53.5 1.6 gmid_kernel.1
  55.1 7.7 %attn_grad_kernel.1 = (f32[128,1024]{1,0:T(8,128)S(1)}, bf16[128,1024]{1,0:T(8,128)(2,1)S(1)}, f32[3,512]{1,0:T(4,128)S(1)}) custom-call(s32[8]{0:T(128)S(1)} %concatenate.18.refs_0_, bf16[256,1024]{1,0:T(8,128)(2,1)S(1)} %get-tuple-element.123.refs_1_.refs_3_, bf16[512,1024]{1,0:T(8,128)(2,1)} %refs_7_.1, bf16[256,1536]{1,0:T(8,128)(2,1)S(1)} %get-tuple-element.124.refs_3_, ...), custom_call_target="tpu_custom_call" | custom-call | flops 3221225472 | bytes 5636128 | tf_op jit(solution)/shard_map/attn_grad_kernel/pallas_call | solution.py:157
  62.8 2.7 %collective-permute-done.5.refs_5_ = bf16[128,2048]{1,0:T(8,128)(2,1)} collective-permute-done((bf16[128,2048]{1,0:T(8,128)(2,1)S(1)}, bf16[128,2048]{1,0:T(8,128)(2,1)}, u32[]{:S(2)}, u32[]{:S(2)}) %collective-permute-start.5) | collective-permute-done | bytes 524320 | tf_op jit(solution)/shard_map/ppermute | solution.py:580
  68.6 1.6 last_kernel.1
  70.2 3.6 %all-to-all-start.1 = ((bf16[16,8,2048]{2,1,0:T(8,128)(2,1)}), bf16[16,8,2048]{2,1,0:T(8,128)(2,1)S(1)}, u32[]{:S(2)}, u32[]{:S(2)}) async-start(bf16[16,8,2048]{2,1,0:T(8,128)(2,1)} %bitcast.8), calls=%async_computation.1 | async-start | bytes 1048576 | tf_op jit(solution)/shard_map/all_to_all | solution.py:583
  73.9 1.9 %collective-permute-start.13 = (f32[73,128]{1,0:T(8,128)S(1)}, f32[73,128]{1,0:T(8,128)S(1)}, u32[]{:S(2)}, u32[]{:S(2)}) collective-permute-start(f32[73,128]{1,0:T(8,128)S(1)} %bitcast.57), channel_id=1, source_target_pairs={{0,4},{2,6},{4,0},{6,2},{8,12},{10,14},{12,8},{14,10},{16,20},{18,... | collective-permute-start | bytes 112136 | tf_op jit(solution)/shard_map/ppermute | solution.py:580
  75.8 2.4 %collective-permute-start.14 = (f32[73,128]{1,0:T(8,128)S(1)}, f32[73,128]{1,0:T(8,128)S(1)}, u32[]{:S(2)}, u32[]{:S(2)}) collective-permute-start(f32[73,128]{1,0:T(8,128)S(1)} %bitcast.58), channel_id=1, source_target_pairs={{0,16},{2,18},{4,20},{6,22},{8,24},{10,26},{12,28},{14,30},{16,0},... | collective-permute-start | bytes 112136 | tf_op jit(solution)/shard_map/ppermute | solution.py:580
  79.2 9.5 %mlp_weights_kernel.1 = (bf16[512,512]{1,0:T(8,128)(2,1)S(1)}, f32[512,512]{1,0:T(8,128)S(1)}, bf16[512,512]{1,0:T(8,128)(2,1)S(1)}, f32[512,512]{1,0:T(8,128)S(1)}) custom-call(s32[8]{0:T(128)S(1)} %concatenate.18.refs_0_, bf16[256,1024]{1,0:T(8,128)(2,1)} %copy-done.7, bf16[256,1024]{1,0:T(8,128)(2,1)} %copy-done.1, bf16[128,2048]{1,0:T(8,128)(2,1)} %copy-done.17, ...), custom_call_target="tpu_custom_call" | custom-call | flops 4294967296 | bytes 12615712 | tf_op jit(solution)/shard_map/mlp_weights_kernel/pallas_call | solution.py:157
  89.4 2.7 %collective-permute-done.14 = f32[73,128]{1,0:T(8,128)S(1)} collective-permute-done((f32[73,128]{1,0:T(8,128)S(1)}, f32[73,128]{1,0:T(8,128)S(1)}, u32[]{:S(2)}, u32[]{:S(2)}) %collective-permute-start.14) | collective-permute-done | bytes 37408 | tf_op jit(solution)/shard_map/ppermute | solution.py:580
  96.5 9.8 %attn_first_kernel.1.refs_2_ = f32[1024,512]{1,0:T(8,128)S(1)} custom-call(s32[8]{0:T(128)S(1)} %concatenate.18.refs_0_, bf16[128,2176]{1,0:T(8,128)(2,1)S(1)} %bitcast.47, bf16[256,1024]{1,0:T(8,128)(2,1)} %copy-done, bf16[256,1024]{1,0:T(8,128)(2,1)} %copy-done.2, bf16[128,2048]{1,0:T(8,128)(2,1)} %collective-permute-done.11.refs_4_, ...), custom_call_target="tpu_custom_call" | custom-call | flops 2415919104 | bytes 7899168 | tf_op jit(solution)/shard_map/attn_first_kernel/pallas_call | solution.py:157
  106.3 2.0 %collective-permute-done.16.refs_3_ = bf16[128,2048]{1,0:T(8,128)(2,1)S(1)} collective-permute-done((bf16[128,2048]{1,0:T(8,128)(2,1)}, bf16[128,2048]{1,0:T(8,128)(2,1)S(1)}, u32[]{:S(2)}, u32[]{:S(2)}) %collective-permute-start.16) | collective-permute-done | bytes 524320 | tf_op jit(solution)/shard_map/ppermute | solution.py:580
  110.4 1.6 collective-permute-start.20
  112.9 1.7 collective-permute-start.22
  115.7 5.7 %attn_weights_kernel.1 = (bf16[512,512]{1,0:T(8,128)(2,1)}, f32[512,512]{1,0:T(8,128)S(1)}) custom-call(s32[8]{0:T(128)S(1)} %concatenate.18.refs_0_, bf16[128,2176]{1,0:T(8,128)(2,1)S(1)} %bitcast.48, f32[1024,512]{1,0:T(8,128)S(1)} %attn_first_kernel.1.refs_2_, bf16[128,2048]{1,0:T(8,128)(2,1)} %copy-done.11, ...), custom_call_target="tpu_custom_call" | custom-call | flops 805306368 | bytes 7899168 | tf_op jit(solution)/shard_map/attn_weights_kernel/pallas_call | solution.py:157
  121.4 4.0 %collective-permute-done.20.refs_2_ = bf16[256,512]{1,0:T(8,128)(2,1)S(1)} collective-permute-done((bf16[256,512]{1,0:T(8,128)(2,1)S(1)}, bf16[256,512]{1,0:T(8,128)(2,1)S(1)}, u32[]{:S(2)}, u32[]{:S(2)}) %collective-permute-start.20) | collective-permute-done | bytes 262176 | tf_op jit(solution)/shard_map/ppermute | solution.py:580
  129.2 2.3 %collective-permute-start.26 = (f32[73,128]{1,0:T(8,128)S(1)}, f32[73,128]{1,0:T(8,128)S(1)}, u32[]{:S(2)}, u32[]{:S(2)}) collective-permute-start(f32[73,128]{1,0:T(8,128)S(1)} %add_select_fusion.1), channel_id=1, source_target_pairs={{0,8},{2,10},{4,12},{6,14},{8,0},{10,2},{12,4},{14,6},{16,24},{18,... | collective-permute-start | bytes 112136 | tf_op jit(solution)/shard_map/ppermute | solution.py:580
  132.2 3.1 %collective-permute-done.26 = f32[73,128]{1,0:T(8,128)S(1)} collective-permute-done((f32[73,128]{1,0:T(8,128)S(1)}, f32[73,128]{1,0:T(8,128)S(1)}, u32[]{:S(2)}, u32[]{:S(2)}) %collective-permute-start.26) | collective-permute-done | bytes 37408 | tf_op jit(solution)/shard_map/ppermute | solution.py:580
  135.4 7.5 %collective-permute-done.24.refs_4_ = bf16[256,512]{1,0:T(8,128)(2,1)S(1)} collective-permute-done((bf16[256,512]{1,0:T(8,128)(2,1)}, bf16[256,512]{1,0:T(8,128)(2,1)S(1)}, u32[]{:S(2)}, u32[]{:S(2)}) %collective-permute-start.24) | collective-permute-done | bytes 262176 | tf_op jit(solution)/shard_map/ppermute | solution.py:580
  146.6 2.4 %collective-permute-start.29 = (bf16[64,1024]{1,0:T(8,128)(2,1)S(1)}, bf16[64,1024]{1,0:T(8,128)(2,1)S(1)}, u32[]{:S(2)}, u32[]{:S(2)}) collective-permute-start(bf16[64,1024]{1,0:T(8,128)(2,1)S(1)} %get-tuple-element.190), channel_id=1, source_target_pairs={{0,8},{2,10},{4,12},{6,14},{8,0},{10,2},{12,4},{14,6},{16,24},{18,... | collective-permute-start | bytes 393224 | tf_op jit(solution)/shard_map/ppermute | solution.py:580
  150.7 5.0 %clip_kernel.1 = bf16[1024,2,512]{2,1,0:T(2,128)(2,1)} custom-call(bf16[3,1024,512]{2,1,0:T(8,128)(2,1)} %bitcast.56, f32[1,512]{1,0:T(1,128)} %reshape_reshape.3.factor), custom_call_target="tpu_custom_call" | custom-call | tf_op jit(solution)/shard_map/clip_kernel/pallas_call | solution.py:777
  157.0 1.9 %collective-permute-done.29.refs_3_ = bf16[64,1024]{1,0:T(8,128)(2,1)S(1)} collective-permute-done((bf16[64,1024]{1,0:T(8,128)(2,1)S(1)}, bf16[64,1024]{1,0:T(8,128)(2,1)S(1)}, u32[]{:S(2)}, u32[]{:S(2)}) %collective-permute-start.29) | collective-permute-done | bytes 131104 | tf_op jit(solution)/shard_map/ppermute | solution.py:580
  158.9 1.6 collective-permute-done.30.refs_4_
  162.7 2.1 %collective-permute-start.33 = (bf16[64,512]{1,0:T(8,128)(2,1)S(1)}, bf16[64,512]{1,0:T(8,128)(2,1)S(1)}, u32[]{:S(2)}, u32[]{:S(2)}) collective-permute-start(bf16[64,512]{1,0:T(8,128)(2,1)S(1)} %get-tuple-element.203), channel_id=1, source_target_pairs={{0,10},{2,8},{4,14},{6,12},{8,2},{10,0},{12,6},{14,4},{16,26},{18,... | collective-permute-start | bytes 196616 | tf_op jit(solution)/shard_map/ppermute | solution.py:580
  165.4 1.6 join_mlp_kernel.1
  (142 shorter events, 39.8 us)
Async XLA Ops:
  2.9 24.0 %all-to-all-start = ((bf16[16,8,2176]{2,1,0:T(8,128)(2,1)}), bf16[16,8,2176]{2,1,0:T(8,128)(2,1)S(1)}, u32[]{:S(2)}, u32[]{:S(2)}) async-start(bf16[16,8,2176]{2,1,0:T(8,128)(2,1)} %bitcast.5), calls=%async_computation | async-start | bytes 1114112 | tf_op jit(solution)/shard_map/all_to_all | solution.py:583
  36.8 14.0 %collective-permute-start.2 = (bf16[128,2048]{1,0:T(8,128)(2,1)S(1)}, bf16[128,2048]{1,0:T(8,128)(2,1)S(1)}, u32[]{:S(2)}, u32[]{:S(2)}) collective-permute-start(bf16[128,2048]{1,0:T(8,128)(2,1)S(1)} %get-tuple-element.119), channel_id=1, source_target_pairs={{0,2},{2,0},{4,6},{6,4},{8,10},{10,8},{12,14},{14,12},{16,18},{18,... | collective-permute-start | bytes 1572872 | tf_op jit(solution)/shard_map/ppermute | solution.py:580
  37.4 13.7 %collective-permute-start.3 = (bf16[128,2048]{1,0:T(8,128)(2,1)S(1)}, bf16[128,2048]{1,0:T(8,128)(2,1)S(1)}, u32[]{:S(2)}, u32[]{:S(2)}) collective-permute-start(bf16[128,2048]{1,0:T(8,128)(2,1)S(1)} %get-tuple-element.119), channel_id=1, source_target_pairs={{0,8},{2,10},{4,12},{6,14},{8,0},{10,2},{12,4},{14,6},{16,24},{18,... | collective-permute-start | bytes 1572872 | tf_op jit(solution)/shard_map/ppermute | solution.py:580
  51.1 14.4 %collective-permute-start.5 = (bf16[128,2048]{1,0:T(8,128)(2,1)S(1)}, bf16[128,2048]{1,0:T(8,128)(2,1)}, u32[]{:S(2)}, u32[]{:S(2)}) collective-permute-start(bf16[128,2048]{1,0:T(8,128)(2,1)S(1)} %collective-permute-done.3.refs_4_), channel_id=1, source_target_pairs={{0,2},{2,0},{4,6},{6,4},{8,10},{10,8},{12,14},{14,12},{16,18},{18,... | collective-permute-start | bytes 1572872 | tf_op jit(solution)/shard_map/ppermute | solution.py:580
  52.6 13.0 %collective-permute-start.6 = (bf16[128,2048]{1,0:T(8,128)(2,1)S(1)}, bf16[128,2048]{1,0:T(8,128)(2,1)S(1)}, u32[]{:S(2)}, u32[]{:S(2)}) collective-permute-start(bf16[128,2048]{1,0:T(8,128)(2,1)S(1)} %collective-permute-done.2.refs_3_), channel_id=1, source_target_pairs={{0,1},{1,0},{2,3},{3,2},{4,5},{5,4},{6,7},{7,6},{8,9},{9,8},{10,11... | collective-permute-start | bytes 1572872 | tf_op jit(solution)/shard_map/ppermute | solution.py:577
  52.8 12.8 %collective-permute-start.7 = (bf16[128,2048]{1,0:T(8,128)(2,1)S(1)}, bf16[128,2048]{1,0:T(8,128)(2,1)S(1)}, u32[]{:S(2)}, u32[]{:S(2)}) collective-permute-start(bf16[128,2048]{1,0:T(8,128)(2,1)S(1)} %collective-permute-done.3.refs_4_), channel_id=1, source_target_pairs={{0,1},{1,0},{2,3},{3,2},{4,5},{5,4},{6,7},{7,6},{8,9},{9,8},{10,11... | collective-permute-start | bytes 1572872 | tf_op jit(solution)/shard_map/ppermute | solution.py:577
  53.2 15.4 %collective-permute-start.9 = (bf16[128,1024]{1,0:T(8,128)(2,1)S(1)}, bf16[128,1024]{1,0:T(8,128)(2,1)S(1)}, u32[]{:S(2)}, u32[]{:S(2)}) collective-permute-start(bf16[128,1024]{1,0:T(8,128)(2,1)S(1)} %get-tuple-element.133), channel_id=1, source_target_pairs={{0,1},{1,0},{2,3},{3,2},{4,5},{5,4},{6,7},{7,6},{8,9},{9,8},{10,11... | collective-permute-start | bytes 786440 | tf_op jit(solution)/shard_map/ppermute | solution.py:577
  65.6 3.1 %collective-permute-start.8 = (bf16[128,1024]{1,0:T(8,128)(2,1)S(1)}, bf16[128,1024]{1,0:T(8,128)(2,1)S(1)}, u32[]{:S(2)}, u32[]{:S(2)}) collective-permute-start(bf16[128,1024]{1,0:T(8,128)(2,1)S(1)} %get-tuple-element.130), channel_id=1, source_target_pairs={{0,1},{1,0},{2,3},{3,2},{4,5},{5,4},{6,7},{7,6},{8,9},{9,8},{10,11... | collective-permute-start | bytes 786440 | tf_op jit(solution)/shard_map/ppermute | solution.py:577
  65.6 27.9 %collective-permute-start.11 = (bf16[128,2048]{1,0:T(8,128)(2,1)}, bf16[128,2048]{1,0:T(8,128)(2,1)}, u32[]{:S(2)}, u32[]{:S(2)}) collective-permute-start(bf16[128,2048]{1,0:T(8,128)(2,1)} %get-tuple-element.143), channel_id=1, source_target_pairs={{0,2},{2,0},{4,6},{6,4},{8,10},{10,8},{12,14},{14,12},{16,18},{18,... | collective-permute-start | bytes 1572872 | tf_op jit(solution)/shard_map/ppermute | solution.py:580
  67.2 26.4 %collective-permute-start.12 = (bf16[128,2048]{1,0:T(8,128)(2,1)}, bf16[128,2048]{1,0:T(8,128)(2,1)}, u32[]{:S(2)}, u32[]{:S(2)}) collective-permute-start(bf16[128,2048]{1,0:T(8,128)(2,1)} %get-tuple-element.143), channel_id=1, source_target_pairs={{0,8},{2,10},{4,12},{6,14},{8,0},{10,2},{12,4},{14,6},{16,24},{18,... | collective-permute-start | bytes 1572872 | tf_op jit(solution)/shard_map/ppermute | solution.py:580
  68.6 9.6 %collective-permute-start.10 = (bf16[128,2048]{1,0:T(8,128)(2,1)}, bf16[128,2048]{1,0:T(8,128)(2,1)S(1)}, u32[]{:S(2)}, u32[]{:S(2)}) collective-permute-start(bf16[128,2048]{1,0:T(8,128)(2,1)} %collective-permute-done.5.refs_5_), channel_id=1, source_target_pairs={{0,1},{1,0},{2,3},{3,2},{4,5},{5,4},{6,7},{7,6},{8,9},{9,8},{10,11... | collective-permute-start | bytes 1572872 | tf_op jit(solution)/shard_map/ppermute | solution.py:577
  70.2 23.3 %all-to-all-start.1 = ((bf16[16,8,2048]{2,1,0:T(8,128)(2,1)}), bf16[16,8,2048]{2,1,0:T(8,128)(2,1)S(1)}, u32[]{:S(2)}, u32[]{:S(2)}) async-start(bf16[16,8,2048]{2,1,0:T(8,128)(2,1)} %bitcast.8), calls=%async_computation.1 | async-start | bytes 1048576 | tf_op jit(solution)/shard_map/all_to_all | solution.py:583
  73.9 15.5 %collective-permute-start.13 = (f32[73,128]{1,0:T(8,128)S(1)}, f32[73,128]{1,0:T(8,128)S(1)}, u32[]{:S(2)}, u32[]{:S(2)}) collective-permute-start(f32[73,128]{1,0:T(8,128)S(1)} %bitcast.57), channel_id=1, source_target_pairs={{0,4},{2,6},{4,0},{6,2},{8,12},{10,14},{12,8},{14,10},{16,20},{18,... | collective-permute-start | bytes 112136 | tf_op jit(solution)/shard_map/ppermute | solution.py:580
  75.8 16.4 %collective-permute-start.14 = (f32[73,128]{1,0:T(8,128)S(1)}, f32[73,128]{1,0:T(8,128)S(1)}, u32[]{:S(2)}, u32[]{:S(2)}) collective-permute-start(f32[73,128]{1,0:T(8,128)S(1)} %bitcast.58), channel_id=1, source_target_pairs={{0,16},{2,18},{4,20},{6,22},{8,24},{10,26},{12,28},{14,30},{16,0},... | collective-permute-start | bytes 112136 | tf_op jit(solution)/shard_map/ppermute | solution.py:580
  79.0 14.5 %collective-permute-start.15 = (f32[73,128]{1,0:T(8,128)S(1)}, f32[73,128]{1,0:T(8,128)S(1)}, u32[]{:S(2)}, u32[]{:S(2)}) collective-permute-start(f32[73,128]{1,0:T(8,128)S(1)} %bitcast.59), channel_id=1, source_target_pairs={{0,20},{2,22},{4,16},{6,18},{8,28},{10,30},{12,24},{14,26},{16,4},... | collective-permute-start | bytes 112136 | tf_op jit(solution)/shard_map/ppermute | solution.py:580
  94.1 14.1 %collective-permute-start.16 = (bf16[128,2048]{1,0:T(8,128)(2,1)}, bf16[128,2048]{1,0:T(8,128)(2,1)S(1)}, u32[]{:S(2)}, u32[]{:S(2)}) collective-permute-start(bf16[128,2048]{1,0:T(8,128)(2,1)} %collective-permute-done.11.refs_4_), channel_id=1, source_target_pairs={{0,8},{2,10},{4,12},{6,14},{8,0},{10,2},{12,4},{14,6},{16,24},{18,... | collective-permute-start | bytes 1572872 | tf_op jit(solution)/shard_map/ppermute | solution.py:580
  94.1 14.1 %collective-permute-start.17 = (bf16[512,512]{1,0:T(8,128)(2,1)}, bf16[512,512]{1,0:T(8,128)(2,1)S(1)}, u32[]{:S(2)}, u32[]{:S(2)}) collective-permute-start(bf16[512,512]{1,0:T(8,128)(2,1)} %copy-done.10), channel_id=1, source_target_pairs={{0,4},{2,6},{4,0},{6,2},{8,12},{10,14},{12,8},{14,10},{16,20},{18,... | collective-permute-start | bytes 1572872 | tf_op jit(solution)/shard_map/ppermute | solution.py:580
  108.3 7.4 %collective-permute-start.23 = (bf16[128,2048]{1,0:T(8,128)(2,1)S(1)}, bf16[128,2048]{1,0:T(8,128)(2,1)S(1)}, u32[]{:S(2)}, u32[]{:S(2)}) collective-permute-start(bf16[128,2048]{1,0:T(8,128)(2,1)S(1)} %collective-permute-done.16.refs_3_), channel_id=1, source_target_pairs={{0,1},{1,0},{2,3},{3,2},{4,5},{5,4},{6,7},{7,6},{8,9},{9,8},{10,11... | collective-permute-start | bytes 1572872 | tf_op jit(solution)/shard_map/ppermute | solution.py:577
  109.8 15.6 %collective-permute-start.21 = (bf16[512,512]{1,0:T(8,128)(2,1)S(1)}, bf16[512,512]{1,0:T(8,128)(2,1)S(1)}, u32[]{:S(2)}, u32[]{:S(2)}) collective-permute-start(bf16[512,512]{1,0:T(8,128)(2,1)S(1)} %copy-done.9), channel_id=1, source_target_pairs={{0,4},{2,6},{4,0},{6,2},{8,12},{10,14},{12,8},{14,10},{16,20},{18,... | collective-permute-start | bytes 1572872 | tf_op jit(solution)/shard_map/ppermute | solution.py:580
  110.4 15.0 %collective-permute-start.20 = (bf16[256,512]{1,0:T(8,128)(2,1)S(1)}, bf16[256,512]{1,0:T(8,128)(2,1)S(1)}, u32[]{:S(2)}, u32[]{:S(2)}) collective-permute-start(bf16[256,512]{1,0:T(8,128)(2,1)S(1)} %get-tuple-element.154), channel_id=1, source_target_pairs={{0,16},{2,18},{4,20},{6,22},{8,24},{10,26},{12,28},{14,30},{16,0},... | collective-permute-start | bytes 786440 | tf_op jit(solution)/shard_map/ppermute | solution.py:580
  112.9 8.5 %collective-permute-start.22 = (f32[73,128]{1,0:T(8,128)S(1)}, f32[73,128]{1,0:T(8,128)S(1)}, u32[]{:S(2)}, u32[]{:S(2)}) collective-permute-start(f32[73,128]{1,0:T(8,128)S(1)} %add_select_fusion.2), channel_id=1, source_target_pairs={{0,2},{2,0},{4,6},{6,4},{8,10},{10,8},{12,14},{14,12},{16,18},{18,... | collective-permute-start | bytes 112136 | tf_op jit(solution)/shard_map/ppermute | solution.py:580
  127.7 15.3 %collective-permute-start.25 = (bf16[512,512]{1,0:T(8,128)(2,1)}, bf16[512,512]{1,0:T(8,128)(2,1)S(1)}, u32[]{:S(2)}, u32[]{:S(2)}) collective-permute-start(bf16[512,512]{1,0:T(8,128)(2,1)} %get-tuple-element.177), channel_id=1, source_target_pairs={{0,4},{2,6},{4,0},{6,2},{8,12},{10,14},{12,8},{14,10},{16,20},{18,... | collective-permute-start | bytes 1572872 | tf_op jit(solution)/shard_map/ppermute | solution.py:580
  129.2 13.8 %collective-permute-start.24 = (bf16[256,512]{1,0:T(8,128)(2,1)}, bf16[256,512]{1,0:T(8,128)(2,1)S(1)}, u32[]{:S(2)}, u32[]{:S(2)}) collective-permute-start(bf16[256,512]{1,0:T(8,128)(2,1)} %get-tuple-element.175), channel_id=1, source_target_pairs={{0,16},{2,18},{4,20},{6,22},{8,24},{10,26},{12,28},{14,30},{16,0},... | collective-permute-start | bytes 786440 | tf_op jit(solution)/shard_map/ppermute | solution.py:580
  129.2 6.1 %collective-permute-start.26 = (f32[73,128]{1,0:T(8,128)S(1)}, f32[73,128]{1,0:T(8,128)S(1)}, u32[]{:S(2)}, u32[]{:S(2)}) collective-permute-start(f32[73,128]{1,0:T(8,128)S(1)} %add_select_fusion.1), channel_id=1, source_target_pairs={{0,8},{2,10},{4,12},{6,14},{8,0},{10,2},{12,4},{14,6},{16,24},{18,... | collective-permute-start | bytes 112136 | tf_op jit(solution)/shard_map/ppermute | solution.py:580
  143.7 16.8 %collective-permute-start.27 = (bf16[256,512]{1,0:T(8,128)(2,1)S(1)}, bf16[256,512]{1,0:T(8,128)(2,1)S(1)}, u32[]{:S(2)}, u32[]{:S(2)}) collective-permute-start(bf16[256,512]{1,0:T(8,128)(2,1)S(1)} %get-tuple-element.183), channel_id=1, source_target_pairs={{0,16},{2,18},{4,20},{6,22},{8,24},{10,26},{12,28},{14,30},{16,0},... | collective-permute-start | bytes 786440 | tf_op jit(solution)/shard_map/ppermute | solution.py:580
  145.5 11.4 %collective-permute-start.28 = (bf16[64,1024]{1,0:T(8,128)(2,1)S(1)}, bf16[64,1024]{1,0:T(8,128)(2,1)S(1)}, u32[]{:S(2)}, u32[]{:S(2)}) collective-permute-start(bf16[64,1024]{1,0:T(8,128)(2,1)S(1)} %get-tuple-element.189), channel_id=1, source_target_pairs={{0,2},{2,0},{4,6},{6,4},{8,10},{10,8},{12,14},{14,12},{16,18},{18,... | collective-permute-start | bytes 393224 | tf_op jit(solution)/shard_map/ppermute | solution.py:580
  146.6 12.3 %collective-permute-start.29 = (bf16[64,1024]{1,0:T(8,128)(2,1)S(1)}, bf16[64,1024]{1,0:T(8,128)(2,1)S(1)}, u32[]{:S(2)}, u32[]{:S(2)}) collective-permute-start(bf16[64,1024]{1,0:T(8,128)(2,1)S(1)} %get-tuple-element.190), channel_id=1, source_target_pairs={{0,8},{2,10},{4,12},{6,14},{8,0},{10,2},{12,4},{14,6},{16,24},{18,... | collective-permute-start | bytes 393224 | tf_op jit(solution)/shard_map/ppermute | solution.py:580
  149.0 11.5 %collective-permute-start.30 = (bf16[64,1024]{1,0:T(8,128)(2,1)S(1)}, bf16[64,1024]{1,0:T(8,128)(2,1)S(1)}, u32[]{:S(2)}, u32[]{:S(2)}) collective-permute-start(bf16[64,1024]{1,0:T(8,128)(2,1)S(1)} %get-tuple-element.191), channel_id=1, source_target_pairs={{0,10},{2,8},{4,14},{6,12},{8,2},{10,0},{12,6},{14,4},{16,26},{18,... | collective-permute-start | bytes 393224 | tf_op jit(solution)/shard_map/ppermute | solution.py:580
  149.2 6.5 %collective-permute-start.34 = (f32[73,128]{1,0:T(8,128)S(1)}, f32[73,128]{1,0:T(8,128)S(1)}, u32[]{:S(2)}, u32[]{:S(2)}) collective-permute-start(f32[73,128]{1,0:T(8,128)S(1)} %add_select_fusion), channel_id=1, source_target_pairs={{0,1},{1,0},{2,3},{3,2},{4,5},{5,4},{6,7},{7,6},{8,9},{9,8},{10,11... | collective-permute-start | bytes 112136 | tf_op jit(solution)/shard_map/ppermute | solution.py:577
  161.2 5.7 %collective-permute-start.31 = (bf16[64,512]{1,0:T(8,128)(2,1)S(1)}, bf16[64,512]{1,0:T(8,128)(2,1)S(1)}, u32[]{:S(2)}, u32[]{:S(2)}) collective-permute-start(bf16[64,512]{1,0:T(8,128)(2,1)S(1)} %get-tuple-element.201), channel_id=1, source_target_pairs={{0,2},{2,0},{4,6},{6,4},{8,10},{10,8},{12,14},{14,12},{16,18},{18,... | collective-permute-start | bytes 196616 | tf_op jit(solution)/shard_map/ppermute | solution.py:580
  162.7 4.3 %collective-permute-start.32 = (bf16[64,512]{1,0:T(8,128)(2,1)S(1)}, bf16[64,512]{1,0:T(8,128)(2,1)S(1)}, u32[]{:S(2)}, u32[]{:S(2)}) collective-permute-start(bf16[64,512]{1,0:T(8,128)(2,1)S(1)} %get-tuple-element.202), channel_id=1, source_target_pairs={{0,8},{2,10},{4,12},{6,14},{8,0},{10,2},{12,4},{14,6},{16,24},{18,... | collective-permute-start | bytes 196616 | tf_op jit(solution)/shard_map/ppermute | solution.py:580
  162.7 5.2 %collective-permute-start.33 = (bf16[64,512]{1,0:T(8,128)(2,1)S(1)}, bf16[64,512]{1,0:T(8,128)(2,1)S(1)}, u32[]{:S(2)}, u32[]{:S(2)}) collective-permute-start(bf16[64,512]{1,0:T(8,128)(2,1)S(1)} %get-tuple-element.203), channel_id=1, source_target_pairs={{0,10},{2,8},{4,14},{6,12},{8,2},{10,0},{12,6},{14,4},{16,26},{18,... | collective-permute-start | bytes 196616 | tf_op jit(solution)/shard_map/ppermute | solution.py:580
  (27 other events, 236.6 us)

commit v3 on v2

--- a/solution.py
+++ b/solution.py
@@ -518,12 +518,10 @@
         out[...] = cur[pl.ds(pl.multiple_of((q ^ j) * n, n), n), :].astype(out.dtype)
 
 
-def join_mlp_kernel(sc, own, p1, p2, p3, down_out, up_out):
-    w = own.shape[1] // 2
+def join_mlp_kernel(sc, own, p1, p2, p3, out):
+    w = own.shape[1]
     for j, p in enumerate((own, p1, p2, p3)):
-        at = pl.ds(pl.multiple_of((sc[2] ^ j) * w, w), w)
-        down_out[:, at] = f(p[:, :w])
-        up_out[:, at] = f(p[:, w:])
+        out[:, pl.ds(pl.multiple_of((sc[2] ^ j) * w, w), w)] = f(p[...])
 
 
 def join_attn_kernel(sc, own, p1, p2, p3, qkv_out, out_out):
@@ -786,6 +784,9 @@
             name="clip_kernel",
         )(w_qkv, column_factor.reshape(1, cols))
         return clipped_qk, head_factor, column_factor
+
+    def join_mlp(pieces):
+        return kernel_call(join_mlp_kernel, [((block, hidden), F32)], [sc] + pieces, smem=(0,))[0]
 
     n_steps = len(rs_bits)
     recvs = {0: recv_down}
@@ -824,10 +825,12 @@
                 flops=1 << 27,
             )
             extra = [out_tokens, grad_tokens, sends[2]]
+        if t >= n_steps:
+            mlp_pieces = hand_out((after(keeps[t - n_steps], *gate), recvs[t - n_steps]))
+            extra = mlp_pieces[1:]
         if t == n_steps + 1:
-            mlp_pieces = hand_out((after(keeps[0], *gate), recvs[0]), (keeps[1], recvs[1]))
             clipped_qk, head_factor, column_factor = clip(msg)
-            extra = mlp_pieces[1:] + [clipped_qk]
+            extra = extra + [clipped_qk, grad_down]
         done = lax.optimization_barrier([recvs[i] for i in active] + [came] + extra)
         recvs.update(zip(active, done))
         if t <= n_steps:
@@ -835,12 +838,13 @@
         if t == 1:
             out_tokens, grad_tokens, sends[2] = done[-3:]
         if t == n_steps + 1:
-            mlp_pieces[1:], clipped_qk = done[-4:-1], done[-1]
+            mlp_pieces[1:], clipped_qk, grad_down = done[-5:-2], done[-2], done[-1]
+            grad_up = join_mlp(mlp_pieces)
+        if t == n_steps:
+            mlp_pieces[1:] = done[-3:]
+            grad_down = join_mlp(mlp_pieces)
     attn_pieces = hand_out((keeps[2], recvs[2]))
-    grad_down, grad_up = kernel_call(
-        join_mlp_kernel, [((block, hidden), F32), ((block, hidden), F32)], [sc] + mlp_pieces, smem=(0,)
-    )
-    grad_down, grad_up, *attn_pieces[1:] = lax.optimization_barrier((grad_down, grad_up, *attn_pieces[1:]))
+    grad_up, *attn_pieces[1:] = lax.optimization_barrier((grad_up, *attn_pieces[1:]))
     grad_down = grad_down.T
     grad_qkv, grad_out = kernel_call(
         join_attn_kernel, [((3, block, cols), F32), ((block, cols), F32)], [sc] + attn_pieces, smem=(0,)

time: 170 us -> 169 us (level)
  starting transfers between devices: 40.1 us -> 45.4 us
  waiting for transfers between devices: 47.8 us -> 43 us
  local copies, waits for them, and re-layouts: 11.4 us -> 8.81 us
    ppermute x23 -> x26, starting transfers between devices: 26.4 us -> 31.8 us  [hop(): return lax.ppermute(x, 'dp', [(i, i ^ mask) for i in range(n_dp)])]
    ppermute x23 -> x26, waiting for transfers between devices: 32.3 us -> 27.4 us  [hop(): return lax.ppermute(x, 'dp', [(i, i ^ mask) for i in range(n_dp)])]
    unnamed x56 -> x44, local copies, waits for them, and re-layouts: 8.45 us -> 5.82 us
    pallas_call x18 -> x20, Pallas kernels: 60.2 us -> 61.3 us  [kernel_call(): pl.pallas_call(run, out_shape=shapes, in_specs=specs, out_specs=out_specs...]
  transfers between devices with their start and end apart: 37 -> 40, of which waited for: 17 -> 17; matrix products, arithmetic and copies ran while one was open for 6% -> 6% of each run, Pallas kernels for 31% -> 32%
where the time goes in v3:
time: 169 us; the launch traced here: 168 us
  Pallas kernels  66.3 us (39%)
  starting transfers between devices  45.4 us (27%)
  waiting for transfers between devices  43 us (25%)
  local copies, waits for them, and re-layouts  8.81 us (5%)
  other arithmetic  2.86 us (2%)
  between operations  1.81 us (1%)
    pallas_call x20, Pallas kernels, kernel_call(): pl.pallas_call(run, out_shape=shapes, in_specs=specs, out_specs=out_specs...  61.3 us
    ppermute x26, starting transfers between devices, hop(): return lax.ppermute(x, 'dp', [(i, i ^ mask) for i in range(n_dp)])  31.8 us
    ppermute x26, waiting for transfers between devices, hop(): return lax.ppermute(x, 'dp', [(i, i ^ mask) for i in range(n_dp)])  27.4 us
    all_to_all x2, starting transfers between devices, exchange(): return lax.all_to_all(x, 'dp', split_axis=0, concat_axis=0, tiled=True)  11.9 us
    all_to_all x2, waiting for transfers between devices, exchange(): return lax.all_to_all(x, 'dp', split_axis=0, concat_axis=0, tiled=True)  10.1 us
    unnamed x44, local copies, waits for them, and re-layouts  5.82 us
    ppermute x12, waiting for transfers between devices, swap(): return lax.ppermute(x, 'tensor', [(0, 1), (1, 0)])  5.46 us
    pallas_call x1, Pallas kernels, clip(): pl.pallas_call(clip_kernel, grid=(4,), out_shape=jax.ShapeDtypeStruct((wi...  4.99 us
  transfers between devices with their start and end apart: 40, of which 17 were waited for; matrix products, arithmetic and copies ran while one was open for 6% of the time, Pallas kernels for 32%

profile of v3, /device:TPU:0, one launch (start us, length us, event | category | flops | bytes accessed | tf_op | source)
XLA Modules:
  0.0 168.1 jit_solution(584618636414496358)
XLA Ops:
  0.6 2.3 %route_kernel.1 = (bf16[128,2176]{1,0:T(8,128)(2,1)}, bf16[128,128]{1,0:T(8,128)(2,1)S(1)}) custom-call(s32[1,128]{1,0:T(1,128)} %bitcast.67, s32[1,4]{1,0:T(1,128)} %refs_1_.1, bf16[128,1024]{1,0:T(8,128)(2,1)} %refs_2_.2, bf16[128,1024]{1,0:T(8,128)(2,1)} %refs_3_.2), custom_call_target="tpu_custom_call" | custom-call | flops 67108864 | bytes 524816 | tf_op jit(solution)/shard_map/route_kernel/pallas_call | solution.py:157
  2.9 8.4 %all-to-all-start = ((bf16[16,8,2176]{2,1,0:T(8,128)(2,1)}), bf16[16,8,2176]{2,1,0:T(8,128)(2,1)S(1)}, u32[]{:S(2)}, u32[]{:S(2)}) async-start(bf16[16,8,2176]{2,1,0:T(8,128)(2,1)} %bitcast.5), calls=%async_computation | async-start | bytes 1114112 | tf_op jit(solution)/shard_map/all_to_all | solution.py:581
  16.9 10.1 %all-to-all-done = bf16[16,8,2176]{2,1,0:T(8,128)(2,1)S(1)} async-done(((bf16[16,8,2176]{2,1,0:T(8,128)(2,1)}), bf16[16,8,2176]{2,1,0:T(8,128)(2,1)S(1)}, u32[]{:S(2)}, u32[]{:S(2)}) %all-to-all-start) | async-done | bytes 557088 | tf_op jit(solution)/shard_map/all_to_all | solution.py:581
  26.9 2.0 %collective-permute-done.refs_2_.refs_5_ = bf16[128,2176]{1,0:T(8,128)(2,1)S(1)} collective-permute-done((bf16[128,2176]{1,0:T(8,128)(2,1)S(1)}, bf16[128,2176]{1,0:T(8,128)(2,1)S(1)}, u32[]{:S(2)}, u32[]{:S(2)}) %collective-permute-start) | collective-permute-done | bytes 557088 | tf_op jit(solution)/shard_map/ppermute | solution.py:575
  28.9 5.2 %attn_kernel.1 = (bf16[256,1024]{1,0:T(8,128)(2,1)S(1)}, bf16[256,1024]{1,0:T(8,128)(2,1)S(1)}, bf16[256,1536]{1,0:T(8,128)(2,1)S(1)}, f32[256,128]{1,0:T(8,128)...) custom-call(s32[8]{0:T(128)S(1)} %concatenate.18.refs_0_, bf16[128,2176]{1,0:T(8,128)(2,1)S(1)} %bitcast.44, ...), custom_call_target="tpu_custom_call" | custom-call | flops 3221225472 | bytes 5343264 | tf_op jit(solution)/shard_map/attn_kernel/pallas_call | solution.py:157
  34.3 1.8 %collective-permute-done.1.refs_2_ = bf16[256,1024]{1,0:T(8,128)(2,1)S(1)} collective-permute-done((bf16[256,1024]{1,0:T(8,128)(2,1)S(1)}, bf16[256,1024]{1,0:T(8,128)(2,1)S(1)}, u32[]{:S(2)}, u32[]{:S(2)}) %collective-permute-start.1) | collective-permute-done | bytes 524320 | tf_op jit(solution)/shard_map/ppermute | solution.py:575
  38.8 8.0 %mlp_kernel.1 = (bf16[256,1024]{1,0:T(8,128)(2,1)S(1)}, f32[128,1024]{1,0:T(8,128)S(1)}, bf16[128,1024]{1,0:T(8,128)(2,1)S(1)}, f32[1,2048]{1,0:T(1,128)S(1)}) custom-call(bf16[256,1024]{1,0:T(8,128)(2,1)S(1)} %get-tuple-element.141.refs_0_.refs_1_, bf16[256,1024]{1,0:T(8,128)(2,1)S(1)} %get-tuple-element.123.refs_1_.refs_3_.refs_2_, ...), custom_call_target="tpu_custom_call" | custom-call | flops 4294967296 | bytes 9469952 | tf_op jit(solution)/shard_map/mlp_kernel/pallas_call | solution.py:157
  46.8 4.0 %collective-permute-done.2.refs_3_ = bf16[128,2048]{1,0:T(8,128)(2,1)S(1)} collective-permute-done((bf16[128,2048]{1,0:T(8,128)(2,1)S(1)}, bf16[128,2048]{1,0:T(8,128)(2,1)S(1)}, u32[]{:S(2)}, u32[]{:S(2)}) %collective-permute-start.2) | collective-permute-done | bytes 524320 | tf_op jit(solution)/shard_map/ppermute | solution.py:578
  53.5 1.6 gmid_kernel.1
  55.1 7.7 %attn_grad_kernel.1 = (f32[128,1024]{1,0:T(8,128)S(1)}, bf16[128,1024]{1,0:T(8,128)(2,1)S(1)}, f32[3,512]{1,0:T(4,128)S(1)}) custom-call(s32[8]{0:T(128)S(1)} %concatenate.18.refs_0_, bf16[256,1024]{1,0:T(8,128)(2,1)S(1)} %get-tuple-element.129.refs_1_.refs_3_, bf16[512,1024]{1,0:T(8,128)(2,1)} %refs_7_.1, bf16[256,1536]{1,0:T(8,128)(2,1)S(1)} %get-tuple-element.130.refs_3_, ...), custom_call_target="tpu_custom_call" | custom-call | flops 3221225472 | bytes 5636128 | tf_op jit(solution)/shard_map/attn_grad_kernel/pallas_call | solution.py:157
  62.8 2.7 %collective-permute-done.5.refs_5_ = bf16[128,2048]{1,0:T(8,128)(2,1)} collective-permute-done((bf16[128,2048]{1,0:T(8,128)(2,1)S(1)}, bf16[128,2048]{1,0:T(8,128)(2,1)}, u32[]{:S(2)}, u32[]{:S(2)}) %collective-permute-start.5) | collective-permute-done | bytes 524320 | tf_op jit(solution)/shard_map/ppermute | solution.py:578
  68.7 1.6 last_kernel.1
  70.3 3.6 %all-to-all-start.1 = ((bf16[16,8,2048]{2,1,0:T(8,128)(2,1)}), bf16[16,8,2048]{2,1,0:T(8,128)(2,1)S(1)}, u32[]{:S(2)}, u32[]{:S(2)}) async-start(bf16[16,8,2048]{2,1,0:T(8,128)(2,1)} %bitcast.8), calls=%async_computation.1 | async-start | bytes 1048576 | tf_op jit(solution)/shard_map/all_to_all | solution.py:581
  73.9 1.9 %collective-permute-start.13 = (f32[73,128]{1,0:T(8,128)S(1)}, f32[73,128]{1,0:T(8,128)S(1)}, u32[]{:S(2)}, u32[]{:S(2)}) collective-permute-start(f32[73,128]{1,0:T(8,128)S(1)} %bitcast.58), channel_id=1, source_target_pairs={{0,4},{2,6},{4,0},{6,2},{8,12},{10,14},{12,8},{14,10},{16,20},{18,... | collective-permute-start | bytes 112136 | tf_op jit(solution)/shard_map/ppermute | solution.py:578
  75.8 2.4 %collective-permute-start.14 = (f32[73,128]{1,0:T(8,128)S(1)}, f32[73,128]{1,0:T(8,128)S(1)}, u32[]{:S(2)}, u32[]{:S(2)}) collective-permute-start(f32[73,128]{1,0:T(8,128)S(1)} %bitcast.59), channel_id=1, source_target_pairs={{0,16},{2,18},{4,20},{6,22},{8,24},{10,26},{12,28},{14,30},{16,0},... | collective-permute-start | bytes 112136 | tf_op jit(solution)/shard_map/ppermute | solution.py:578
  79.2 9.5 %mlp_weights_kernel.1 = (bf16[512,512]{1,0:T(8,128)(2,1)S(1)}, f32[512,512]{1,0:T(8,128)S(1)}, bf16[512,512]{1,0:T(8,128)(2,1)S(1)}, f32[512,512]{1,0:T(8,128)S(1)}) custom-call(s32[8]{0:T(128)S(1)} %concatenate.18.refs_0_, bf16[256,1024]{1,0:T(8,128)(2,1)} %copy-done.3, bf16[256,1024]{1,0:T(8,128)(2,1)} %copy-done.1, bf16[128,2048]{1,0:T(8,128)(2,1)} %copy-done.11, ...), custom_call_target="tpu_custom_call" | custom-call | flops 4294967296 | bytes 12615712 | tf_op jit(solution)/shard_map/mlp_weights_kernel/pallas_call | solution.py:157
  89.4 2.7 %collective-permute-done.14 = f32[73,128]{1,0:T(8,128)S(1)} collective-permute-done((f32[73,128]{1,0:T(8,128)S(1)}, f32[73,128]{1,0:T(8,128)S(1)}, u32[]{:S(2)}, u32[]{:S(2)}) %collective-permute-start.14) | collective-permute-done | bytes 37408 | tf_op jit(solution)/shard_map/ppermute | solution.py:578
  96.5 9.8 %attn_first_kernel.1.refs_2_ = f32[1024,512]{1,0:T(8,128)S(1)} custom-call(s32[8]{0:T(128)S(1)} %concatenate.18.refs_0_, bf16[128,2176]{1,0:T(8,128)(2,1)S(1)} %bitcast.47, bf16[256,1024]{1,0:T(8,128)(2,1)} %copy-done, bf16[256,1024]{1,0:T(8,128)(2,1)} %copy-done.2, bf16[128,2048]{1,0:T(8,128)(2,1)} %collective-permute-done.11.refs_4_, ...), custom_call_target="tpu_custom_call" | custom-call | flops 2415919104 | bytes 7899168 | tf_op jit(solution)/shard_map/attn_first_kernel/pallas_call | solution.py:157
  106.3 1.9 %collective-permute-done.16.refs_3_ = bf16[128,2048]{1,0:T(8,128)(2,1)S(1)} collective-permute-done((bf16[128,2048]{1,0:T(8,128)(2,1)}, bf16[128,2048]{1,0:T(8,128)(2,1)S(1)}, u32[]{:S(2)}, u32[]{:S(2)}) %collective-permute-start.16) | collective-permute-done | bytes 524320 | tf_op jit(solution)/shard_map/ppermute | solution.py:578
  109.7 1.6 collective-permute-start.20
  111.3 1.6 collective-permute-start.22
  114.0 5.7 %attn_weights_kernel.1 = (bf16[512,512]{1,0:T(8,128)(2,1)}, f32[512,512]{1,0:T(8,128)S(1)}) custom-call(s32[8]{0:T(128)S(1)} %concatenate.18.refs_0_, bf16[128,2176]{1,0:T(8,128)(2,1)S(1)} %bitcast.48, f32[1024,512]{1,0:T(8,128)S(1)} %attn_first_kernel.1.refs_2_, bf16[128,2048]{1,0:T(8,128)(2,1)} %copy-done.7, ...), custom_call_target="tpu_custom_call" | custom-call | flops 805306368 | bytes 7899168 | tf_op jit(solution)/shard_map/attn_weights_kernel/pallas_call | solution.py:157
  119.8 4.9 %collective-permute-done.20.refs_2_ = bf16[256,512]{1,0:T(8,128)(2,1)S(1)} collective-permute-done((bf16[256,512]{1,0:T(8,128)(2,1)S(1)}, bf16[256,512]{1,0:T(8,128)(2,1)S(1)}, u32[]{:S(2)}, u32[]{:S(2)}) %collective-permute-start.20) | collective-permute-done | bytes 262176 | tf_op jit(solution)/shard_map/ppermute | solution.py:578
  125.4 1.5 collective-permute-start.25
  127.0 2.4 %collective-permute-start.26 = (f32[73,128]{1,0:T(8,128)S(1)}, f32[73,128]{1,0:T(8,128)}, u32[]{:S(2)}, u32[]{:S(2)}) collective-permute-start(f32[73,128]{1,0:T(8,128)S(1)} %add_select_fusion.1), channel_id=1, source_target_pairs={{0,8},{2,10},{4,12},{6,14},{8,0},{10,2},{12,4},{14,6},{16,24},{18,... | collective-permute-start | bytes 112136 | tf_op jit(solution)/shard_map/ppermute | solution.py:578
  131.3 2.4 %collective-permute-done.26 = f32[73,128]{1,0:T(8,128)} collective-permute-done((f32[73,128]{1,0:T(8,128)S(1)}, f32[73,128]{1,0:T(8,128)}, u32[]{:S(2)}, u32[]{:S(2)}) %collective-permute-start.26) | collective-permute-done | bytes 37408 | tf_op jit(solution)/shard_map/ppermute | solution.py:578
  133.7 3.5 %collective-permute-start.29 = (bf16[64,512]{1,0:T(8,128)(2,1)S(1)}, bf16[64,512]{1,0:T(8,128)(2,1)S(1)}, u32[]{:S(2)}, u32[]{:S(2)}) collective-permute-start(bf16[64,512]{1,0:T(8,128)(2,1)S(1)} %get-tuple-element.191), channel_id=1, source_target_pairs={{0,10},{2,8},{4,14},{6,12},{8,2},{10,0},{12,6},{14,4},{16,26},{18,... | collective-permute-start | bytes 196616 | tf_op jit(solution)/shard_map/ppermute | solution.py:578
  137.8 3.4 %collective-permute-done.28.refs_3_ = bf16[64,512]{1,0:T(8,128)(2,1)S(1)} collective-permute-done((bf16[64,512]{1,0:T(8,128)(2,1)S(1)}, bf16[64,512]{1,0:T(8,128)(2,1)S(1)}, u32[]{:S(2)}, u32[]{:S(2)}) %collective-permute-start.28) | collective-permute-done | bytes 65568 | tf_op jit(solution)/shard_map/ppermute | solution.py:578
  145.0 2.3 %collective-permute-start.32 = (bf16[64,512]{1,0:T(8,128)(2,1)S(1)}, bf16[64,512]{1,0:T(8,128)(2,1)S(1)}, u32[]{:S(2)}, u32[]{:S(2)}) collective-permute-start(bf16[64,512]{1,0:T(8,128)(2,1)S(1)} %get-tuple-element.200), channel_id=1, source_target_pairs={{0,8},{2,10},{4,12},{6,14},{8,0},{10,2},{12,4},{14,6},{16,24},{18,... | collective-permute-start | bytes 196616 | tf_op jit(solution)/shard_map/ppermute | solution.py:578
  150.0 5.0 %clip_kernel.1 = bf16[1024,2,512]{2,1,0:T(2,128)(2,1)} custom-call(bf16[3,1024,512]{2,1,0:T(8,128)(2,1)} %bitcast.56, f32[1,512]{1,0:T(1,128)} %reshape_reshape.3.factor), custom_call_target="tpu_custom_call" | custom-call | tf_op jit(solution)/shard_map/clip_kernel/pallas_call | solution.py:775
  159.6 2.0 %collective-permute-start.35 = (bf16[64,512]{1,0:T(8,128)(2,1)S(1)}, bf16[64,512]{1,0:T(8,128)(2,1)S(1)}, u32[]{:S(2)}, u32[]{:S(2)}) collective-permute-start(bf16[64,512]{1,0:T(8,128)(2,1)S(1)} %get-tuple-element.214), channel_id=1, source_target_pairs={{0,8},{2,10},{4,12},{6,14},{8,0},{10,2},{12,4},{14,6},{16,24},{18,... | collective-permute-start | bytes 196616 | tf_op jit(solution)/shard_map/ppermute | solution.py:578
  164.0 2.7 %collective-permute-done.36.refs_4_ = bf16[64,512]{1,0:T(8,128)(2,1)S(1)} collective-permute-done((bf16[64,512]{1,0:T(8,128)(2,1)S(1)}, bf16[64,512]{1,0:T(8,128)(2,1)S(1)}, u32[]{:S(2)}, u32[]{:S(2)}) %collective-permute-start.36) | collective-permute-done | bytes 65568 | tf_op jit(solution)/shard_map/ppermute | solution.py:578
  (138 shorter events, 40.4 us)
Async XLA Ops:
  2.9 24.0 %all-to-all-start = ((bf16[16,8,2176]{2,1,0:T(8,128)(2,1)}), bf16[16,8,2176]{2,1,0:T(8,128)(2,1)S(1)}, u32[]{:S(2)}, u32[]{:S(2)}) async-start(bf16[16,8,2176]{2,1,0:T(8,128)(2,1)} %bitcast.5), calls=%async_computation | async-start | bytes 1114112 | tf_op jit(solution)/shard_map/all_to_all | solution.py:581
  36.8 14.0 %collective-permute-start.2 = (bf16[128,2048]{1,0:T(8,128)(2,1)S(1)}, bf16[128,2048]{1,0:T(8,128)(2,1)S(1)}, u32[]{:S(2)}, u32[]{:S(2)}) collective-permute-start(bf16[128,2048]{1,0:T(8,128)(2,1)S(1)} %get-tuple-element.125), channel_id=1, source_target_pairs={{0,2},{2,0},{4,6},{6,4},{8,10},{10,8},{12,14},{14,12},{16,18},{18,... | collective-permute-start | bytes 1572872 | tf_op jit(solution)/shard_map/ppermute | solution.py:578
  37.4 13.7 %collective-permute-start.3 = (bf16[128,2048]{1,0:T(8,128)(2,1)S(1)}, bf16[128,2048]{1,0:T(8,128)(2,1)S(1)}, u32[]{:S(2)}, u32[]{:S(2)}) collective-permute-start(bf16[128,2048]{1,0:T(8,128)(2,1)S(1)} %get-tuple-element.125), channel_id=1, source_target_pairs={{0,8},{2,10},{4,12},{6,14},{8,0},{10,2},{12,4},{14,6},{16,24},{18,... | collective-permute-start | bytes 1572872 | tf_op jit(solution)/shard_map/ppermute | solution.py:578
  51.1 14.4 %collective-permute-start.5 = (bf16[128,2048]{1,0:T(8,128)(2,1)S(1)}, bf16[128,2048]{1,0:T(8,128)(2,1)}, u32[]{:S(2)}, u32[]{:S(2)}) collective-permute-start(bf16[128,2048]{1,0:T(8,128)(2,1)S(1)} %collective-permute-done.3.refs_4_), channel_id=1, source_target_pairs={{0,2},{2,0},{4,6},{6,4},{8,10},{10,8},{12,14},{14,12},{16,18},{18,... | collective-permute-start | bytes 1572872 | tf_op jit(solution)/shard_map/ppermute | solution.py:578
  52.6 13.0 %collective-permute-start.6 = (bf16[128,2048]{1,0:T(8,128)(2,1)S(1)}, bf16[128,2048]{1,0:T(8,128)(2,1)S(1)}, u32[]{:S(2)}, u32[]{:S(2)}) collective-permute-start(bf16[128,2048]{1,0:T(8,128)(2,1)S(1)} %collective-permute-done.2.refs_3_), channel_id=1, source_target_pairs={{0,1},{1,0},{2,3},{3,2},{4,5},{5,4},{6,7},{7,6},{8,9},{9,8},{10,11... | collective-permute-start | bytes 1572872 | tf_op jit(solution)/shard_map/ppermute | solution.py:575
  52.8 12.8 %collective-permute-start.7 = (bf16[128,2048]{1,0:T(8,128)(2,1)S(1)}, bf16[128,2048]{1,0:T(8,128)(2,1)S(1)}, u32[]{:S(2)}, u32[]{:S(2)}) collective-permute-start(bf16[128,2048]{1,0:T(8,128)(2,1)S(1)} %collective-permute-done.3.refs_4_), channel_id=1, source_target_pairs={{0,1},{1,0},{2,3},{3,2},{4,5},{5,4},{6,7},{7,6},{8,9},{9,8},{10,11... | collective-permute-start | bytes 1572872 | tf_op jit(solution)/shard_map/ppermute | solution.py:575
  53.2 15.4 %collective-permute-start.9 = (bf16[128,1024]{1,0:T(8,128)(2,1)S(1)}, bf16[128,1024]{1,0:T(8,128)(2,1)S(1)}, u32[]{:S(2)}, u32[]{:S(2)}) collective-permute-start(bf16[128,1024]{1,0:T(8,128)(2,1)S(1)} %get-tuple-element.139), channel_id=1, source_target_pairs={{0,1},{1,0},{2,3},{3,2},{4,5},{5,4},{6,7},{7,6},{8,9},{9,8},{10,11... | collective-permute-start | bytes 786440 | tf_op jit(solution)/shard_map/ppermute | solution.py:575
  65.6 27.9 %collective-permute-start.11 = (bf16[128,2048]{1,0:T(8,128)(2,1)}, bf16[128,2048]{1,0:T(8,128)(2,1)}, u32[]{:S(2)}, u32[]{:S(2)}) collective-permute-start(bf16[128,2048]{1,0:T(8,128)(2,1)} %get-tuple-element.149), channel_id=1, source_target_pairs={{0,2},{2,0},{4,6},{6,4},{8,10},{10,8},{12,14},{14,12},{16,18},{18,... | collective-permute-start | bytes 1572872 | tf_op jit(solution)/shard_map/ppermute | solution.py:578
  67.2 26.4 %collective-permute-start.12 = (bf16[128,2048]{1,0:T(8,128)(2,1)}, bf16[128,2048]{1,0:T(8,128)(2,1)}, u32[]{:S(2)}, u32[]{:S(2)}) collective-permute-start(bf16[128,2048]{1,0:T(8,128)(2,1)} %get-tuple-element.149), channel_id=1, source_target_pairs={{0,8},{2,10},{4,12},{6,14},{8,0},{10,2},{12,4},{14,6},{16,24},{18,... | collective-permute-start | bytes 1572872 | tf_op jit(solution)/shard_map/ppermute | solution.py:578
  68.6 9.6 %collective-permute-start.10 = (bf16[128,2048]{1,0:T(8,128)(2,1)}, bf16[128,2048]{1,0:T(8,128)(2,1)S(1)}, u32[]{:S(2)}, u32[]{:S(2)}) collective-permute-start(bf16[128,2048]{1,0:T(8,128)(2,1)} %collective-permute-done.5.refs_5_), channel_id=1, source_target_pairs={{0,1},{1,0},{2,3},{3,2},{4,5},{5,4},{6,7},{7,6},{8,9},{9,8},{10,11... | collective-permute-start | bytes 1572872 | tf_op jit(solution)/shard_map/ppermute | solution.py:575
  70.3 23.3 %all-to-all-start.1 = ((bf16[16,8,2048]{2,1,0:T(8,128)(2,1)}), bf16[16,8,2048]{2,1,0:T(8,128)(2,1)S(1)}, u32[]{:S(2)}, u32[]{:S(2)}) async-start(bf16[16,8,2048]{2,1,0:T(8,128)(2,1)} %bitcast.8), calls=%async_computation.1 | async-start | bytes 1048576 | tf_op jit(solution)/shard_map/all_to_all | solution.py:581
  73.9 15.5 %collective-permute-start.13 = (f32[73,128]{1,0:T(8,128)S(1)}, f32[73,128]{1,0:T(8,128)S(1)}, u32[]{:S(2)}, u32[]{:S(2)}) collective-permute-start(f32[73,128]{1,0:T(8,128)S(1)} %bitcast.58), channel_id=1, source_target_pairs={{0,4},{2,6},{4,0},{6,2},{8,12},{10,14},{12,8},{14,10},{16,20},{18,... | collective-permute-start | bytes 112136 | tf_op jit(solution)/shard_map/ppermute | solution.py:578
  75.8 16.4 %collective-permute-start.14 = (f32[73,128]{1,0:T(8,128)S(1)}, f32[73,128]{1,0:T(8,128)S(1)}, u32[]{:S(2)}, u32[]{:S(2)}) collective-permute-start(f32[73,128]{1,0:T(8,128)S(1)} %bitcast.59), channel_id=1, source_target_pairs={{0,16},{2,18},{4,20},{6,22},{8,24},{10,26},{12,28},{14,30},{16,0},... | collective-permute-start | bytes 112136 | tf_op jit(solution)/shard_map/ppermute | solution.py:578
  79.0 14.5 %collective-permute-start.15 = (f32[73,128]{1,0:T(8,128)S(1)}, f32[73,128]{1,0:T(8,128)S(1)}, u32[]{:S(2)}, u32[]{:S(2)}) collective-permute-start(f32[73,128]{1,0:T(8,128)S(1)} %bitcast.60), channel_id=1, source_target_pairs={{0,20},{2,22},{4,16},{6,18},{8,28},{10,30},{12,24},{14,26},{16,4},... | collective-permute-start | bytes 112136 | tf_op jit(solution)/shard_map/ppermute | solution.py:578
  94.1 14.1 %collective-permute-start.16 = (bf16[128,2048]{1,0:T(8,128)(2,1)}, bf16[128,2048]{1,0:T(8,128)(2,1)S(1)}, u32[]{:S(2)}, u32[]{:S(2)}) collective-permute-start(bf16[128,2048]{1,0:T(8,128)(2,1)} %collective-permute-done.11.refs_4_), channel_id=1, source_target_pairs={{0,8},{2,10},{4,12},{6,14},{8,0},{10,2},{12,4},{14,6},{16,24},{18,... | collective-permute-start | bytes 1572872 | tf_op jit(solution)/shard_map/ppermute | solution.py:578
  94.1 14.1 %collective-permute-start.17 = (bf16[512,512]{1,0:T(8,128)(2,1)}, bf16[512,512]{1,0:T(8,128)(2,1)S(1)}, u32[]{:S(2)}, u32[]{:S(2)}) collective-permute-start(bf16[512,512]{1,0:T(8,128)(2,1)} %copy-done.6), channel_id=1, source_target_pairs={{0,4},{2,6},{4,0},{6,2},{8,12},{10,14},{12,8},{14,10},{16,20},{18,... | collective-permute-start | bytes 1572872 | tf_op jit(solution)/shard_map/ppermute | solution.py:578
  108.3 5.8 %collective-permute-start.23 = (bf16[128,2048]{1,0:T(8,128)(2,1)S(1)}, bf16[128,2048]{1,0:T(8,128)(2,1)S(1)}, u32[]{:S(2)}, u32[]{:S(2)}) collective-permute-start(bf16[128,2048]{1,0:T(8,128)(2,1)S(1)} %collective-permute-done.16.refs_3_), channel_id=1, source_target_pairs={{0,1},{1,0},{2,3},{3,2},{4,5},{5,4},{6,7},{7,6},{8,9},{9,8},{10,11... | collective-permute-start | bytes 1572872 | tf_op jit(solution)/shard_map/ppermute | solution.py:575
  109.0 15.6 %collective-permute-start.21 = (bf16[512,512]{1,0:T(8,128)(2,1)S(1)}, bf16[512,512]{1,0:T(8,128)(2,1)S(1)}, u32[]{:S(2)}, u32[]{:S(2)}) collective-permute-start(bf16[512,512]{1,0:T(8,128)(2,1)S(1)} %copy-done.5), channel_id=1, source_target_pairs={{0,4},{2,6},{4,0},{6,2},{8,12},{10,14},{12,8},{14,10},{16,20},{18,... | collective-permute-start | bytes 1572872 | tf_op jit(solution)/shard_map/ppermute | solution.py:578
  109.7 15.0 %collective-permute-start.20 = (bf16[256,512]{1,0:T(8,128)(2,1)S(1)}, bf16[256,512]{1,0:T(8,128)(2,1)S(1)}, u32[]{:S(2)}, u32[]{:S(2)}) collective-permute-start(bf16[256,512]{1,0:T(8,128)(2,1)S(1)} %get-tuple-element.160), channel_id=1, source_target_pairs={{0,16},{2,18},{4,20},{6,22},{8,24},{10,26},{12,28},{14,30},{16,0},... | collective-permute-start | bytes 786440 | tf_op jit(solution)/shard_map/ppermute | solution.py:578
  111.3 8.4 %collective-permute-start.22 = (f32[73,128]{1,0:T(8,128)S(1)}, f32[73,128]{1,0:T(8,128)S(1)}, u32[]{:S(2)}, u32[]{:S(2)}) collective-permute-start(f32[73,128]{1,0:T(8,128)S(1)} %add_select_fusion.2), channel_id=1, source_target_pairs={{0,2},{2,0},{4,6},{6,4},{8,10},{10,8},{12,14},{14,12},{16,18},{18,... | collective-permute-start | bytes 112136 | tf_op jit(solution)/shard_map/ppermute | solution.py:578
  125.4 16.8 %collective-permute-start.25 = (bf16[512,512]{1,0:T(8,128)(2,1)}, bf16[512,512]{1,0:T(8,128)(2,1)S(1)}, u32[]{:S(2)}, u32[]{:S(2)}) collective-permute-start(bf16[512,512]{1,0:T(8,128)(2,1)} %get-tuple-element.183), channel_id=1, source_target_pairs={{0,4},{2,6},{4,0},{6,2},{8,12},{10,14},{12,8},{14,10},{16,20},{18,... | collective-permute-start | bytes 1572872 | tf_op jit(solution)/shard_map/ppermute | solution.py:578
  126.9 15.2 %collective-permute-start.24 = (bf16[256,512]{1,0:T(8,128)(2,1)S(1)}, bf16[256,512]{1,0:T(8,128)(2,1)S(1)}, u32[]{:S(2)}, u32[]{:S(2)}) collective-permute-start(bf16[256,512]{1,0:T(8,128)(2,1)S(1)} %get-tuple-element.181), channel_id=1, source_target_pairs={{0,16},{2,18},{4,20},{6,22},{8,24},{10,26},{12,28},{14,30},{16,0},... | collective-permute-start | bytes 786440 | tf_op jit(solution)/shard_map/ppermute | solution.py:578
  127.0 6.6 %collective-permute-start.26 = (f32[73,128]{1,0:T(8,128)S(1)}, f32[73,128]{1,0:T(8,128)}, u32[]{:S(2)}, u32[]{:S(2)}) collective-permute-start(f32[73,128]{1,0:T(8,128)S(1)} %add_select_fusion.1), channel_id=1, source_target_pairs={{0,8},{2,10},{4,12},{6,14},{8,0},{10,2},{12,4},{14,6},{16,24},{18,... | collective-permute-start | bytes 112136 | tf_op jit(solution)/shard_map/ppermute | solution.py:578
  130.0 7.8 %collective-permute-start.27 = (bf16[64,512]{1,0:T(8,128)(2,1)S(1)}, bf16[64,512]{1,0:T(8,128)(2,1)S(1)}, u32[]{:S(2)}, u32[]{:S(2)}) collective-permute-start(bf16[64,512]{1,0:T(8,128)(2,1)S(1)} %get-tuple-element.189), channel_id=1, source_target_pairs={{0,2},{2,0},{4,6},{6,4},{8,10},{10,8},{12,14},{14,12},{16,18},{18,... | collective-permute-start | bytes 196616 | tf_op jit(solution)/shard_map/ppermute | solution.py:578
  131.3 9.9 %collective-permute-start.28 = (bf16[64,512]{1,0:T(8,128)(2,1)S(1)}, bf16[64,512]{1,0:T(8,128)(2,1)S(1)}, u32[]{:S(2)}, u32[]{:S(2)}) collective-permute-start(bf16[64,512]{1,0:T(8,128)(2,1)S(1)} %get-tuple-element.190), channel_id=1, source_target_pairs={{0,8},{2,10},{4,12},{6,14},{8,0},{10,2},{12,4},{14,6},{16,24},{18,... | collective-permute-start | bytes 196616 | tf_op jit(solution)/shard_map/ppermute | solution.py:578
  133.7 8.5 %collective-permute-start.29 = (bf16[64,512]{1,0:T(8,128)(2,1)S(1)}, bf16[64,512]{1,0:T(8,128)(2,1)S(1)}, u32[]{:S(2)}, u32[]{:S(2)}) collective-permute-start(bf16[64,512]{1,0:T(8,128)(2,1)S(1)} %get-tuple-element.191), channel_id=1, source_target_pairs={{0,10},{2,8},{4,14},{6,12},{8,2},{10,0},{12,6},{14,4},{16,26},{18,... | collective-permute-start | bytes 196616 | tf_op jit(solution)/shard_map/ppermute | solution.py:578
  142.9 14.8 %collective-permute-start.30 = (bf16[256,512]{1,0:T(8,128)(2,1)S(1)}, bf16[256,512]{1,0:T(8,128)(2,1)S(1)}, u32[]{:S(2)}, u32[]{:S(2)}) collective-permute-start(bf16[256,512]{1,0:T(8,128)(2,1)S(1)} %get-tuple-element.195), channel_id=1, source_target_pairs={{0,16},{2,18},{4,20},{6,22},{8,24},{10,26},{12,28},{14,30},{16,0},... | collective-permute-start | bytes 786440 | tf_op jit(solution)/shard_map/ppermute | solution.py:578
  143.8 13.9 %collective-permute-start.31 = (bf16[64,512]{1,0:T(8,128)(2,1)S(1)}, bf16[64,512]{1,0:T(8,128)(2,1)S(1)}, u32[]{:S(2)}, u32[]{:S(2)}) collective-permute-start(bf16[64,512]{1,0:T(8,128)(2,1)S(1)} %get-tuple-element.199), channel_id=1, source_target_pairs={{0,2},{2,0},{4,6},{6,4},{8,10},{10,8},{12,14},{14,12},{16,18},{18,... | collective-permute-start | bytes 196616 | tf_op jit(solution)/shard_map/ppermute | solution.py:578
  145.0 12.7 %collective-permute-start.32 = (bf16[64,512]{1,0:T(8,128)(2,1)S(1)}, bf16[64,512]{1,0:T(8,128)(2,1)S(1)}, u32[]{:S(2)}, u32[]{:S(2)}) collective-permute-start(bf16[64,512]{1,0:T(8,128)(2,1)S(1)} %get-tuple-element.200), channel_id=1, source_target_pairs={{0,8},{2,10},{4,12},{6,14},{8,0},{10,2},{12,4},{14,6},{16,24},{18,... | collective-permute-start | bytes 196616 | tf_op jit(solution)/shard_map/ppermute | solution.py:578
  147.3 10.4 %collective-permute-start.33 = (bf16[64,512]{1,0:T(8,128)(2,1)S(1)}, bf16[64,512]{1,0:T(8,128)(2,1)S(1)}, u32[]{:S(2)}, u32[]{:S(2)}) collective-permute-start(bf16[64,512]{1,0:T(8,128)(2,1)S(1)} %get-tuple-element.201), channel_id=1, source_target_pairs={{0,10},{2,8},{4,14},{6,12},{8,2},{10,0},{12,6},{14,4},{16,26},{18,... | collective-permute-start | bytes 196616 | tf_op jit(solution)/shard_map/ppermute | solution.py:578
  148.6 7.8 %collective-permute-start.37 = (f32[73,128]{1,0:T(8,128)S(1)}, f32[73,128]{1,0:T(8,128)S(1)}, u32[]{:S(2)}, u32[]{:S(2)}) collective-permute-start(f32[73,128]{1,0:T(8,128)S(1)} %add_select_fusion), channel_id=1, source_target_pairs={{0,1},{1,0},{2,3},{3,2},{4,5},{5,4},{6,7},{7,6},{8,9},{9,8},{10,11... | collective-permute-start | bytes 112136 | tf_op jit(solution)/shard_map/ppermute | solution.py:575
  158.4 5.5 %collective-permute-start.34 = (bf16[64,512]{1,0:T(8,128)(2,1)S(1)}, bf16[64,512]{1,0:T(8,128)(2,1)S(1)}, u32[]{:S(2)}, u32[]{:S(2)}) collective-permute-start(bf16[64,512]{1,0:T(8,128)(2,1)S(1)} %get-tuple-element.213), channel_id=1, source_target_pairs={{0,2},{2,0},{4,6},{6,4},{8,10},{10,8},{12,14},{14,12},{16,18},{18,... | collective-permute-start | bytes 196616 | tf_op jit(solution)/shard_map/ppermute | solution.py:578
  (24 other events, 184.1 us)

commit v4 on v3

--- a/solution.py
+++ b/solution.py
@@ -681,7 +681,7 @@
         return functools.reduce(lambda a, b: jnp.where(is_top, jnp.maximum(a, b), a + b), (msg, *came))
 
     near = [1 << b for b in rs_bits[:2]]
-    came = [hop(msg, m) for m in near + [near[0] | near[1]]]
+    came = [hop(msg, m) for m in [near[0] | near[1]] + near]
     later = [b for b in range(n_bits) if b not in rs_bits[:2]]
     restored = exchange(back)
 
@@ -766,7 +766,8 @@
             flops=1 << 26,
             scratch=[pltpu.VMEM((n, w), F32)],
         )
-        return [pieces[0]] + [hop(p, m) for p, m in zip(pieces[1:], masks)]
+        far_first = [hop(p, m) for p, m in zip(pieces[:0:-1], masks[::-1])]
+        return [pieces[0]] + far_first[::-1]
 
     def clip(msg):
         threshold = clip_tau[0].astype(F32)
@@ -844,6 +845,7 @@
             mlp_pieces[1:] = done[-3:]
             grad_down = join_mlp(mlp_pieces)
     attn_pieces = hand_out((keeps[2], recvs[2]))
+    msg = after(msg, attn_pieces[0])
     grad_up, *attn_pieces[1:] = lax.optimization_barrier((grad_up, *attn_pieces[1:]))
     grad_down = grad_down.T
     grad_qkv, grad_out = kernel_call(

time: 169 us -> 167 us (0.988)
  transfers between devices with their start and end apart: 40 -> 40, of which waited for: 17 -> 16; matrix products, arithmetic and copies ran while one was open for 6% -> 6% of each run, Pallas kernels for 32% -> 33%
where the time goes in v4:
time: 167 us
  Pallas kernels  66.3 us (40%)
  starting transfers between devices  45.5 us (27%)
  waiting for transfers between devices  41.5 us (25%)
  local copies, waits for them, and re-layouts  8.81 us (5%)
  other arithmetic  2.86 us (2%)
  between operations  1.8 us (1%)
    pallas_call x20, Pallas kernels, kernel_call(): pl.pallas_call(run, out_shape=shapes, in_specs=specs, out_specs=out_specs...  61.3 us
    ppermute x26, starting transfers between devices, hop(): return lax.ppermute(x, 'dp', [(i, i ^ mask) for i in range(n_dp)])  31.8 us
    ppermute x26, waiting for transfers between devices, hop(): return lax.ppermute(x, 'dp', [(i, i ^ mask) for i in range(n_dp)])  26.4 us
    all_to_all x2, starting transfers between devices, exchange(): return lax.all_to_all(x, 'dp', split_axis=0, concat_axis=0, tiled=True)  11.9 us
    all_to_all x2, waiting for transfers between devices, exchange(): return lax.all_to_all(x, 'dp', split_axis=0, concat_axis=0, tiled=True)  10.1 us
    unnamed x44, local copies, waits for them, and re-layouts  5.82 us
    ppermute x12, waiting for transfers between devices, swap(): return lax.ppermute(x, 'tensor', [(0, 1), (1, 0)])  5.04 us
    pallas_call x1, Pallas kernels, clip(): pl.pallas_call(clip_kernel, grid=(4,), out_shape=jax.ShapeDtypeStruct((wi...  4.99 us
  transfers between devices with their start and end apart: 40, of which 16 were waited for; matrix products, arithmetic and copies ran while one was open for 6% of the time, Pallas kernels for 33%

profile of v4, /device:TPU:0, one launch (start us, length us, event | category | flops | bytes accessed | tf_op | source)
XLA Modules:
  0.0 166.7 jit_solution(4761425035498843993)
XLA Ops:
  0.6 2.3 %route_kernel.1 = (bf16[128,2176]{1,0:T(8,128)(2,1)}, bf16[128,128]{1,0:T(8,128)(2,1)S(1)}) custom-call(s32[1,128]{1,0:T(1,128)} %bitcast.67, s32[1,4]{1,0:T(1,128)} %refs_1_.1, bf16[128,1024]{1,0:T(8,128)(2,1)} %refs_2_.2, bf16[128,1024]{1,0:T(8,128)(2,1)} %refs_3_.2), custom_call_target="tpu_custom_call" | custom-call | flops 67108864 | bytes 524816 | tf_op jit(solution)/shard_map/route_kernel/pallas_call | solution.py:157
  2.9 8.4 %all-to-all-start = ((bf16[16,8,2176]{2,1,0:T(8,128)(2,1)}), bf16[16,8,2176]{2,1,0:T(8,128)(2,1)S(1)}, u32[]{:S(2)}, u32[]{:S(2)}) async-start(bf16[16,8,2176]{2,1,0:T(8,128)(2,1)} %bitcast.5), calls=%async_computation | async-start | bytes 1114112 | tf_op jit(solution)/shard_map/all_to_all | solution.py:581
  16.9 10.1 %all-to-all-done = bf16[16,8,2176]{2,1,0:T(8,128)(2,1)S(1)} async-done(((bf16[16,8,2176]{2,1,0:T(8,128)(2,1)}), bf16[16,8,2176]{2,1,0:T(8,128)(2,1)S(1)}, u32[]{:S(2)}, u32[]{:S(2)}) %all-to-all-start) | async-done | bytes 557088 | tf_op jit(solution)/shard_map/all_to_all | solution.py:581
  26.9 2.0 %collective-permute-done.refs_2_.refs_5_ = bf16[128,2176]{1,0:T(8,128)(2,1)S(1)} collective-permute-done((bf16[128,2176]{1,0:T(8,128)(2,1)S(1)}, bf16[128,2176]{1,0:T(8,128)(2,1)S(1)}, u32[]{:S(2)}, u32[]{:S(2)}) %collective-permute-start) | collective-permute-done | bytes 557088 | tf_op jit(solution)/shard_map/ppermute | solution.py:575
  28.9 5.2 %attn_kernel.1 = (bf16[256,1024]{1,0:T(8,128)(2,1)S(1)}, bf16[256,1024]{1,0:T(8,128)(2,1)S(1)}, bf16[256,1536]{1,0:T(8,128)(2,1)S(1)}, f32[256,128]{1,0:T(8,128)...) custom-call(s32[8]{0:T(128)S(1)} %concatenate.18.refs_0_, bf16[128,2176]{1,0:T(8,128)(2,1)S(1)} %bitcast.44, ...), custom_call_target="tpu_custom_call" | custom-call | flops 3221225472 | bytes 5343264 | tf_op jit(solution)/shard_map/attn_kernel/pallas_call | solution.py:157
  34.3 1.8 %collective-permute-done.1.refs_2_ = bf16[256,1024]{1,0:T(8,128)(2,1)S(1)} collective-permute-done((bf16[256,1024]{1,0:T(8,128)(2,1)S(1)}, bf16[256,1024]{1,0:T(8,128)(2,1)S(1)}, u32[]{:S(2)}, u32[]{:S(2)}) %collective-permute-start.1) | collective-permute-done | bytes 524320 | tf_op jit(solution)/shard_map/ppermute | solution.py:575
  38.8 8.0 %mlp_kernel.1 = (bf16[256,1024]{1,0:T(8,128)(2,1)S(1)}, f32[128,1024]{1,0:T(8,128)S(1)}, bf16[128,1024]{1,0:T(8,128)(2,1)S(1)}, f32[1,2048]{1,0:T(1,128)S(1)}) custom-call(bf16[256,1024]{1,0:T(8,128)(2,1)S(1)} %get-tuple-element.142.refs_0_.refs_1_, bf16[256,1024]{1,0:T(8,128)(2,1)S(1)} %get-tuple-element.124.refs_1_.refs_3_.refs_2_, ...), custom_call_target="tpu_custom_call" | custom-call | flops 4294967296 | bytes 9469952 | tf_op jit(solution)/shard_map/mlp_kernel/pallas_call | solution.py:157
  46.8 4.0 %collective-permute-done.2.refs_3_ = bf16[128,2048]{1,0:T(8,128)(2,1)S(1)} collective-permute-done((bf16[128,2048]{1,0:T(8,128)(2,1)S(1)}, bf16[128,2048]{1,0:T(8,128)(2,1)S(1)}, u32[]{:S(2)}, u32[]{:S(2)}) %collective-permute-start.2) | collective-permute-done | bytes 524320 | tf_op jit(solution)/shard_map/ppermute | solution.py:578
  51.1 1.5 collective-permute-start.5
  53.5 1.6 gmid_kernel.1
  55.1 7.7 %attn_grad_kernel.1 = (f32[128,1024]{1,0:T(8,128)S(1)}, bf16[128,1024]{1,0:T(8,128)(2,1)S(1)}, f32[3,512]{1,0:T(4,128)S(1)}) custom-call(s32[8]{0:T(128)S(1)} %concatenate.18.refs_0_, bf16[256,1024]{1,0:T(8,128)(2,1)S(1)} %get-tuple-element.130.refs_1_.refs_3_, bf16[512,1024]{1,0:T(8,128)(2,1)} %refs_7_.1, bf16[256,1536]{1,0:T(8,128)(2,1)S(1)} %get-tuple-element.131.refs_3_, ...), custom_call_target="tpu_custom_call" | custom-call | flops 3221225472 | bytes 5636128 | tf_op jit(solution)/shard_map/attn_grad_kernel/pallas_call | solution.py:157
  62.8 2.7 %collective-permute-done.5.refs_5_ = bf16[128,2048]{1,0:T(8,128)(2,1)} collective-permute-done((bf16[128,2048]{1,0:T(8,128)(2,1)S(1)}, bf16[128,2048]{1,0:T(8,128)(2,1)}, u32[]{:S(2)}, u32[]{:S(2)}) %collective-permute-start.5) | collective-permute-done | bytes 524320 | tf_op jit(solution)/shard_map/ppermute | solution.py:578
  65.6 1.5 collective-permute-start.11
  68.7 1.6 last_kernel.1
  70.3 3.6 %all-to-all-start.1 = ((bf16[16,8,2048]{2,1,0:T(8,128)(2,1)}), bf16[16,8,2048]{2,1,0:T(8,128)(2,1)S(1)}, u32[]{:S(2)}, u32[]{:S(2)}) async-start(bf16[16,8,2048]{2,1,0:T(8,128)(2,1)} %bitcast.8), calls=%async_computation.1 | async-start | bytes 1048576 | tf_op jit(solution)/shard_map/all_to_all | solution.py:581
  73.9 3.7 %collective-permute-start.13 = (f32[73,128]{1,0:T(8,128)S(1)}, f32[73,128]{1,0:T(8,128)S(1)}, u32[]{:S(2)}, u32[]{:S(2)}) collective-permute-start(f32[73,128]{1,0:T(8,128)S(1)} %bitcast.58), channel_id=1, source_target_pairs={{0,20},{2,22},{4,16},{6,18},{8,28},{10,30},{12,24},{14,26},{16,4},... | collective-permute-start | bytes 112136 | tf_op jit(solution)/shard_map/ppermute | solution.py:578
  79.2 9.4 %mlp_weights_kernel.1 = (bf16[512,512]{1,0:T(8,128)(2,1)S(1)}, f32[512,512]{1,0:T(8,128)S(1)}, bf16[512,512]{1,0:T(8,128)(2,1)S(1)}, f32[512,512]{1,0:T(8,128)S(1)}) custom-call(s32[8]{0:T(128)S(1)} %concatenate.18.refs_0_, bf16[256,1024]{1,0:T(8,128)(2,1)} %copy-done.3, bf16[256,1024]{1,0:T(8,128)(2,1)} %copy-done.1, bf16[128,2048]{1,0:T(8,128)(2,1)} %copy-done.11, ...), custom_call_target="tpu_custom_call" | custom-call | flops 4294967296 | bytes 12615712 | tf_op jit(solution)/shard_map/mlp_weights_kernel/pallas_call | solution.py:157
  89.4 3.7 %collective-permute-done.13 = f32[73,128]{1,0:T(8,128)S(1)} collective-permute-done((f32[73,128]{1,0:T(8,128)S(1)}, f32[73,128]{1,0:T(8,128)S(1)}, u32[]{:S(2)}, u32[]{:S(2)}) %collective-permute-start.13) | collective-permute-done | bytes 37408 | tf_op jit(solution)/shard_map/ppermute | solution.py:578
  96.1 9.8 %attn_first_kernel.1.refs_2_ = f32[1024,512]{1,0:T(8,128)S(1)} custom-call(s32[8]{0:T(128)S(1)} %concatenate.18.refs_0_, bf16[128,2176]{1,0:T(8,128)(2,1)S(1)} %bitcast.47, bf16[256,1024]{1,0:T(8,128)(2,1)} %copy-done, bf16[256,1024]{1,0:T(8,128)(2,1)} %copy-done.2, bf16[128,2048]{1,0:T(8,128)(2,1)} %collective-permute-done.11.refs_4_, ...), custom_call_target="tpu_custom_call" | custom-call | flops 2415919104 | bytes 7899168 | tf_op jit(solution)/shard_map/attn_first_kernel/pallas_call | solution.py:157
  105.9 2.0 %collective-permute-done.16.refs_3_ = bf16[128,2048]{1,0:T(8,128)(2,1)S(1)} collective-permute-done((bf16[128,2048]{1,0:T(8,128)(2,1)}, bf16[128,2048]{1,0:T(8,128)(2,1)S(1)}, u32[]{:S(2)}, u32[]{:S(2)}) %collective-permute-start.16) | collective-permute-done | bytes 524320 | tf_op jit(solution)/shard_map/ppermute | solution.py:578
  109.7 1.6 collective-permute-start.20
  111.3 1.7 collective-permute-start.22
  114.1 5.7 %attn_weights_kernel.1 = (bf16[512,512]{1,0:T(8,128)(2,1)}, f32[512,512]{1,0:T(8,128)S(1)}) custom-call(s32[8]{0:T(128)S(1)} %concatenate.18.refs_0_, bf16[128,2176]{1,0:T(8,128)(2,1)S(1)} %bitcast.48, f32[1024,512]{1,0:T(8,128)S(1)} %attn_first_kernel.1.refs_2_, bf16[128,2048]{1,0:T(8,128)(2,1)} %copy-done.7, ...), custom_call_target="tpu_custom_call" | custom-call | flops 805306368 | bytes 7899168 | tf_op jit(solution)/shard_map/attn_weights_kernel/pallas_call | solution.py:157
  119.8 4.9 %collective-permute-done.20.refs_2_ = bf16[256,512]{1,0:T(8,128)(2,1)S(1)} collective-permute-done((bf16[256,512]{1,0:T(8,128)(2,1)S(1)}, bf16[256,512]{1,0:T(8,128)(2,1)S(1)}, u32[]{:S(2)}, u32[]{:S(2)}) %collective-permute-start.20) | collective-permute-done | bytes 262176 | tf_op jit(solution)/shard_map/ppermute | solution.py:578
  126.6 2.6 %collective-permute-start.26 = (f32[73,128]{1,0:T(8,128)S(1)}, f32[73,128]{1,0:T(8,128)}, u32[]{:S(2)}, u32[]{:S(2)}) collective-permute-start(f32[73,128]{1,0:T(8,128)S(1)} %add_select_fusion.1), channel_id=1, source_target_pairs={{0,8},{2,10},{4,12},{6,14},{8,0},{10,2},{12,4},{14,6},{16,24},{18,... | collective-permute-start | bytes 112136 | tf_op jit(solution)/shard_map/ppermute | solution.py:578
  130.9 2.3 %collective-permute-done.26 = f32[73,128]{1,0:T(8,128)} collective-permute-done((f32[73,128]{1,0:T(8,128)S(1)}, f32[73,128]{1,0:T(8,128)}, u32[]{:S(2)}, u32[]{:S(2)}) %collective-permute-start.26) | collective-permute-done | bytes 37408 | tf_op jit(solution)/shard_map/ppermute | solution.py:578
  133.2 3.5 %collective-permute-start.29 = (bf16[64,512]{1,0:T(8,128)(2,1)S(1)}, bf16[64,512]{1,0:T(8,128)(2,1)S(1)}, u32[]{:S(2)}, u32[]{:S(2)}) collective-permute-start(bf16[64,512]{1,0:T(8,128)(2,1)S(1)} %get-tuple-element.192), channel_id=1, source_target_pairs={{0,10},{2,8},{4,14},{6,12},{8,2},{10,0},{12,6},{14,4},{16,26},{18,... | collective-permute-start | bytes 196616 | tf_op jit(solution)/shard_map/ppermute | solution.py:578
  137.4 3.2 %collective-permute-done.28.refs_3_ = bf16[64,512]{1,0:T(8,128)(2,1)S(1)} collective-permute-done((bf16[64,512]{1,0:T(8,128)(2,1)S(1)}, bf16[64,512]{1,0:T(8,128)(2,1)S(1)}, u32[]{:S(2)}, u32[]{:S(2)}) %collective-permute-start.28) | collective-permute-done | bytes 65568 | tf_op jit(solution)/shard_map/ppermute | solution.py:578
  145.0 1.9 %collective-permute-start.32 = (bf16[64,512]{1,0:T(8,128)(2,1)S(1)}, bf16[64,512]{1,0:T(8,128)(2,1)S(1)}, u32[]{:S(2)}, u32[]{:S(2)}) collective-permute-start(bf16[64,512]{1,0:T(8,128)(2,1)S(1)} %get-tuple-element.201), channel_id=1, source_target_pairs={{0,8},{2,10},{4,12},{6,14},{8,0},{10,2},{12,4},{14,6},{16,24},{18,... | collective-permute-start | bytes 196616 | tf_op jit(solution)/shard_map/ppermute | solution.py:578
  149.0 5.0 %clip_kernel.1 = bf16[1024,2,512]{2,1,0:T(2,128)(2,1)} custom-call(bf16[3,1024,512]{2,1,0:T(8,128)(2,1)} %bitcast.56, f32[1,512]{1,0:T(1,128)} %reshape_reshape.3.factor), custom_call_target="tpu_custom_call" | custom-call | tf_op jit(solution)/shard_map/clip_kernel/pallas_call | solution.py:776
  155.4 1.6 collective-permute-done.33.refs_4_
  159.8 2.0 %collective-permute-start.36 = (bf16[64,512]{1,0:T(8,128)(2,1)S(1)}, bf16[64,512]{1,0:T(8,128)(2,1)S(1)}, u32[]{:S(2)}, u32[]{:S(2)}) collective-permute-start(bf16[64,512]{1,0:T(8,128)(2,1)S(1)} %get-tuple-element.216), channel_id=1, source_target_pairs={{0,10},{2,8},{4,14},{6,12},{8,2},{10,0},{12,6},{14,4},{16,26},{18,... | collective-permute-start | bytes 196616 | tf_op jit(solution)/shard_map/ppermute | solution.py:578
  (138 shorter events, 38.6 us)
Async XLA Ops:
  2.9 24.0 %all-to-all-start = ((bf16[16,8,2176]{2,1,0:T(8,128)(2,1)}), bf16[16,8,2176]{2,1,0:T(8,128)(2,1)S(1)}, u32[]{:S(2)}, u32[]{:S(2)}) async-start(bf16[16,8,2176]{2,1,0:T(8,128)(2,1)} %bitcast.5), calls=%async_computation | async-start | bytes 1114112 | tf_op jit(solution)/shard_map/all_to_all | solution.py:581
  36.8 14.0 %collective-permute-start.2 = (bf16[128,2048]{1,0:T(8,128)(2,1)S(1)}, bf16[128,2048]{1,0:T(8,128)(2,1)S(1)}, u32[]{:S(2)}, u32[]{:S(2)}) collective-permute-start(bf16[128,2048]{1,0:T(8,128)(2,1)S(1)} %get-tuple-element.126), channel_id=1, source_target_pairs={{0,2},{2,0},{4,6},{6,4},{8,10},{10,8},{12,14},{14,12},{16,18},{18,... | collective-permute-start | bytes 1572872 | tf_op jit(solution)/shard_map/ppermute | solution.py:578
  37.4 13.7 %collective-permute-start.3 = (bf16[128,2048]{1,0:T(8,128)(2,1)S(1)}, bf16[128,2048]{1,0:T(8,128)(2,1)S(1)}, u32[]{:S(2)}, u32[]{:S(2)}) collective-permute-start(bf16[128,2048]{1,0:T(8,128)(2,1)S(1)} %get-tuple-element.126), channel_id=1, source_target_pairs={{0,8},{2,10},{4,12},{6,14},{8,0},{10,2},{12,4},{14,6},{16,24},{18,... | collective-permute-start | bytes 1572872 | tf_op jit(solution)/shard_map/ppermute | solution.py:578
  51.1 14.4 %collective-permute-start.5 = (bf16[128,2048]{1,0:T(8,128)(2,1)S(1)}, bf16[128,2048]{1,0:T(8,128)(2,1)}, u32[]{:S(2)}, u32[]{:S(2)}) collective-permute-start(bf16[128,2048]{1,0:T(8,128)(2,1)S(1)} %collective-permute-done.3.refs_4_), channel_id=1, source_target_pairs={{0,2},{2,0},{4,6},{6,4},{8,10},{10,8},{12,14},{14,12},{16,18},{18,... | collective-permute-start | bytes 1572872 | tf_op jit(solution)/shard_map/ppermute | solution.py:578
  52.6 13.0 %collective-permute-start.6 = (bf16[128,2048]{1,0:T(8,128)(2,1)S(1)}, bf16[128,2048]{1,0:T(8,128)(2,1)S(1)}, u32[]{:S(2)}, u32[]{:S(2)}) collective-permute-start(bf16[128,2048]{1,0:T(8,128)(2,1)S(1)} %collective-permute-done.2.refs_3_), channel_id=1, source_target_pairs={{0,1},{1,0},{2,3},{3,2},{4,5},{5,4},{6,7},{7,6},{8,9},{9,8},{10,11... | collective-permute-start | bytes 1572872 | tf_op jit(solution)/shard_map/ppermute | solution.py:575
  52.8 12.8 %collective-permute-start.7 = (bf16[128,2048]{1,0:T(8,128)(2,1)S(1)}, bf16[128,2048]{1,0:T(8,128)(2,1)S(1)}, u32[]{:S(2)}, u32[]{:S(2)}) collective-permute-start(bf16[128,2048]{1,0:T(8,128)(2,1)S(1)} %collective-permute-done.3.refs_4_), channel_id=1, source_target_pairs={{0,1},{1,0},{2,3},{3,2},{4,5},{5,4},{6,7},{7,6},{8,9},{9,8},{10,11... | collective-permute-start | bytes 1572872 | tf_op jit(solution)/shard_map/ppermute | solution.py:575
  53.2 15.4 %collective-permute-start.9 = (bf16[128,1024]{1,0:T(8,128)(2,1)S(1)}, bf16[128,1024]{1,0:T(8,128)(2,1)S(1)}, u32[]{:S(2)}, u32[]{:S(2)}) collective-permute-start(bf16[128,1024]{1,0:T(8,128)(2,1)S(1)} %get-tuple-element.140), channel_id=1, source_target_pairs={{0,1},{1,0},{2,3},{3,2},{4,5},{5,4},{6,7},{7,6},{8,9},{9,8},{10,11... | collective-permute-start | bytes 786440 | tf_op jit(solution)/shard_map/ppermute | solution.py:575
  65.6 27.5 %collective-permute-start.11 = (bf16[128,2048]{1,0:T(8,128)(2,1)}, bf16[128,2048]{1,0:T(8,128)(2,1)}, u32[]{:S(2)}, u32[]{:S(2)}) collective-permute-start(bf16[128,2048]{1,0:T(8,128)(2,1)} %get-tuple-element.150), channel_id=1, source_target_pairs={{0,2},{2,0},{4,6},{6,4},{8,10},{10,8},{12,14},{14,12},{16,18},{18,... | collective-permute-start | bytes 1572872 | tf_op jit(solution)/shard_map/ppermute | solution.py:578
  67.2 25.9 %collective-permute-start.12 = (bf16[128,2048]{1,0:T(8,128)(2,1)}, bf16[128,2048]{1,0:T(8,128)(2,1)}, u32[]{:S(2)}, u32[]{:S(2)}) collective-permute-start(bf16[128,2048]{1,0:T(8,128)(2,1)} %get-tuple-element.150), channel_id=1, source_target_pairs={{0,8},{2,10},{4,12},{6,14},{8,0},{10,2},{12,4},{14,6},{16,24},{18,... | collective-permute-start | bytes 1572872 | tf_op jit(solution)/shard_map/ppermute | solution.py:578
  68.6 9.6 %collective-permute-start.10 = (bf16[128,2048]{1,0:T(8,128)(2,1)}, bf16[128,2048]{1,0:T(8,128)(2,1)S(1)}, u32[]{:S(2)}, u32[]{:S(2)}) collective-permute-start(bf16[128,2048]{1,0:T(8,128)(2,1)} %collective-permute-done.5.refs_5_), channel_id=1, source_target_pairs={{0,1},{1,0},{2,3},{3,2},{4,5},{5,4},{6,7},{7,6},{8,9},{9,8},{10,11... | collective-permute-start | bytes 1572872 | tf_op jit(solution)/shard_map/ppermute | solution.py:575
  70.3 22.9 %all-to-all-start.1 = ((bf16[16,8,2048]{2,1,0:T(8,128)(2,1)}), bf16[16,8,2048]{2,1,0:T(8,128)(2,1)S(1)}, u32[]{:S(2)}, u32[]{:S(2)}) async-start(bf16[16,8,2048]{2,1,0:T(8,128)(2,1)} %bitcast.8), calls=%async_computation.1 | async-start | bytes 1048576 | tf_op jit(solution)/shard_map/all_to_all | solution.py:581
  73.9 19.2 %collective-permute-start.13 = (f32[73,128]{1,0:T(8,128)S(1)}, f32[73,128]{1,0:T(8,128)S(1)}, u32[]{:S(2)}, u32[]{:S(2)}) collective-permute-start(f32[73,128]{1,0:T(8,128)S(1)} %bitcast.58), channel_id=1, source_target_pairs={{0,20},{2,22},{4,16},{6,18},{8,28},{10,30},{12,24},{14,26},{16,4},... | collective-permute-start | bytes 112136 | tf_op jit(solution)/shard_map/ppermute | solution.py:578
  77.6 15.5 %collective-permute-start.14 = (f32[73,128]{1,0:T(8,128)S(1)}, f32[73,128]{1,0:T(8,128)S(1)}, u32[]{:S(2)}, u32[]{:S(2)}) collective-permute-start(f32[73,128]{1,0:T(8,128)S(1)} %bitcast.59), channel_id=1, source_target_pairs={{0,4},{2,6},{4,0},{6,2},{8,12},{10,14},{12,8},{14,10},{16,20},{18,... | collective-permute-start | bytes 112136 | tf_op jit(solution)/shard_map/ppermute | solution.py:578
  79.0 14.1 %collective-permute-start.15 = (f32[73,128]{1,0:T(8,128)S(1)}, f32[73,128]{1,0:T(8,128)S(1)}, u32[]{:S(2)}, u32[]{:S(2)}) collective-permute-start(f32[73,128]{1,0:T(8,128)S(1)} %bitcast.60), channel_id=1, source_target_pairs={{0,16},{2,18},{4,20},{6,22},{8,24},{10,26},{12,28},{14,30},{16,0},... | collective-permute-start | bytes 112136 | tf_op jit(solution)/shard_map/ppermute | solution.py:578
  93.7 14.1 %collective-permute-start.16 = (bf16[128,2048]{1,0:T(8,128)(2,1)}, bf16[128,2048]{1,0:T(8,128)(2,1)S(1)}, u32[]{:S(2)}, u32[]{:S(2)}) collective-permute-start(bf16[128,2048]{1,0:T(8,128)(2,1)} %collective-permute-done.11.refs_4_), channel_id=1, source_target_pairs={{0,8},{2,10},{4,12},{6,14},{8,0},{10,2},{12,4},{14,6},{16,24},{18,... | collective-permute-start | bytes 1572872 | tf_op jit(solution)/shard_map/ppermute | solution.py:578
  93.7 14.1 %collective-permute-start.17 = (bf16[512,512]{1,0:T(8,128)(2,1)}, bf16[512,512]{1,0:T(8,128)(2,1)S(1)}, u32[]{:S(2)}, u32[]{:S(2)}) collective-permute-start(bf16[512,512]{1,0:T(8,128)(2,1)} %copy-done.6), channel_id=1, source_target_pairs={{0,4},{2,6},{4,0},{6,2},{8,12},{10,14},{12,8},{14,10},{16,20},{18,... | collective-permute-start | bytes 1572872 | tf_op jit(solution)/shard_map/ppermute | solution.py:578
  107.8 6.2 %collective-permute-start.23 = (bf16[128,2048]{1,0:T(8,128)(2,1)S(1)}, bf16[128,2048]{1,0:T(8,128)(2,1)S(1)}, u32[]{:S(2)}, u32[]{:S(2)}) collective-permute-start(bf16[128,2048]{1,0:T(8,128)(2,1)S(1)} %collective-permute-done.16.refs_3_), channel_id=1, source_target_pairs={{0,1},{1,0},{2,3},{3,2},{4,5},{5,4},{6,7},{7,6},{8,9},{9,8},{10,11... | collective-permute-start | bytes 1572872 | tf_op jit(solution)/shard_map/ppermute | solution.py:575
  108.6 16.0 %collective-permute-start.21 = (bf16[512,512]{1,0:T(8,128)(2,1)S(1)}, bf16[512,512]{1,0:T(8,128)(2,1)S(1)}, u32[]{:S(2)}, u32[]{:S(2)}) collective-permute-start(bf16[512,512]{1,0:T(8,128)(2,1)S(1)} %copy-done.5), channel_id=1, source_target_pairs={{0,4},{2,6},{4,0},{6,2},{8,12},{10,14},{12,8},{14,10},{16,20},{18,... | collective-permute-start | bytes 1572872 | tf_op jit(solution)/shard_map/ppermute | solution.py:578
  109.7 15.0 %collective-permute-start.20 = (bf16[256,512]{1,0:T(8,128)(2,1)S(1)}, bf16[256,512]{1,0:T(8,128)(2,1)S(1)}, u32[]{:S(2)}, u32[]{:S(2)}) collective-permute-start(bf16[256,512]{1,0:T(8,128)(2,1)S(1)} %get-tuple-element.161), channel_id=1, source_target_pairs={{0,16},{2,18},{4,20},{6,22},{8,24},{10,26},{12,28},{14,30},{16,0},... | collective-permute-start | bytes 786440 | tf_op jit(solution)/shard_map/ppermute | solution.py:578
  111.3 8.4 %collective-permute-start.22 = (f32[73,128]{1,0:T(8,128)S(1)}, f32[73,128]{1,0:T(8,128)S(1)}, u32[]{:S(2)}, u32[]{:S(2)}) collective-permute-start(f32[73,128]{1,0:T(8,128)S(1)} %add_select_fusion.2), channel_id=1, source_target_pairs={{0,2},{2,0},{4,6},{6,4},{8,10},{10,8},{12,14},{14,12},{16,18},{18,... | collective-permute-start | bytes 112136 | tf_op jit(solution)/shard_map/ppermute | solution.py:578
  125.4 16.7 %collective-permute-start.25 = (bf16[512,512]{1,0:T(8,128)(2,1)}, bf16[512,512]{1,0:T(8,128)(2,1)S(1)}, u32[]{:S(2)}, u32[]{:S(2)}) collective-permute-start(bf16[512,512]{1,0:T(8,128)(2,1)} %get-tuple-element.184), channel_id=1, source_target_pairs={{0,4},{2,6},{4,0},{6,2},{8,12},{10,14},{12,8},{14,10},{16,20},{18,... | collective-permute-start | bytes 1572872 | tf_op jit(solution)/shard_map/ppermute | solution.py:578
  126.5 15.6 %collective-permute-start.24 = (bf16[256,512]{1,0:T(8,128)(2,1)S(1)}, bf16[256,512]{1,0:T(8,128)(2,1)S(1)}, u32[]{:S(2)}, u32[]{:S(2)}) collective-permute-start(bf16[256,512]{1,0:T(8,128)(2,1)S(1)} %get-tuple-element.182), channel_id=1, source_target_pairs={{0,16},{2,18},{4,20},{6,22},{8,24},{10,26},{12,28},{14,30},{16,0},... | collective-permute-start | bytes 786440 | tf_op jit(solution)/shard_map/ppermute | solution.py:578
  126.6 6.6 %collective-permute-start.26 = (f32[73,128]{1,0:T(8,128)S(1)}, f32[73,128]{1,0:T(8,128)}, u32[]{:S(2)}, u32[]{:S(2)}) collective-permute-start(f32[73,128]{1,0:T(8,128)S(1)} %add_select_fusion.1), channel_id=1, source_target_pairs={{0,8},{2,10},{4,12},{6,14},{8,0},{10,2},{12,4},{14,6},{16,24},{18,... | collective-permute-start | bytes 112136 | tf_op jit(solution)/shard_map/ppermute | solution.py:578
  129.9 7.6 %collective-permute-start.27 = (bf16[64,512]{1,0:T(8,128)(2,1)S(1)}, bf16[64,512]{1,0:T(8,128)(2,1)S(1)}, u32[]{:S(2)}, u32[]{:S(2)}) collective-permute-start(bf16[64,512]{1,0:T(8,128)(2,1)S(1)} %get-tuple-element.190), channel_id=1, source_target_pairs={{0,2},{2,0},{4,6},{6,4},{8,10},{10,8},{12,14},{14,12},{16,18},{18,... | collective-permute-start | bytes 196616 | tf_op jit(solution)/shard_map/ppermute | solution.py:578
  130.9 9.8 %collective-permute-start.28 = (bf16[64,512]{1,0:T(8,128)(2,1)S(1)}, bf16[64,512]{1,0:T(8,128)(2,1)S(1)}, u32[]{:S(2)}, u32[]{:S(2)}) collective-permute-start(bf16[64,512]{1,0:T(8,128)(2,1)S(1)} %get-tuple-element.191), channel_id=1, source_target_pairs={{0,8},{2,10},{4,12},{6,14},{8,0},{10,2},{12,4},{14,6},{16,24},{18,... | collective-permute-start | bytes 196616 | tf_op jit(solution)/shard_map/ppermute | solution.py:578
  133.2 8.8 %collective-permute-start.29 = (bf16[64,512]{1,0:T(8,128)(2,1)S(1)}, bf16[64,512]{1,0:T(8,128)(2,1)S(1)}, u32[]{:S(2)}, u32[]{:S(2)}) collective-permute-start(bf16[64,512]{1,0:T(8,128)(2,1)S(1)} %get-tuple-element.192), channel_id=1, source_target_pairs={{0,10},{2,8},{4,14},{6,12},{8,2},{10,0},{12,6},{14,4},{16,26},{18,... | collective-permute-start | bytes 196616 | tf_op jit(solution)/shard_map/ppermute | solution.py:578
  142.9 14.1 %collective-permute-start.30 = (bf16[256,512]{1,0:T(8,128)(2,1)S(1)}, bf16[256,512]{1,0:T(8,128)(2,1)S(1)}, u32[]{:S(2)}, u32[]{:S(2)}) collective-permute-start(bf16[256,512]{1,0:T(8,128)(2,1)S(1)} %get-tuple-element.196), channel_id=1, source_target_pairs={{0,16},{2,18},{4,20},{6,22},{8,24},{10,26},{12,28},{14,30},{16,0},... | collective-permute-start | bytes 786440 | tf_op jit(solution)/shard_map/ppermute | solution.py:578
  143.6 11.8 %collective-permute-start.31 = (bf16[64,512]{1,0:T(8,128)(2,1)S(1)}, bf16[64,512]{1,0:T(8,128)(2,1)S(1)}, u32[]{:S(2)}, u32[]{:S(2)}) collective-permute-start(bf16[64,512]{1,0:T(8,128)(2,1)S(1)} %get-tuple-element.200), channel_id=1, source_target_pairs={{0,2},{2,0},{4,6},{6,4},{8,10},{10,8},{12,14},{14,12},{16,18},{18,... | collective-permute-start | bytes 196616 | tf_op jit(solution)/shard_map/ppermute | solution.py:578
  145.0 10.4 %collective-permute-start.32 = (bf16[64,512]{1,0:T(8,128)(2,1)S(1)}, bf16[64,512]{1,0:T(8,128)(2,1)S(1)}, u32[]{:S(2)}, u32[]{:S(2)}) collective-permute-start(bf16[64,512]{1,0:T(8,128)(2,1)S(1)} %get-tuple-element.201), channel_id=1, source_target_pairs={{0,8},{2,10},{4,12},{6,14},{8,0},{10,2},{12,4},{14,6},{16,24},{18,... | collective-permute-start | bytes 196616 | tf_op jit(solution)/shard_map/ppermute | solution.py:578
  146.9 10.1 %collective-permute-start.33 = (bf16[64,512]{1,0:T(8,128)(2,1)S(1)}, bf16[64,512]{1,0:T(8,128)(2,1)S(1)}, u32[]{:S(2)}, u32[]{:S(2)}) collective-permute-start(bf16[64,512]{1,0:T(8,128)(2,1)S(1)} %get-tuple-element.202), channel_id=1, source_target_pairs={{0,10},{2,8},{4,14},{6,12},{8,2},{10,0},{12,6},{14,4},{16,26},{18,... | collective-permute-start | bytes 196616 | tf_op jit(solution)/shard_map/ppermute | solution.py:578
  158.3 6.8 %collective-permute-start.34 = (bf16[64,512]{1,0:T(8,128)(2,1)S(1)}, bf16[64,512]{1,0:T(8,128)(2,1)S(1)}, u32[]{:S(2)}, u32[]{:S(2)}) collective-permute-start(bf16[64,512]{1,0:T(8,128)(2,1)S(1)} %get-tuple-element.214), channel_id=1, source_target_pairs={{0,2},{2,0},{4,6},{6,4},{8,10},{10,8},{12,14},{14,12},{16,18},{18,... | collective-permute-start | bytes 196616 | tf_op jit(solution)/shard_map/ppermute | solution.py:578
  159.8 5.6 %collective-permute-start.36 = (bf16[64,512]{1,0:T(8,128)(2,1)S(1)}, bf16[64,512]{1,0:T(8,128)(2,1)S(1)}, u32[]{:S(2)}, u32[]{:S(2)}) collective-permute-start(bf16[64,512]{1,0:T(8,128)(2,1)S(1)} %get-tuple-element.216), channel_id=1, source_target_pairs={{0,10},{2,8},{4,14},{6,12},{8,2},{10,0},{12,6},{14,4},{16,26},{18,... | collective-permute-start | bytes 196616 | tf_op jit(solution)/shard_map/ppermute | solution.py:578
  (24 other events, 178.2 us)

commit v5 on v4

--- a/solution.py
+++ b/solution.py
@@ -831,7 +831,7 @@
             extra = mlp_pieces[1:]
         if t == n_steps + 1:
             clipped_qk, head_factor, column_factor = clip(msg)
-            extra = extra + [clipped_qk, grad_down]
+            extra = [extra[0], clipped_qk, grad_down]
         done = lax.optimization_barrier([recvs[i] for i in active] + [came] + extra)
         recvs.update(zip(active, done))
         if t <= n_steps:
@@ -839,7 +839,7 @@
         if t == 1:
             out_tokens, grad_tokens, sends[2] = done[-3:]
         if t == n_steps + 1:
-            mlp_pieces[1:], clipped_qk, grad_down = done[-5:-2], done[-2], done[-1]
+            mlp_pieces[1], clipped_qk, grad_down = done[-3:]
             grad_up = join_mlp(mlp_pieces)
         if t == n_steps:
             mlp_pieces[1:] = done[-3:]

time: 167 us -> 167 us (level)
  no operation moved by 1% of the time
where the time goes in v5:
time: 167 us; the launch traced here: 166 us
  Pallas kernels  66.3 us (40%)
  starting transfers between devices  45.5 us (27%)
  waiting for transfers between devices  41.2 us (25%)
  local copies, waits for them, and re-layouts  8.81 us (5%)
  other arithmetic  2.86 us (2%)
  between operations  1.8 us (1%)
    pallas_call x20, Pallas kernels, kernel_call(): pl.pallas_call(run, out_shape=shapes, in_specs=specs, out_specs=out_specs...  61.3 us
    ppermute x26, starting transfers between devices, hop(): return lax.ppermute(x, 'dp', [(i, i ^ mask) for i in range(n_dp)])  31.8 us
    ppermute x26, waiting for transfers between devices, hop(): return lax.ppermute(x, 'dp', [(i, i ^ mask) for i in range(n_dp)])  26.1 us
    all_to_all x2, starting transfers between devices, exchange(): return lax.all_to_all(x, 'dp', split_axis=0, concat_axis=0, tiled=True)  11.9 us
    all_to_all x2, waiting for transfers between devices, exchange(): return lax.all_to_all(x, 'dp', split_axis=0, concat_axis=0, tiled=True)  10.1 us
    unnamed x44, local copies, waits for them, and re-layouts  5.82 us
    ppermute x12, waiting for transfers between devices, swap(): return lax.ppermute(x, 'tensor', [(0, 1), (1, 0)])  5.04 us
    pallas_call x1, Pallas kernels, clip(): pl.pallas_call(clip_kernel, grid=(4,), out_shape=jax.ShapeDtypeStruct((wi...  4.99 us
  transfers between devices with their start and end apart: 40, of which 16 were waited for; matrix products, arithmetic and copies ran while one was open for 6% of the time, Pallas kernels for 33%

profile of v5, /device:TPU:0, one launch (start us, length us, event | category | flops | bytes accessed | tf_op | source)
XLA Modules:
  0.0 166.4 jit_solution(3531975108264767954)
XLA Ops:
  0.6 2.3 %route_kernel.1 = (bf16[128,2176]{1,0:T(8,128)(2,1)}, bf16[128,128]{1,0:T(8,128)(2,1)S(1)}) custom-call(s32[1,128]{1,0:T(1,128)} %bitcast.67, s32[1,4]{1,0:T(1,128)} %refs_1_.1, bf16[128,1024]{1,0:T(8,128)(2,1)} %refs_2_.2, bf16[128,1024]{1,0:T(8,128)(2,1)} %refs_3_.2), custom_call_target="tpu_custom_call" | custom-call | flops 67108864 | bytes 524816 | tf_op jit(solution)/shard_map/route_kernel/pallas_call | solution.py:157
  2.9 8.4 %all-to-all-start = ((bf16[16,8,2176]{2,1,0:T(8,128)(2,1)}), bf16[16,8,2176]{2,1,0:T(8,128)(2,1)S(1)}, u32[]{:S(2)}, u32[]{:S(2)}) async-start(bf16[16,8,2176]{2,1,0:T(8,128)(2,1)} %bitcast.5), calls=%async_computation | async-start | bytes 1114112 | tf_op jit(solution)/shard_map/all_to_all | solution.py:581
  16.9 10.1 %all-to-all-done = bf16[16,8,2176]{2,1,0:T(8,128)(2,1)S(1)} async-done(((bf16[16,8,2176]{2,1,0:T(8,128)(2,1)}), bf16[16,8,2176]{2,1,0:T(8,128)(2,1)S(1)}, u32[]{:S(2)}, u32[]{:S(2)}) %all-to-all-start) | async-done | bytes 557088 | tf_op jit(solution)/shard_map/all_to_all | solution.py:581
  26.9 2.0 %collective-permute-done.refs_2_.refs_5_ = bf16[128,2176]{1,0:T(8,128)(2,1)S(1)} collective-permute-done((bf16[128,2176]{1,0:T(8,128)(2,1)S(1)}, bf16[128,2176]{1,0:T(8,128)(2,1)S(1)}, u32[]{:S(2)}, u32[]{:S(2)}) %collective-permute-start) | collective-permute-done | bytes 557088 | tf_op jit(solution)/shard_map/ppermute | solution.py:575
  28.9 5.2 %attn_kernel.1 = (bf16[256,1024]{1,0:T(8,128)(2,1)S(1)}, bf16[256,1024]{1,0:T(8,128)(2,1)S(1)}, bf16[256,1536]{1,0:T(8,128)(2,1)S(1)}, f32[256,128]{1,0:T(8,128)...) custom-call(s32[8]{0:T(128)S(1)} %concatenate.18.refs_0_, bf16[128,2176]{1,0:T(8,128)(2,1)S(1)} %bitcast.44, ...), custom_call_target="tpu_custom_call" | custom-call | flops 3221225472 | bytes 5343264 | tf_op jit(solution)/shard_map/attn_kernel/pallas_call | solution.py:157
  34.3 1.8 %collective-permute-done.1.refs_2_ = bf16[256,1024]{1,0:T(8,128)(2,1)S(1)} collective-permute-done((bf16[256,1024]{1,0:T(8,128)(2,1)S(1)}, bf16[256,1024]{1,0:T(8,128)(2,1)S(1)}, u32[]{:S(2)}, u32[]{:S(2)}) %collective-permute-start.1) | collective-permute-done | bytes 524320 | tf_op jit(solution)/shard_map/ppermute | solution.py:575
  38.8 8.0 %mlp_kernel.1 = (bf16[256,1024]{1,0:T(8,128)(2,1)S(1)}, f32[128,1024]{1,0:T(8,128)S(1)}, bf16[128,1024]{1,0:T(8,128)(2,1)S(1)}, f32[1,2048]{1,0:T(1,128)S(1)}) custom-call(bf16[256,1024]{1,0:T(8,128)(2,1)S(1)} %get-tuple-element.140.refs_0_.refs_1_, bf16[256,1024]{1,0:T(8,128)(2,1)S(1)} %get-tuple-element.122.refs_1_.refs_3_.refs_2_, ...), custom_call_target="tpu_custom_call" | custom-call | flops 4294967296 | bytes 9469952 | tf_op jit(solution)/shard_map/mlp_kernel/pallas_call | solution.py:157
  46.8 4.0 %collective-permute-done.2.refs_3_ = bf16[128,2048]{1,0:T(8,128)(2,1)S(1)} collective-permute-done((bf16[128,2048]{1,0:T(8,128)(2,1)S(1)}, bf16[128,2048]{1,0:T(8,128)(2,1)S(1)}, u32[]{:S(2)}, u32[]{:S(2)}) %collective-permute-start.2) | collective-permute-done | bytes 524320 | tf_op jit(solution)/shard_map/ppermute | solution.py:578
  51.1 1.5 collective-permute-start.5
  53.5 1.6 gmid_kernel.1
  55.1 7.7 %attn_grad_kernel.1 = (f32[128,1024]{1,0:T(8,128)S(1)}, bf16[128,1024]{1,0:T(8,128)(2,1)S(1)}, f32[3,512]{1,0:T(4,128)S(1)}) custom-call(s32[8]{0:T(128)S(1)} %concatenate.18.refs_0_, bf16[256,1024]{1,0:T(8,128)(2,1)S(1)} %get-tuple-element.128.refs_1_.refs_3_, bf16[512,1024]{1,0:T(8,128)(2,1)} %refs_7_.1, bf16[256,1536]{1,0:T(8,128)(2,1)S(1)} %get-tuple-element.129.refs_3_, ...), custom_call_target="tpu_custom_call" | custom-call | flops 3221225472 | bytes 5636128 | tf_op jit(solution)/shard_map/attn_grad_kernel/pallas_call | solution.py:157
  62.8 2.7 %collective-permute-done.5.refs_5_ = bf16[128,2048]{1,0:T(8,128)(2,1)} collective-permute-done((bf16[128,2048]{1,0:T(8,128)(2,1)S(1)}, bf16[128,2048]{1,0:T(8,128)(2,1)}, u32[]{:S(2)}, u32[]{:S(2)}) %collective-permute-start.5) | collective-permute-done | bytes 524320 | tf_op jit(solution)/shard_map/ppermute | solution.py:578
  65.6 1.5 collective-permute-start.11
  68.7 1.6 last_kernel.1
  70.3 3.6 %all-to-all-start.1 = ((bf16[16,8,2048]{2,1,0:T(8,128)(2,1)}), bf16[16,8,2048]{2,1,0:T(8,128)(2,1)S(1)}, u32[]{:S(2)}, u32[]{:S(2)}) async-start(bf16[16,8,2048]{2,1,0:T(8,128)(2,1)} %bitcast.8), calls=%async_computation.1 | async-start | bytes 1048576 | tf_op jit(solution)/shard_map/all_to_all | solution.py:581
  73.9 3.7 %collective-permute-start.13 = (f32[73,128]{1,0:T(8,128)S(1)}, f32[73,128]{1,0:T(8,128)S(1)}, u32[]{:S(2)}, u32[]{:S(2)}) collective-permute-start(f32[73,128]{1,0:T(8,128)S(1)} %bitcast.58), channel_id=1, source_target_pairs={{0,20},{2,22},{4,16},{6,18},{8,28},{10,30},{12,24},{14,26},{16,4},... | collective-permute-start | bytes 112136 | tf_op jit(solution)/shard_map/ppermute | solution.py:578
  79.2 9.4 %mlp_weights_kernel.1 = (bf16[512,512]{1,0:T(8,128)(2,1)S(1)}, f32[512,512]{1,0:T(8,128)S(1)}, bf16[512,512]{1,0:T(8,128)(2,1)S(1)}, f32[512,512]{1,0:T(8,128)S(1)}) custom-call(s32[8]{0:T(128)S(1)} %concatenate.18.refs_0_, bf16[256,1024]{1,0:T(8,128)(2,1)} %copy-done.3, bf16[256,1024]{1,0:T(8,128)(2,1)} %copy-done.1, bf16[128,2048]{1,0:T(8,128)(2,1)} %copy-done.11, ...), custom_call_target="tpu_custom_call" | custom-call | flops 4294967296 | bytes 12615712 | tf_op jit(solution)/shard_map/mlp_weights_kernel/pallas_call | solution.py:157
  89.4 3.7 %collective-permute-done.13 = f32[73,128]{1,0:T(8,128)S(1)} collective-permute-done((f32[73,128]{1,0:T(8,128)S(1)}, f32[73,128]{1,0:T(8,128)S(1)}, u32[]{:S(2)}, u32[]{:S(2)}) %collective-permute-start.13) | collective-permute-done | bytes 37408 | tf_op jit(solution)/shard_map/ppermute | solution.py:578
  96.1 9.8 %attn_first_kernel.1.refs_2_ = f32[1024,512]{1,0:T(8,128)S(1)} custom-call(s32[8]{0:T(128)S(1)} %concatenate.18.refs_0_, bf16[128,2176]{1,0:T(8,128)(2,1)S(1)} %bitcast.47, bf16[256,1024]{1,0:T(8,128)(2,1)} %copy-done, bf16[256,1024]{1,0:T(8,128)(2,1)} %copy-done.2, bf16[128,2048]{1,0:T(8,128)(2,1)} %collective-permute-done.11.refs_4_, ...), custom_call_target="tpu_custom_call" | custom-call | flops 2415919104 | bytes 7899168 | tf_op jit(solution)/shard_map/attn_first_kernel/pallas_call | solution.py:157
  105.9 2.0 %collective-permute-done.16.refs_3_ = bf16[128,2048]{1,0:T(8,128)(2,1)S(1)} collective-permute-done((bf16[128,2048]{1,0:T(8,128)(2,1)}, bf16[128,2048]{1,0:T(8,128)(2,1)S(1)}, u32[]{:S(2)}, u32[]{:S(2)}) %collective-permute-start.16) | collective-permute-done | bytes 524320 | tf_op jit(solution)/shard_map/ppermute | solution.py:578
  109.7 1.6 collective-permute-start.20
  111.3 1.7 collective-permute-start.22
  114.1 5.7 %attn_weights_kernel.1 = (bf16[512,512]{1,0:T(8,128)(2,1)}, f32[512,512]{1,0:T(8,128)S(1)}) custom-call(s32[8]{0:T(128)S(1)} %concatenate.18.refs_0_, bf16[128,2176]{1,0:T(8,128)(2,1)S(1)} %bitcast.48, f32[1024,512]{1,0:T(8,128)S(1)} %attn_first_kernel.1.refs_2_, bf16[128,2048]{1,0:T(8,128)(2,1)} %copy-done.7, ...), custom_call_target="tpu_custom_call" | custom-call | flops 805306368 | bytes 7899168 | tf_op jit(solution)/shard_map/attn_weights_kernel/pallas_call | solution.py:157
  119.8 4.9 %collective-permute-done.20.refs_2_ = bf16[256,512]{1,0:T(8,128)(2,1)S(1)} collective-permute-done((bf16[256,512]{1,0:T(8,128)(2,1)S(1)}, bf16[256,512]{1,0:T(8,128)(2,1)S(1)}, u32[]{:S(2)}, u32[]{:S(2)}) %collective-permute-start.20) | collective-permute-done | bytes 262176 | tf_op jit(solution)/shard_map/ppermute | solution.py:578
  126.6 2.6 %collective-permute-start.26 = (f32[73,128]{1,0:T(8,128)S(1)}, f32[73,128]{1,0:T(8,128)}, u32[]{:S(2)}, u32[]{:S(2)}) collective-permute-start(f32[73,128]{1,0:T(8,128)S(1)} %add_select_fusion.1), channel_id=1, source_target_pairs={{0,8},{2,10},{4,12},{6,14},{8,0},{10,2},{12,4},{14,6},{16,24},{18,... | collective-permute-start | bytes 112136 | tf_op jit(solution)/shard_map/ppermute | solution.py:578
  130.9 2.3 %collective-permute-done.26 = f32[73,128]{1,0:T(8,128)} collective-permute-done((f32[73,128]{1,0:T(8,128)S(1)}, f32[73,128]{1,0:T(8,128)}, u32[]{:S(2)}, u32[]{:S(2)}) %collective-permute-start.26) | collective-permute-done | bytes 37408 | tf_op jit(solution)/shard_map/ppermute | solution.py:578
  133.2 3.5 %collective-permute-start.29 = (bf16[64,512]{1,0:T(8,128)(2,1)S(1)}, bf16[64,512]{1,0:T(8,128)(2,1)S(1)}, u32[]{:S(2)}, u32[]{:S(2)}) collective-permute-start(bf16[64,512]{1,0:T(8,128)(2,1)S(1)} %get-tuple-element.190), channel_id=1, source_target_pairs={{0,10},{2,8},{4,14},{6,12},{8,2},{10,0},{12,6},{14,4},{16,26},{18,... | collective-permute-start | bytes 196616 | tf_op jit(solution)/shard_map/ppermute | solution.py:578
  137.4 3.2 %collective-permute-done.28.refs_3_ = bf16[64,512]{1,0:T(8,128)(2,1)S(1)} collective-permute-done((bf16[64,512]{1,0:T(8,128)(2,1)S(1)}, bf16[64,512]{1,0:T(8,128)(2,1)S(1)}, u32[]{:S(2)}, u32[]{:S(2)}) %collective-permute-start.28) | collective-permute-done | bytes 65568 | tf_op jit(solution)/shard_map/ppermute | solution.py:578
  140.6 1.4 collective-permute-done.29.refs_4_
  146.7 5.0 %clip_kernel.1 = bf16[1024,2,512]{2,1,0:T(2,128)(2,1)} custom-call(bf16[3,1024,512]{2,1,0:T(8,128)(2,1)} %bitcast.56, f32[1,512]{1,0:T(1,128)} %reshape_reshape.3.factor), custom_call_target="tpu_custom_call" | custom-call | tf_op jit(solution)/shard_map/clip_kernel/pallas_call | solution.py:776
  151.7 1.9 %collective-permute-start.32 = (bf16[64,512]{1,0:T(8,128)(2,1)S(1)}, bf16[64,512]{1,0:T(8,128)(2,1)S(1)}, u32[]{:S(2)}, u32[]{:S(2)}) collective-permute-start(bf16[64,512]{1,0:T(8,128)(2,1)S(1)} %get-tuple-element.208), channel_id=1, source_target_pairs={{0,8},{2,10},{4,12},{6,14},{8,0},{10,2},{12,4},{14,6},{16,24},{18,... | collective-permute-start | bytes 196616 | tf_op jit(solution)/shard_map/ppermute | solution.py:578
  159.8 1.6 collective-permute-start.36
  (138 shorter events, 38.8 us)
Async XLA Ops:
  2.9 24.0 %all-to-all-start = ((bf16[16,8,2176]{2,1,0:T(8,128)(2,1)}), bf16[16,8,2176]{2,1,0:T(8,128)(2,1)S(1)}, u32[]{:S(2)}, u32[]{:S(2)}) async-start(bf16[16,8,2176]{2,1,0:T(8,128)(2,1)} %bitcast.5), calls=%async_computation | async-start | bytes 1114112 | tf_op jit(solution)/shard_map/all_to_all | solution.py:581
  36.8 14.0 %collective-permute-start.2 = (bf16[128,2048]{1,0:T(8,128)(2,1)S(1)}, bf16[128,2048]{1,0:T(8,128)(2,1)S(1)}, u32[]{:S(2)}, u32[]{:S(2)}) collective-permute-start(bf16[128,2048]{1,0:T(8,128)(2,1)S(1)} %get-tuple-element.124), channel_id=1, source_target_pairs={{0,2},{2,0},{4,6},{6,4},{8,10},{10,8},{12,14},{14,12},{16,18},{18,... | collective-permute-start | bytes 1572872 | tf_op jit(solution)/shard_map/ppermute | solution.py:578
  37.4 13.7 %collective-permute-start.3 = (bf16[128,2048]{1,0:T(8,128)(2,1)S(1)}, bf16[128,2048]{1,0:T(8,128)(2,1)S(1)}, u32[]{:S(2)}, u32[]{:S(2)}) collective-permute-start(bf16[128,2048]{1,0:T(8,128)(2,1)S(1)} %get-tuple-element.124), channel_id=1, source_target_pairs={{0,8},{2,10},{4,12},{6,14},{8,0},{10,2},{12,4},{14,6},{16,24},{18,... | collective-permute-start | bytes 1572872 | tf_op jit(solution)/shard_map/ppermute | solution.py:578
  51.1 14.4 %collective-permute-start.5 = (bf16[128,2048]{1,0:T(8,128)(2,1)S(1)}, bf16[128,2048]{1,0:T(8,128)(2,1)}, u32[]{:S(2)}, u32[]{:S(2)}) collective-permute-start(bf16[128,2048]{1,0:T(8,128)(2,1)S(1)} %collective-permute-done.3.refs_4_), channel_id=1, source_target_pairs={{0,2},{2,0},{4,6},{6,4},{8,10},{10,8},{12,14},{14,12},{16,18},{18,... | collective-permute-start | bytes 1572872 | tf_op jit(solution)/shard_map/ppermute | solution.py:578
  52.6 13.0 %collective-permute-start.6 = (bf16[128,2048]{1,0:T(8,128)(2,1)S(1)}, bf16[128,2048]{1,0:T(8,128)(2,1)S(1)}, u32[]{:S(2)}, u32[]{:S(2)}) collective-permute-start(bf16[128,2048]{1,0:T(8,128)(2,1)S(1)} %collective-permute-done.2.refs_3_), channel_id=1, source_target_pairs={{0,1},{1,0},{2,3},{3,2},{4,5},{5,4},{6,7},{7,6},{8,9},{9,8},{10,11... | collective-permute-start | bytes 1572872 | tf_op jit(solution)/shard_map/ppermute | solution.py:575
  52.8 12.8 %collective-permute-start.7 = (bf16[128,2048]{1,0:T(8,128)(2,1)S(1)}, bf16[128,2048]{1,0:T(8,128)(2,1)S(1)}, u32[]{:S(2)}, u32[]{:S(2)}) collective-permute-start(bf16[128,2048]{1,0:T(8,128)(2,1)S(1)} %collective-permute-done.3.refs_4_), channel_id=1, source_target_pairs={{0,1},{1,0},{2,3},{3,2},{4,5},{5,4},{6,7},{7,6},{8,9},{9,8},{10,11... | collective-permute-start | bytes 1572872 | tf_op jit(solution)/shard_map/ppermute | solution.py:575
  53.2 15.4 %collective-permute-start.9 = (bf16[128,1024]{1,0:T(8,128)(2,1)S(1)}, bf16[128,1024]{1,0:T(8,128)(2,1)S(1)}, u32[]{:S(2)}, u32[]{:S(2)}) collective-permute-start(bf16[128,1024]{1,0:T(8,128)(2,1)S(1)} %get-tuple-element.138), channel_id=1, source_target_pairs={{0,1},{1,0},{2,3},{3,2},{4,5},{5,4},{6,7},{7,6},{8,9},{9,8},{10,11... | collective-permute-start | bytes 786440 | tf_op jit(solution)/shard_map/ppermute | solution.py:575
  65.6 27.5 %collective-permute-start.11 = (bf16[128,2048]{1,0:T(8,128)(2,1)}, bf16[128,2048]{1,0:T(8,128)(2,1)}, u32[]{:S(2)}, u32[]{:S(2)}) collective-permute-start(bf16[128,2048]{1,0:T(8,128)(2,1)} %get-tuple-element.148), channel_id=1, source_target_pairs={{0,2},{2,0},{4,6},{6,4},{8,10},{10,8},{12,14},{14,12},{16,18},{18,... | collective-permute-start | bytes 1572872 | tf_op jit(solution)/shard_map/ppermute | solution.py:578
  67.2 25.9 %collective-permute-start.12 = (bf16[128,2048]{1,0:T(8,128)(2,1)}, bf16[128,2048]{1,0:T(8,128)(2,1)}, u32[]{:S(2)}, u32[]{:S(2)}) collective-permute-start(bf16[128,2048]{1,0:T(8,128)(2,1)} %get-tuple-element.148), channel_id=1, source_target_pairs={{0,8},{2,10},{4,12},{6,14},{8,0},{10,2},{12,4},{14,6},{16,24},{18,... | collective-permute-start | bytes 1572872 | tf_op jit(solution)/shard_map/ppermute | solution.py:578
  68.6 9.6 %collective-permute-start.10 = (bf16[128,2048]{1,0:T(8,128)(2,1)}, bf16[128,2048]{1,0:T(8,128)(2,1)S(1)}, u32[]{:S(2)}, u32[]{:S(2)}) collective-permute-start(bf16[128,2048]{1,0:T(8,128)(2,1)} %collective-permute-done.5.refs_5_), channel_id=1, source_target_pairs={{0,1},{1,0},{2,3},{3,2},{4,5},{5,4},{6,7},{7,6},{8,9},{9,8},{10,11... | collective-permute-start | bytes 1572872 | tf_op jit(solution)/shard_map/ppermute | solution.py:575
  70.3 22.9 %all-to-all-start.1 = ((bf16[16,8,2048]{2,1,0:T(8,128)(2,1)}), bf16[16,8,2048]{2,1,0:T(8,128)(2,1)S(1)}, u32[]{:S(2)}, u32[]{:S(2)}) async-start(bf16[16,8,2048]{2,1,0:T(8,128)(2,1)} %bitcast.8), calls=%async_computation.1 | async-start | bytes 1048576 | tf_op jit(solution)/shard_map/all_to_all | solution.py:581
  73.9 19.2 %collective-permute-start.13 = (f32[73,128]{1,0:T(8,128)S(1)}, f32[73,128]{1,0:T(8,128)S(1)}, u32[]{:S(2)}, u32[]{:S(2)}) collective-permute-start(f32[73,128]{1,0:T(8,128)S(1)} %bitcast.58), channel_id=1, source_target_pairs={{0,20},{2,22},{4,16},{6,18},{8,28},{10,30},{12,24},{14,26},{16,4},... | collective-permute-start | bytes 112136 | tf_op jit(solution)/shard_map/ppermute | solution.py:578
  77.6 15.5 %collective-permute-start.14 = (f32[73,128]{1,0:T(8,128)S(1)}, f32[73,128]{1,0:T(8,128)S(1)}, u32[]{:S(2)}, u32[]{:S(2)}) collective-permute-start(f32[73,128]{1,0:T(8,128)S(1)} %bitcast.59), channel_id=1, source_target_pairs={{0,4},{2,6},{4,0},{6,2},{8,12},{10,14},{12,8},{14,10},{16,20},{18,... | collective-permute-start | bytes 112136 | tf_op jit(solution)/shard_map/ppermute | solution.py:578
  79.0 14.1 %collective-permute-start.15 = (f32[73,128]{1,0:T(8,128)S(1)}, f32[73,128]{1,0:T(8,128)S(1)}, u32[]{:S(2)}, u32[]{:S(2)}) collective-permute-start(f32[73,128]{1,0:T(8,128)S(1)} %bitcast.60), channel_id=1, source_target_pairs={{0,16},{2,18},{4,20},{6,22},{8,24},{10,26},{12,28},{14,30},{16,0},... | collective-permute-start | bytes 112136 | tf_op jit(solution)/shard_map/ppermute | solution.py:578
  93.7 14.1 %collective-permute-start.16 = (bf16[128,2048]{1,0:T(8,128)(2,1)}, bf16[128,2048]{1,0:T(8,128)(2,1)S(1)}, u32[]{:S(2)}, u32[]{:S(2)}) collective-permute-start(bf16[128,2048]{1,0:T(8,128)(2,1)} %collective-permute-done.11.refs_4_), channel_id=1, source_target_pairs={{0,8},{2,10},{4,12},{6,14},{8,0},{10,2},{12,4},{14,6},{16,24},{18,... | collective-permute-start | bytes 1572872 | tf_op jit(solution)/shard_map/ppermute | solution.py:578
  93.7 14.1 %collective-permute-start.17 = (bf16[512,512]{1,0:T(8,128)(2,1)}, bf16[512,512]{1,0:T(8,128)(2,1)S(1)}, u32[]{:S(2)}, u32[]{:S(2)}) collective-permute-start(bf16[512,512]{1,0:T(8,128)(2,1)} %copy-done.6), channel_id=1, source_target_pairs={{0,4},{2,6},{4,0},{6,2},{8,12},{10,14},{12,8},{14,10},{16,20},{18,... | collective-permute-start | bytes 1572872 | tf_op jit(solution)/shard_map/ppermute | solution.py:578
  107.8 6.2 %collective-permute-start.23 = (bf16[128,2048]{1,0:T(8,128)(2,1)S(1)}, bf16[128,2048]{1,0:T(8,128)(2,1)S(1)}, u32[]{:S(2)}, u32[]{:S(2)}) collective-permute-start(bf16[128,2048]{1,0:T(8,128)(2,1)S(1)} %collective-permute-done.16.refs_3_), channel_id=1, source_target_pairs={{0,1},{1,0},{2,3},{3,2},{4,5},{5,4},{6,7},{7,6},{8,9},{9,8},{10,11... | collective-permute-start | bytes 1572872 | tf_op jit(solution)/shard_map/ppermute | solution.py:575
  108.6 16.0 %collective-permute-start.21 = (bf16[512,512]{1,0:T(8,128)(2,1)S(1)}, bf16[512,512]{1,0:T(8,128)(2,1)S(1)}, u32[]{:S(2)}, u32[]{:S(2)}) collective-permute-start(bf16[512,512]{1,0:T(8,128)(2,1)S(1)} %copy-done.5), channel_id=1, source_target_pairs={{0,4},{2,6},{4,0},{6,2},{8,12},{10,14},{12,8},{14,10},{16,20},{18,... | collective-permute-start | bytes 1572872 | tf_op jit(solution)/shard_map/ppermute | solution.py:578
  109.7 15.0 %collective-permute-start.20 = (bf16[256,512]{1,0:T(8,128)(2,1)S(1)}, bf16[256,512]{1,0:T(8,128)(2,1)S(1)}, u32[]{:S(2)}, u32[]{:S(2)}) collective-permute-start(bf16[256,512]{1,0:T(8,128)(2,1)S(1)} %get-tuple-element.159), channel_id=1, source_target_pairs={{0,16},{2,18},{4,20},{6,22},{8,24},{10,26},{12,28},{14,30},{16,0},... | collective-permute-start | bytes 786440 | tf_op jit(solution)/shard_map/ppermute | solution.py:578
  111.3 8.4 %collective-permute-start.22 = (f32[73,128]{1,0:T(8,128)S(1)}, f32[73,128]{1,0:T(8,128)S(1)}, u32[]{:S(2)}, u32[]{:S(2)}) collective-permute-start(f32[73,128]{1,0:T(8,128)S(1)} %add_select_fusion.2), channel_id=1, source_target_pairs={{0,2},{2,0},{4,6},{6,4},{8,10},{10,8},{12,14},{14,12},{16,18},{18,... | collective-permute-start | bytes 112136 | tf_op jit(solution)/shard_map/ppermute | solution.py:578
  125.4 16.7 %collective-permute-start.25 = (bf16[512,512]{1,0:T(8,128)(2,1)}, bf16[512,512]{1,0:T(8,128)(2,1)S(1)}, u32[]{:S(2)}, u32[]{:S(2)}) collective-permute-start(bf16[512,512]{1,0:T(8,128)(2,1)} %get-tuple-element.182), channel_id=1, source_target_pairs={{0,4},{2,6},{4,0},{6,2},{8,12},{10,14},{12,8},{14,10},{16,20},{18,... | collective-permute-start | bytes 1572872 | tf_op jit(solution)/shard_map/ppermute | solution.py:578
  126.5 15.6 %collective-permute-start.24 = (bf16[256,512]{1,0:T(8,128)(2,1)S(1)}, bf16[256,512]{1,0:T(8,128)(2,1)S(1)}, u32[]{:S(2)}, u32[]{:S(2)}) collective-permute-start(bf16[256,512]{1,0:T(8,128)(2,1)S(1)} %get-tuple-element.180), channel_id=1, source_target_pairs={{0,16},{2,18},{4,20},{6,22},{8,24},{10,26},{12,28},{14,30},{16,0},... | collective-permute-start | bytes 786440 | tf_op jit(solution)/shard_map/ppermute | solution.py:578
  126.6 6.6 %collective-permute-start.26 = (f32[73,128]{1,0:T(8,128)S(1)}, f32[73,128]{1,0:T(8,128)}, u32[]{:S(2)}, u32[]{:S(2)}) collective-permute-start(f32[73,128]{1,0:T(8,128)S(1)} %add_select_fusion.1), channel_id=1, source_target_pairs={{0,8},{2,10},{4,12},{6,14},{8,0},{10,2},{12,4},{14,6},{16,24},{18,... | collective-permute-start | bytes 112136 | tf_op jit(solution)/shard_map/ppermute | solution.py:578
  129.9 7.6 %collective-permute-start.27 = (bf16[64,512]{1,0:T(8,128)(2,1)S(1)}, bf16[64,512]{1,0:T(8,128)(2,1)S(1)}, u32[]{:S(2)}, u32[]{:S(2)}) collective-permute-start(bf16[64,512]{1,0:T(8,128)(2,1)S(1)} %get-tuple-element.188), channel_id=1, source_target_pairs={{0,2},{2,0},{4,6},{6,4},{8,10},{10,8},{12,14},{14,12},{16,18},{18,... | collective-permute-start | bytes 196616 | tf_op jit(solution)/shard_map/ppermute | solution.py:578
  130.9 9.8 %collective-permute-start.28 = (bf16[64,512]{1,0:T(8,128)(2,1)S(1)}, bf16[64,512]{1,0:T(8,128)(2,1)S(1)}, u32[]{:S(2)}, u32[]{:S(2)}) collective-permute-start(bf16[64,512]{1,0:T(8,128)(2,1)S(1)} %get-tuple-element.189), channel_id=1, source_target_pairs={{0,8},{2,10},{4,12},{6,14},{8,0},{10,2},{12,4},{14,6},{16,24},{18,... | collective-permute-start | bytes 196616 | tf_op jit(solution)/shard_map/ppermute | solution.py:578
  133.2 8.8 %collective-permute-start.29 = (bf16[64,512]{1,0:T(8,128)(2,1)S(1)}, bf16[64,512]{1,0:T(8,128)(2,1)S(1)}, u32[]{:S(2)}, u32[]{:S(2)}) collective-permute-start(bf16[64,512]{1,0:T(8,128)(2,1)S(1)} %get-tuple-element.190), channel_id=1, source_target_pairs={{0,10},{2,8},{4,14},{6,12},{8,2},{10,0},{12,6},{14,4},{16,26},{18,... | collective-permute-start | bytes 196616 | tf_op jit(solution)/shard_map/ppermute | solution.py:578
  142.9 13.8 %collective-permute-start.30 = (bf16[256,512]{1,0:T(8,128)(2,1)S(1)}, bf16[256,512]{1,0:T(8,128)(2,1)S(1)}, u32[]{:S(2)}, u32[]{:S(2)}) collective-permute-start(bf16[256,512]{1,0:T(8,128)(2,1)S(1)} %get-tuple-element.194), channel_id=1, source_target_pairs={{0,16},{2,18},{4,20},{6,22},{8,24},{10,26},{12,28},{14,30},{16,0},... | collective-permute-start | bytes 786440 | tf_op jit(solution)/shard_map/ppermute | solution.py:578
  143.6 11.8 %collective-permute-start.31 = (bf16[64,512]{1,0:T(8,128)(2,1)S(1)}, bf16[64,512]{1,0:T(8,128)(2,1)S(1)}, u32[]{:S(2)}, u32[]{:S(2)}) collective-permute-start(bf16[64,512]{1,0:T(8,128)(2,1)S(1)} %get-tuple-element.198), channel_id=1, source_target_pairs={{0,2},{2,0},{4,6},{6,4},{8,10},{10,8},{12,14},{14,12},{16,18},{18,... | collective-permute-start | bytes 196616 | tf_op jit(solution)/shard_map/ppermute | solution.py:578
  151.7 8.1 %collective-permute-start.32 = (bf16[64,512]{1,0:T(8,128)(2,1)S(1)}, bf16[64,512]{1,0:T(8,128)(2,1)S(1)}, u32[]{:S(2)}, u32[]{:S(2)}) collective-permute-start(bf16[64,512]{1,0:T(8,128)(2,1)S(1)} %get-tuple-element.208), channel_id=1, source_target_pairs={{0,8},{2,10},{4,12},{6,14},{8,0},{10,2},{12,4},{14,6},{16,24},{18,... | collective-permute-start | bytes 196616 | tf_op jit(solution)/shard_map/ppermute | solution.py:578
  153.6 7.8 %collective-permute-start.33 = (bf16[64,512]{1,0:T(8,128)(2,1)S(1)}, bf16[64,512]{1,0:T(8,128)(2,1)S(1)}, u32[]{:S(2)}, u32[]{:S(2)}) collective-permute-start(bf16[64,512]{1,0:T(8,128)(2,1)S(1)} %get-tuple-element.209), channel_id=1, source_target_pairs={{0,10},{2,8},{4,14},{6,12},{8,2},{10,0},{12,6},{14,4},{16,26},{18,... | collective-permute-start | bytes 196616 | tf_op jit(solution)/shard_map/ppermute | solution.py:578
  157.9 6.8 %collective-permute-start.34 = (bf16[64,512]{1,0:T(8,128)(2,1)S(1)}, bf16[64,512]{1,0:T(8,128)(2,1)S(1)}, u32[]{:S(2)}, u32[]{:S(2)}) collective-permute-start(bf16[64,512]{1,0:T(8,128)(2,1)S(1)} %get-tuple-element.210), channel_id=1, source_target_pairs={{0,2},{2,0},{4,6},{6,4},{8,10},{10,8},{12,14},{14,12},{16,18},{18,... | collective-permute-start | bytes 196616 | tf_op jit(solution)/shard_map/ppermute | solution.py:578
  158.7 6.0 %collective-permute-start.35 = (bf16[64,512]{1,0:T(8,128)(2,1)S(1)}, bf16[64,512]{1,0:T(8,128)(2,1)S(1)}, u32[]{:S(2)}, u32[]{:S(2)}) collective-permute-start(bf16[64,512]{1,0:T(8,128)(2,1)S(1)} %get-tuple-element.211), channel_id=1, source_target_pairs={{0,8},{2,10},{4,12},{6,14},{8,0},{10,2},{12,4},{14,6},{16,24},{18,... | collective-permute-start | bytes 196616 | tf_op jit(solution)/shard_map/ppermute | solution.py:578
  (24 other events, 179.9 us)
